TPU v7x, 256 devices: a whole 4x4x8 slice. The times are simulated.
256 devices in a mesh: row: 32 (over y, z), col: 8 (over x, core).
Axes of the slice: x: 4, y: 4, z: 8, core: 2. Of those that a mesh axis runs over, the one named last changes fastest.
Arguments:
- panel: bfloat16 [2, 32, 512, 8, 512], P(None, 'row', None, 'col'), may hold values from -0.1875 to 0.1875
- rhs: float32 [2, 32, 512, 2048], P(None, 'row', None, 'col'), may hold values from -6 to 6
- inverse: bfloat16 [8, 512, 512], replicated, as said below
Outputs:
- solved: float32 [8, 512, 2048], P(None, None, 'col')
- remainder: float32 [2, 32, 512, 2048], P(None, 'row', None, 'col')
Inputs may be any that keep to these rules, and one draw needn't show every extreme that they name: Each block of inverse is lower triangular with a positive diagonal.
All inputs are finite; a program needn't handle non-finite values.
Results may differ from a plain program's by a relative error of at most 0.008.
Values may be sent and summed in bfloat16 or wider, within the bound.
No kernel may reach another device: no remote copies, remote signals or barrier semaphores. Data moves between devices by JAX's collectives and lax.ppermute only.
A program may use at most 128 MiB of HBM per device.

v0:
```python
import jax
import jax.numpy as jnp
from jax import lax
from jax.experimental import pallas as pl
from jax.experimental.pallas import tpu as pltpu
from jax.sharding import PartitionSpec as P


NY, NZ, NX = 4, 8, 4
NT = (((1,), (1,)), ((), ()))
BF = jnp.bfloat16
F32 = jnp.float32


def row_of(y, z):
    return (y % NY) * NZ + z % NZ


def shift_y(d):
    return [(row_of(y, z), row_of(y + d, z)) for y in range(NY) for z in range(NZ)]


def from_plane(y, to):
    return [(row_of(y, z), row_of(to, z)) for z in range(NZ)]


def back_z(d, rows):
    return [(row_of(y, k), row_of(y, k - d)) for y in range(NY) for k in rows if k >= d]


def hop_z(t):
    return [(row_of(y, t - 1), row_of(y, t)) for y in range(NY)]


def hop_z_early(t):
    return hop_z(t) + [(row_of(0, t + 3), row_of(0, t + 4))]


def shift_x(d):
    n = 2 * NX
    return [(i, (i + 2 * d) % n) for i in range(n)]


SWAP = [(i, i ^ 1) for i in range(2 * NX)]


def after(x, *deps):
    return lax.optimization_barrier((x, *deps))[0]


VMEM = pl.BlockSpec(memory_space=pltpu.VMEM)
SMEM = pl.BlockSpec(memory_space=pltpu.SMEM)
LIMIT = 8 * 1024 * 1024
PLACE, KIND, ROWS, AT_Z, PLANE = 0, 8, 16, 17, 18


def params(limit=LIMIT):
    return pltpu.CompilerParams(vmem_limit_bytes=limit)


def times_block(sc, j, low, blocks, use, flip=False):
    place = sc[PLACE + j]
    for kind, ref in enumerate(blocks):

        @pl.when(sc[KIND + j] == kind)
        def _():
            block = ref[place] if len(ref.shape) == 3 else ref[...]
            pair = (block, low) if flip else (low, block)
            use(lax.dot_general(*pair, NT, preferred_element_type=F32))


def early_kernel(sc, base, solved, *refs):
    *blocks, out = refs
    out[...] = base[...].astype(F32)

    def subtract(value):
        out[...] -= value

    @pl.loop(0, solved.shape[0])
    def _(j):
        times_block(sc, j, solved[j], blocks, subtract)


def early(sc, base, solved, blocks):
    n = solved.shape[0]
    c, b = base.shape
    return pl.pallas_call(
        early_kernel,
        out_shape=jax.ShapeDtypeStruct((c, b), F32),
        in_specs=[SMEM] + [VMEM] * (2 + len(blocks)),
        out_specs=VMEM,
        compiler_params=params(),
        cost_estimate=pl.CostEstimate(
            flops=2 * n * c * b * b, bytes_accessed=n * b * b, transcendentals=0
        ),
        name="early",
    )(sc, base, solved, *blocks)


def step_kernel(t, sc, acc, last, inv, *refs):
    *blocks, out, base = refs

    def subtract(value):
        base[...] = (acc[...] - value).astype(BF)

    times_block(sc, t - 1, last[...], blocks, subtract)
    out[...] = lax.dot_general(
        base[...], inv[t], NT, preferred_element_type=F32
    ).astype(BF)


def step(t, sc, acc, last, inv, blocks):
    c, b = acc.shape
    return pl.pallas_call(
        lambda *refs: step_kernel(t, *refs),
        out_shape=jax.ShapeDtypeStruct((c, b), BF),
        in_specs=[SMEM] + [VMEM] * (3 + len(blocks)),
        out_specs=VMEM,
        scratch_shapes=[pltpu.VMEM((c, b), BF)],
        compiler_params=params(),
        cost_estimate=pl.CostEstimate(
            flops=4 * c * b * b, bytes_accessed=2 * b * b, transcendentals=0
        ),
        name="step",
    )(sc, acc, last, inv, *blocks)


def first_kernel(base, inv, out):
    out[...] = lax.dot_general(
        base[...], inv[0], NT, preferred_element_type=F32
    ).astype(BF)


def first(base, inv):
    return pl.pallas_call(
        first_kernel,
        out_shape=jax.ShapeDtypeStruct(base.shape, BF),
        in_specs=[VMEM, VMEM],
        out_specs=VMEM,
        compiler_params=params(),
        name="first",
    )(base, inv)


def hold(parts, stack=False):
    one = parts[0].shape
    shape = (len(parts), *one) if stack else (len(parts) * one[0], *one[1:])

    def kernel(*refs):
        *ins, out = refs
        for i, ref in enumerate(ins):
            if stack:
                out[i] = ref[...]
            else:
                out[i * one[0] : (i + 1) * one[0]] = ref[...]

    return pl.pallas_call(
        kernel,
        out_shape=jax.ShapeDtypeStruct(shape, parts[0].dtype),
        in_specs=[VMEM] * len(parts),
        out_specs=VMEM,
        compiler_params=params(),
        cost_estimate=pl.CostEstimate(
            flops=0, bytes_accessed=4 * len(parts) * one[0] * one[1], transcendentals=0
        ),
        name="hold",
    )(*parts)


def collect(sc, rows, own, before, after_own):
    c, b = own.shape
    names, arrays = {}, []

    def ref_of(x):
        if id(x) not in names:
            names[id(x)] = len(arrays)
            arrays.append(x)
        return names[id(x)]

    def source(z, k):
        if k == z:
            return ref_of(own), None
        if k > z:
            return ref_of(after_own[k - z - 1]), None
        at = 0
        for x in before[z]:
            if len(x.shape) == 2:
                if at == k:
                    return ref_of(x), None
                at += 1
            else:
                if at <= k < at + x.shape[0]:
                    return ref_of(x), k - at
                at += x.shape[0]

    plan = [[source(z, k) for k in rows] for z in range(NZ)]

    def kernel(sc, *refs):
        *ins, out = refs
        for z in range(NZ):

            @pl.when(sc[AT_Z] == z)
            def _():
                for i, (which, at) in enumerate(plan[z]):
                    out[i] = ins[which][...] if at is None else ins[which][at]

    return pl.pallas_call(
        kernel,
        out_shape=jax.ShapeDtypeStruct((len(rows), c, b), BF),
        in_specs=[SMEM] + [VMEM] * len(arrays),
        out_specs=VMEM,
        compiler_params=params(),
        cost_estimate=pl.CostEstimate(
            flops=0, bytes_accessed=4 * len(rows) * c * b, transcendentals=0
        ),
        name="collect",
    )(sc, *arrays)


def spread_y(rows):
    half = rows.shape[0] // 2
    before = lax.ppermute(rows, "row", shift_y(1))
    behind = lax.ppermute(rows, "row", shift_y(-1))
    far_a = lax.ppermute(before[:half], "row", shift_y(1))
    far_b = lax.ppermute(behind[half:], "row", shift_y(-1))
    return rows, behind, far_a, far_b, before


def final_kernel(start, sc, every, behind, far_a, far_b, before, *refs):
    blocks0, blocks1, rest = refs[:4], refs[4:8], refs[8:]
    rhs, (out_s, out_r, low, eye) = rest[0], rest[-4:]
    i = pl.program_id(0)
    c = every.shape[1]
    half = far_a.shape[0]
    split = half < every.shape[0]

    @pl.when(i == 0)
    def _():
        out_r[...] = rhs[...]
        across = lax.broadcasted_iota(jnp.int32, eye.shape, 0)
        down = lax.broadcasted_iota(jnp.int32, eye.shape, 1)
        eye[...] = (across == down).astype(F32).astype(BF)

    def put(m, value):
        low[pl.ds(pl.multiple_of(sc[PLANE + m] * c, c), c), :] = value

    put(0, every[i])
    put(1, behind[i])
    put(3, before[i])

    @pl.when(i < half)
    def _():
        put(2, far_a[i])

    if split:

        @pl.when(i >= half)
        def _():
            put(2, far_b[i - half])

    solved = low[...]
    out_s[0] = lax.dot_general(eye[...], solved, NT, preferred_element_type=F32)

    def remove(q):
        def use(value):
            out_r[q, 0] -= value

        return use

    k = start + i
    times_block(sc, k, solved, blocks1, remove(1), flip=True)

    @pl.when(k < sc[ROWS])
    def _():
        times_block(sc, k, solved, blocks0, remove(0), flip=True)


def final(start, sc, steps, pieces, blocks0, blocks1, rhs, out_s=None):
    n, _, b = pieces[0].shape
    cols = rhs.shape[3]
    args = [sc, *pieces, *blocks0, *blocks1, rhs]
    specs = [SMEM] + [VMEM] * (len(args) - 1)
    alias = {}
    if out_s is not None:
        alias = {len(args): 0}
        args.append(out_s)
        specs.append(pl.BlockSpec(memory_space=pl.ANY))
    return pl.pallas_call(
        lambda *refs: final_kernel(start, *refs),
        out_shape=(
            jax.ShapeDtypeStruct((steps, b, cols), F32),
            jax.ShapeDtypeStruct(rhs.shape, F32),
        ),
        grid=(n,),
        in_specs=specs,
        out_specs=(
            pl.BlockSpec((1, b, cols), lambda i: (start + i, 0, 0)),
            pl.BlockSpec(rhs.shape, lambda i: (0, 0, 0, 0)),
        ),
        scratch_shapes=[pltpu.VMEM((cols, b), BF), pltpu.VMEM((b, b), BF)],
        input_output_aliases=alias,
        compiler_params=params(2 * LIMIT),
        cost_estimate=pl.CostEstimate(
            flops=6 * n * b * b * cols,
            bytes_accessed=4 * n * b * cols,
            transcendentals=0,
        ),
        name="final",
    )(*args)


def on_device(panel, rhs, inverse):
    steps = inverse.shape[0]
    block = panel.shape[2]
    quarter = rhs.shape[3] // NY
    half = block // 2
    row = lax.axis_index("row")
    col = lax.axis_index("col")
    y, z = row // NZ, row % NZ
    x, core = col // 2, col % 2

    j = jnp.arange(steps, dtype=jnp.int32)
    away = (j // 2 - x) % NX
    place = jnp.where(away == 3, 1, jnp.where(away == 1, 2, 0))
    kind = (away == 2) + 2 * (j % 2 != core)
    limit = jnp.where(y == NY - 1, z, 0)
    plane = (jnp.arange(NY, dtype=jnp.int32) + y) % NY
    sc = jnp.concatenate(
        [place, kind.astype(jnp.int32), limit[None], z[None], plane]
    ).astype(jnp.int32)

    panel0 = panel[0, 0, :, 0, :]
    top, low = panel0[:half], panel0[half:]
    up_a = lax.ppermute(top, "row", from_plane(3, 0))
    down_b = lax.ppermute(low, "row", from_plane(3, 2))
    up_b = lax.ppermute(low, "row", from_plane(3, 0) + [(row_of(1, 0), row_of(2, 0))])
    down_a = lax.ppermute(top, "row", from_plane(3, 2) + [(row_of(0, 0), row_of(1, 0))])
    far_a = lax.ppermute(up_a, "row", from_plane(0, 1))
    far_b = lax.ppermute(down_b, "row", from_plane(2, 1))

    def by_plane(at0, at1, at2, at3):
        return jnp.where(
            y == 3, at3, jnp.where(y == 0, at0, jnp.where(y == 2, at2, at1))
        )

    window = jnp.concatenate(
        [by_plane(up_a, far_a, down_a, top), by_plane(up_b, far_b, down_b, low)]
    )

    panel1 = panel[1, 0, :, 0, :]
    left1 = lax.ppermute(panel1, "col", shift_x(1))
    right1 = lax.ppermute(panel1, "col", shift_x(-1))
    window, left1, right1 = lax.optimization_barrier((window, left1, right1))

    left = lax.ppermute(window, "col", shift_x(1))
    right = lax.ppermute(window, "col", shift_x(-1))
    zt = rhs[0, 0].astype(BF).T
    zq = [zt[i * quarter : (i + 1) * quarter] for i in range(NY)]
    ready = [after(zq[0], up_a), after(zq[1], far_a), after(zq[2], down_b)]
    zr = [lax.ppermute(ready[i], "row", from_plane(3, i)) for i in range(NY - 1)]
    near1 = hold([after(panel1, zr[0]), left1, right1], stack=True)
    near_other1 = lax.ppermute(near1, "col", SWAP)
    inverse = hold([inverse])
    left, right, near_other1, left1, right1, inverse, *zr = lax.optimization_barrier(
        (left, right, near_other1, left1[:half], right1[half:], inverse, *zr)
    )
    base = by_plane(*zr, zq[3])
    far_a, far_b = left[:half], right[half:]
    near = jnp.stack([after(window, far_a, far_b), left, right])
    far_a = lax.ppermute(far_a, "col", shift_x(1))
    far_b = lax.ppermute(far_b, "col", shift_x(-1))
    near_other = lax.ppermute(near, "col", SWAP)
    far_a, far_b, near_other = lax.optimization_barrier((far_a, far_b, near_other))
    far = hold([far_a, far_b])
    far_other = hold([lax.ppermute(far, "col", SWAP)])
    blocks0 = [near, far, near_other, far_other]

    fresh = first(base, inverse)
    own_s = fresh
    acc = base.astype(F32)
    known = None
    before = {0: []}
    for t in range(1, steps):
        sent = None
        if t > 1:
            sent = lax.ppermute(known, "row", hop_z_early(t))
        last = lax.ppermute(fresh, "row", hop_z(t))
        if t > 1:
            acc = early(sc, base, after(sent, fresh), blocks0)
            last = after(last, acc)
        if t == 2:
            left1, right1 = after(left1, acc), after(right1, acc)
            far1 = [
                lax.ppermute(left1, "col", shift_x(1)),
                lax.ppermute(right1, "col", shift_x(-1)),
            ]
        fresh = step(t, sc, acc, last, inverse, blocks0)
        own_s = jnp.where(z == t, fresh, own_s)
        before[t] = [last] if t == 1 else [sent, last]
        known = last[None] if t == 1 else jnp.concatenate([sent, last[None]])

    far1 = hold([after(far1[0], fresh), far1[1]])
    far_other1 = lax.ppermute(far1, "col", SWAP)
    blocks1 = [near1, far1, near_other1, far_other1]
    back = [
        lax.ppermute(own_s, "row", back_z(d, range(1 if d < 4 else 4, 8)))
        for d in range(1, 8)
    ]
    rows_a = collect(sc, range(4), own_s, before, back)
    before_a = lax.ppermute(rows_a, "row", shift_y(1))
    behind_a = lax.ppermute(rows_a, "row", shift_y(-1))
    far_a = lax.ppermute(rows_a, "row", shift_y(2))
    pieces_a = (rows_a, behind_a, far_a, far_a, before_a)
    out_s, rest = final(0, sc, steps, pieces_a, blocks0, blocks1, rhs)
    rows_b = collect(sc, range(4, 8), own_s, before, back)
    rows_b = after(rows_b, before_a, behind_a)
    pieces_b = spread_y(rows_b)
    return tuple(final(4, sc, steps, pieces_b, blocks0, blocks1, rest, out_s))


def solution(mesh):
    placed = (P(None, "row", None, "col", None), P(None, "row", None, "col"), P())
    return jax.shard_map(
        on_device,
        mesh=mesh,
        in_specs=placed,
        out_specs=(P(None, None, "col"), P(None, "row", None, "col")),
        check_vma=False,
    )
```

profile of v0, /device:TPU:34, one launch (start us, length us, event | category | flops | bytes accessed | tf_op | source)
XLA Modules:
  0.0 204.0 jit_solution(12379102294003148633)
XLA Ops:
  3.1 1.4 collective-permute-start.4
  4.5 1.4 collective-permute-start.1
  9.0 4.0 %collective-permute-done = bf16[256,512]{1,0:T(8,128)(2,1)} collective-permute-done((bf16[256,512]{1,0:T(8,128)(2,1)S(1)}, bf16[256,512]{1,0:T(8,128)(2,1)}, u32[]{:S(2)}, u32[]{:S(2)}) %collective-permute-start) | collective-permute-done | bytes 262176 | tf_op jit(solution)/shard_map/ppermute | solution.py:334
  15.7 1.4 collective-permute-start.5
  17.7 2.7 %collective-permute-done.10 = bf16[64,512]{1,0:T(8,128)(2,1)S(1)} collective-permute-done((bf16[64,512]{1,0:T(8,128)(2,1)S(1)}, bf16[64,512]{1,0:T(8,128)(2,1)S(1)}, u32[]{:S(2)}, u32[]{:S(2)}) %collective-permute-start.10) | collective-permute-done | bytes 65568 | tf_op jit(solution)/shard_map/ppermute | solution.py:360
  20.4 1.5 collective-permute-start.6
  23.2 6.8 %collective-permute-done.7.refs_2_ = bf16[512,512]{1,0:T(8,128)(2,1)S(1)} collective-permute-done((bf16[512,512]{1,0:T(8,128)(2,1)S(1)}, bf16[512,512]{1,0:T(8,128)(2,1)S(1)}, u32[]{:S(2)}, u32[]{:S(2)}) %collective-permute-start.7) | collective-permute-done | bytes 524320 | tf_op jit(solution)/shard_map/ppermute | solution.py:352
  30.0 3.2 %collective-permute-done.6.refs_1_ = bf16[512,512]{1,0:T(8,128)(2,1)S(1)} collective-permute-done((bf16[512,512]{1,0:T(8,128)(2,1)S(1)}, bf16[512,512]{1,0:T(8,128)(2,1)S(1)}, u32[]{:S(2)}, u32[]{:S(2)}) %collective-permute-start.6) | collective-permute-done | bytes 524320 | tf_op jit(solution)/shard_map/ppermute | solution.py:351
  33.4 1.8 collective-permute-start.9
  37.8 2.0 copy-done
  41.2 6.5 %collective-permute-done.9 = bf16[512,512]{1,0:T(8,128)(2,1)S(1)} collective-permute-done((bf16[512,512]{1,0:T(8,128)(2,1)S(1)}, bf16[512,512]{1,0:T(8,128)(2,1)S(1)}, u32[]{:S(2)}, u32[]{:S(2)}) %collective-permute-start.9) | collective-permute-done | bytes 524320 | tf_op jit(solution)/shard_map/ppermute | solution.py:356
  47.8 1.5 collective-permute-done.8
  50.8 2.8 %collective-permute-start.17 = (bf16[256,512]{1,0:T(8,128)(2,1)S(1)}, bf16[256,512]{1,0:T(8,128)(2,1)S(1)}, u32[]{:S(2)}, u32[]{:S(2)}) collective-permute-start(bf16[256,512]{1,0:T(8,128)(2,1)S(1)} %slice.65), channel_id=1, source_target_pairs={{0,6},{1,7},{2,0},{3,1},{4,2},{5,3},{6,4},{7,5},{8,14},{9,15},{10,... | collective-permute-start | bytes 786440 | tf_op jit(solution)/shard_map/ppermute | solution.py:371
  53.6 6.1 %collective-permute-done.17.refs_1_ = bf16[256,512]{1,0:T(8,128)(2,1)S(1)} collective-permute-done((bf16[256,512]{1,0:T(8,128)(2,1)S(1)}, bf16[256,512]{1,0:T(8,128)(2,1)S(1)}, u32[]{:S(2)}, u32[]{:S(2)}) %collective-permute-start.17) | collective-permute-done | bytes 262176 | tf_op jit(solution)/shard_map/ppermute | solution.py:371
  59.7 2.2 %collective-permute-done.16.refs_0_ = bf16[256,512]{1,0:T(8,128)(2,1)S(1)} collective-permute-done((bf16[256,512]{1,0:T(8,128)(2,1)S(1)}, bf16[256,512]{1,0:T(8,128)(2,1)S(1)}, u32[]{:S(2)}, u32[]{:S(2)}) %collective-permute-start.16) | collective-permute-done | bytes 262176 | tf_op jit(solution)/shard_map/ppermute | solution.py:370
  63.7 2.2 %copy-done.1 = bf16[8,512,512]{2,1,0:T(8,128)(2,1)S(1)} copy-done((bf16[8,512,512]{2,1,0:T(8,128)(2,1)S(1)}, bf16[8,512,512]{2,1,0:T(8,128)(2,1)}, u32[]{:S(2)}) %copy-start.1) | copy-done | bytes 4194328
  67.6 5.0 %collective-permute-done.14.refs_2_.refs_4_ = bf16[64,512]{1,0:T(8,128)(2,1)S(1)} collective-permute-done((bf16[64,512]{1,0:T(8,128)(2,1)S(1)}, bf16[64,512]{1,0:T(8,128)(2,1)S(1)}, u32[]{:S(2)}, u32[]{:S(2)}) %collective-permute-start.14) | collective-permute-done | bytes 65568 | tf_op jit(solution)/shard_map/ppermute | solution.py:387
  75.0 2.4 %copy-done.2 = bf16[8,512,512]{2,1,0:T(8,128)(2,1)S(1)} copy-done((bf16[8,512,512]{2,1,0:T(8,128)(2,1)S(1)}, bf16[8,512,512]{2,1,0:T(8,128)(2,1)}, u32[]{:S(2)}) %copy-start.2) | copy-done | bytes 4194328
  77.4 1.6 step.7
  79.0 1.6 collective-permute-start.20
  80.6 1.4 early.6.refs_1_
  83.2 1.6 step.8
  85.5 1.7 early.7.refs_1_
  88.0 1.6 step.9
  90.4 2.1 %early.8.refs_1_ = f32[64,512]{1,0:T(8,128)S(1)} custom-call(s32[22]{0:T(128)S(1)} %concatenate.21.refs_0_.sc, bf16[64,512]{1,0:T(8,128)(2,1)S(1)} %get-tuple-element.79.base, bf16[3,64,512]{2,1,0:T(8,128)(2,1)S(1)} %collective-permute-done.23.solved.refs_9_, bf16[3,512,512]{2,1,0:T(8,128)(2,1)S(1)} %pad_maximum_fusion.refs_4_.refs_0_.refs_6_, ...), custom_call_target="tpu_custom_call" | custom-call | flops 100663296 | bytes 786432 | tf_op jit(solution)/shard_map/early/pallas_call | solution.py:87
  93.8 1.8 step.10
  96.3 9.7 %collective-permute-done.25.solved.refs_11_ = bf16[4,64,512]{2,1,0:T(8,128)(2,1)S(1)} collective-permute-done((bf16[4,64,512]{2,1,0:T(8,128)(2,1)S(1)}, bf16[4,64,512]{2,1,0:T(8,128)(2,1)S(1)}, u32[]{:S(2)}, u32[]{:S(2)}) %collective-permute-start.25) | collective-permute-done | bytes 262176 | tf_op jit(solution)/shard_map/ppermute | solution.py:386
  106.0 2.4 %early.9.refs_1_ = f32[64,512]{1,0:T(8,128)S(1)} custom-call(s32[22]{0:T(128)S(1)} %concatenate.21.refs_0_.sc, bf16[64,512]{1,0:T(8,128)(2,1)S(1)} %get-tuple-element.79.base, bf16[4,64,512]{2,1,0:T(8,128)(2,1)S(1)} %collective-permute-done.25.solved.refs_11_, bf16[3,512,512]{2,1,0:T(8,128)(2,1)S(1)} %pad_maximum_fusion.refs_4_.refs_0_.refs_6_, ...), custom_call_target="tpu_custom_call" | custom-call | flops 134217728 | bytes 1048576 | tf_op jit(solution)/shard_map/early/pallas_call | solution.py:87
  109.8 1.6 step.11
  112.2 3.5 %collective-permute-done.27.solved.refs_9_.refs_12_ = bf16[5,64,512]{2,1,0:T(8,128)(2,1)S(1)} collective-permute-done((bf16[5,64,512]{2,1,0:T(8,128)(2,1)S(1)}, bf16[5,64,512]{2,1,0:T(8,128)(2,1)S(1)}, u32[]{:S(2)}, u32[]{:S(2)}) %collective-permute-start.27) | collective-permute-done | bytes 327712 | tf_op jit(solution)/shard_map/ppermute | solution.py:386
  115.7 2.6 %early.10.refs_1_ = f32[64,512]{1,0:T(8,128)S(1)} custom-call(s32[22]{0:T(128)S(1)} %concatenate.21.refs_0_.sc, bf16[64,512]{1,0:T(8,128)(2,1)S(1)} %get-tuple-element.79.base, bf16[5,64,512]{2,1,0:T(8,128)(2,1)S(1)} %collective-permute-done.27.solved.refs_9_.refs_12_, bf16[3,512,512]{2,1,0:T(8,128)(2,1)S(1)} %pad_maximum_fusion.refs_4_.refs_0_.refs_6_, ...), custom_call_target="tpu_custom_call" | custom-call | flops 167772160 | bytes 1310720 | tf_op jit(solution)/shard_map/early/pallas_call | solution.py:87
  119.1 1.4 collective-permute-start.29
  120.5 2.3 %step.12 = bf16[64,512]{1,0:T(8,128)(2,1)} custom-call(s32[22]{0:T(128)S(1)} %concatenate.21.refs_0_.sc, f32[64,512]{1,0:T(8,128)S(1)} %early.10.refs_1_, bf16[64,512]{1,0:T(8,128)(2,1)S(1)} %collective-permute-done.28.refs_2_.refs_10_, bf16[8,512,512]{2,1,0:T(8,128)(2,1)S(1)} %copy-done.3, bf16[3,512,512]{2,1,0:T(8,128)(2,1)S(1)} %pad_maximum_fusion.refs_4_.refs_0_.refs_6_, ...), custom_call_target="tpu_custom_call" | custom-call | flops 67108864 | bytes 524288 | tf_op jit(solution)/shard_map/step/pallas_call | solution.py:114
  124.4 1.8 collective-permute-start.45
  127.2 3.0 %early.11.refs_1_ = f32[64,512]{1,0:T(8,128)S(1)} custom-call(s32[22]{0:T(128)S(1)} %concatenate.21.refs_0_.sc, bf16[64,512]{1,0:T(8,128)(2,1)S(1)} %get-tuple-element.79.base, bf16[6,64,512]{2,1,0:T(8,128)(2,1)} %collective-permute-done.29.solved.refs_11_.refs_13_, bf16[3,512,512]{2,1,0:T(8,128)(2,1)S(1)} %pad_maximum_fusion.refs_4_.refs_0_.refs_6_, ...), custom_call_target="tpu_custom_call" | custom-call | flops 201326592 | bytes 1572864 | tf_op jit(solution)/shard_map/early/pallas_call | solution.py:87
  130.4 1.8 step.13
  132.3 2.1 %collective-permute-start.37 = (bf16[64,512]{1,0:T(8,128)(2,1)S(1)}, bf16[64,512]{1,0:T(8,128)(2,1)S(1)}, u32[]{:S(2)}, u32[]{:S(2)}) collective-permute-start(bf16[64,512]{1,0:T(8,128)(2,1)S(1)} %select_select_fusion.2.refs_7_.refs_0_), channel_id=1, source_target_pairs={{8,0},{16,8},{24,16},{32,24},{40,32},{48,40},{56,48},{72,64},{80,7... | collective-permute-start | bytes 196616 | tf_op jit(solution)/shard_map/ppermute | solution.py:406
  137.0 4.1 %collective-permute-done.37.refs_6_.refs_1_ = bf16[64,512]{1,0:T(8,128)(2,1)S(1)} collective-permute-done((bf16[64,512]{1,0:T(8,128)(2,1)S(1)}, bf16[64,512]{1,0:T(8,128)(2,1)S(1)}, u32[]{:S(2)}, u32[]{:S(2)}) %collective-permute-start.37) | collective-permute-done | bytes 65568 | tf_op jit(solution)/shard_map/ppermute | solution.py:406
  141.1 3.3 %collective-permute-done.36.refs_5_.refs_2_ = bf16[64,512]{1,0:T(8,128)(2,1)S(1)} collective-permute-done((bf16[64,512]{1,0:T(8,128)(2,1)S(1)}, bf16[64,512]{1,0:T(8,128)(2,1)S(1)}, u32[]{:S(2)}, u32[]{:S(2)}) %collective-permute-start.36) | collective-permute-done | bytes 65568 | tf_op jit(solution)/shard_map/ppermute | solution.py:406
  144.4 4.8 %collective-permute-done.35.refs_4_.refs_3_ = bf16[64,512]{1,0:T(8,128)(2,1)S(1)} collective-permute-done((bf16[64,512]{1,0:T(8,128)(2,1)S(1)}, bf16[64,512]{1,0:T(8,128)(2,1)S(1)}, u32[]{:S(2)}, u32[]{:S(2)}) %collective-permute-start.35) | collective-permute-done | bytes 65568 | tf_op jit(solution)/shard_map/ppermute | solution.py:406
  150.6 2.0 collective-permute-start.38
  156.0 8.4 %collective-permute-done.33.refs_2_ = bf16[64,512]{1,0:T(8,128)(2,1)S(1)} collective-permute-done((bf16[64,512]{1,0:T(8,128)(2,1)S(1)}, bf16[64,512]{1,0:T(8,128)(2,1)S(1)}, u32[]{:S(2)}, u32[]{:S(2)}) %collective-permute-start.33) | collective-permute-done | bytes 65568 | tf_op jit(solution)/shard_map/ppermute | solution.py:406
  165.7 8.8 %collective-permute-done.31.refs_0_ = bf16[64,512]{1,0:T(8,128)(2,1)S(1)} collective-permute-done((bf16[64,512]{1,0:T(8,128)(2,1)S(1)}, bf16[64,512]{1,0:T(8,128)(2,1)S(1)}, u32[]{:S(2)}, u32[]{:S(2)}) %collective-permute-start.31) | collective-permute-done | bytes 65568 | tf_op jit(solution)/shard_map/ppermute | solution.py:406
  175.7 3.2 %collective-permute-start.40 = (bf16[4,64,512]{2,1,0:T(8,128)(2,1)S(1)}, bf16[4,64,512]{2,1,0:T(8,128)(2,1)S(1)}, u32[]{:S(2)}, u32[]{:S(2)}) collective-permute-start(bf16[4,64,512]{2,1,0:T(8,128)(2,1)S(1)} %collect.2.refs_1_), channel_id=1, source_target_pairs={{0,192},{8,200},{16,208},{24,216},{32,224},{40,232},{48,240},{56,2... | collective-permute-start | bytes 786440 | tf_op jit(solution)/shard_map/ppermute | solution.py:223
  178.9 9.8 %collective-permute-done.41.refs_5_ = bf16[4,64,512]{2,1,0:T(8,128)(2,1)S(1)} collective-permute-done((bf16[4,64,512]{2,1,0:T(8,128)(2,1)S(1)}, bf16[4,64,512]{2,1,0:T(8,128)(2,1)S(1)}, u32[]{:S(2)}, u32[]{:S(2)}) %collective-permute-start.41) | collective-permute-done | bytes 262176 | tf_op jit(solution)/shard_map/ppermute | solution.py:222
  189.6 4.1 %collective-permute-start.43 = (bf16[2,64,512]{2,1,0:T(8,128)(2,1)S(1)}, bf16[2,64,512]{2,1,0:T(8,128)(2,1)S(1)}, u32[]{:S(2)}, u32[]{:S(2)}) collective-permute-start(bf16[2,64,512]{2,1,0:T(8,128)(2,1)S(1)} %slice.74), channel_id=1, source_target_pairs={{0,192},{8,200},{16,208},{24,216},{32,224},{40,232},{48,240},{56,2... | collective-permute-start | bytes 393224 | tf_op jit(solution)/shard_map/ppermute | solution.py:225
  193.8 4.9 %final.2 = (f32[8,512,256]{2,1,0:T(8,128)}, f32[2,1,512,256]{3,2,1,0:T(8,128)S(1)}) custom-call(s32[22]{0:T(128)S(1)} %concatenate.21.refs_0_.sc, bf16[4,64,512]{2,1,0:T(8,128)(2,1)S(1)} %collect.3.refs_1_, bf16[4,64,512]{2,1,0:T(8,128)(2,1)S(1)} %collective-permute-done.39.refs_2_, bf16[4,64,512]{2,1,0:T(8,128)(2,1)S(1)} %collective-permute-done.47.refs_3_.refs_4_, ...), custom_call_target="tpu_custom_call" | custom-call | flops 1610612736 | bytes 2097152 | tf_op jit(solution)/shard_map/final/pallas_call | solution.py:288
  198.7 5.3 %final.3 = (f32[8,512,256]{2,1,0:T(8,128)}, f32[2,1,512,256]{3,2,1,0:T(8,128)}) custom-call(s32[22]{0:T(128)S(1)} %concatenate.21.refs_0_.sc, bf16[4,64,512]{2,1,0:T(8,128)(2,1)S(1)} %collect.2.refs_1_, bf16[4,64,512]{2,1,0:T(8,128)(2,1)S(1)} %collective-permute-done.40.refs_2_, ...), custom_call_target="tpu_custom_call", output_to_operand_aliasing={{0}: (15, {})} | custom-call | flops 1610612736 | bytes 2097152 | tf_op jit(solution)/shard_map/final/pallas_call | solution.py:288
  (197 shorter events, 42.9 us)
Async XLA Ops:
  1.8 11.3 %collective-permute-start = (bf16[256,512]{1,0:T(8,128)(2,1)S(1)}, bf16[256,512]{1,0:T(8,128)(2,1)}, u32[]{:S(2)}, u32[]{:S(2)}) collective-permute-start(bf16[256,512]{1,0:T(8,128)(2,1)S(1)} %get-tuple-element.82), channel_id=1, source_target_pairs={{192,0},{200,8},{208,16},{216,24},{224,32},{232,40},{240,48},{248,... | collective-permute-start | bytes 786440 | tf_op jit(solution)/shard_map/ppermute | solution.py:334
  3.1 12.6 %collective-permute-start.4 = (bf16[256,512]{1,0:T(8,128)(2,1)S(1)}, bf16[256,512]{1,0:T(8,128)(2,1)}, u32[]{:S(2)}, u32[]{:S(2)}) collective-permute-start(bf16[256,512]{1,0:T(8,128)(2,1)S(1)} %get-tuple-element.83), channel_id=1, source_target_pairs={{192,128},{200,136},{208,144},{216,152},{224,160},{232,168},{240,1... | collective-permute-start | bytes 786440 | tf_op jit(solution)/shard_map/ppermute | solution.py:335
  4.5 12.6 %collective-permute-start.1 = (bf16[256,512]{1,0:T(8,128)(2,1)S(1)}, bf16[256,512]{1,0:T(8,128)(2,1)}, u32[]{:S(2)}, u32[]{:S(2)}) collective-permute-start(bf16[256,512]{1,0:T(8,128)(2,1)S(1)} %get-tuple-element.82), channel_id=1, source_target_pairs={{192,128},{200,136},{208,144},{216,152},{224,160},{232,168},{240,1... | collective-permute-start | bytes 786440 | tf_op jit(solution)/shard_map/ppermute | solution.py:337
  5.8 16.1 %collective-permute-start.3 = (bf16[256,512]{1,0:T(8,128)(2,1)S(1)}, bf16[256,512]{1,0:T(8,128)(2,1)}, u32[]{:S(2)}, u32[]{:S(2)}) collective-permute-start(bf16[256,512]{1,0:T(8,128)(2,1)S(1)} %get-tuple-element.83), channel_id=1, source_target_pairs={{192,0},{200,8},{208,16},{216,24},{224,32},{232,40},{240,48},{248,... | collective-permute-start | bytes 786440 | tf_op jit(solution)/shard_map/ppermute | solution.py:336
  13.1 7.4 %collective-permute-start.10 = (bf16[64,512]{1,0:T(8,128)(2,1)S(1)}, bf16[64,512]{1,0:T(8,128)(2,1)S(1)}, u32[]{:S(2)}, u32[]{:S(2)}) collective-permute-start(bf16[64,512]{1,0:T(8,128)(2,1)S(1)} %get-tuple-element.41), channel_id=1, source_target_pairs={{192,0},{200,8},{208,16},{216,24},{224,32},{232,40},{240,48},{248,... | collective-permute-start | bytes 196616 | tf_op jit(solution)/shard_map/ppermute | solution.py:360
  14.3 7.6 %collective-permute-start.2 = (bf16[256,512]{1,0:T(8,128)(2,1)}, bf16[256,512]{1,0:T(8,128)(2,1)S(1)}, u32[]{:S(2)}, u32[]{:S(2)}) collective-permute-start(bf16[256,512]{1,0:T(8,128)(2,1)} %collective-permute-done), channel_id=1, source_target_pairs={{0,64},{8,72},{16,80},{24,88},{32,96},{40,104},{48,112},{56,120},{... | collective-permute-start | bytes 786440 | tf_op jit(solution)/shard_map/ppermute | solution.py:338
  15.7 6.2 %collective-permute-start.5 = (bf16[256,512]{1,0:T(8,128)(2,1)}, bf16[256,512]{1,0:T(8,128)(2,1)}, u32[]{:S(2)}, u32[]{:S(2)}) collective-permute-start(bf16[256,512]{1,0:T(8,128)(2,1)} %collective-permute-done.4), channel_id=1, source_target_pairs={{128,64},{136,72},{144,80},{152,88},{160,96},{168,104},{176,112},{... | collective-permute-start | bytes 786440 | tf_op jit(solution)/shard_map/ppermute | solution.py:339
  17.1 12.9 %collective-permute-start.7 = (bf16[512,512]{1,0:T(8,128)(2,1)S(1)}, bf16[512,512]{1,0:T(8,128)(2,1)S(1)}, u32[]{:S(2)}, u32[]{:S(2)}) collective-permute-start(bf16[512,512]{1,0:T(8,128)(2,1)S(1)} %slice_bitcast_fusion.refs_0_), channel_id=1, source_target_pairs={{0,6},{1,7},{2,0},{3,1},{4,2},{5,3},{6,4},{7,5},{8,14},{9,15},{10,... | collective-permute-start | bytes 1572872 | tf_op jit(solution)/shard_map/ppermute | solution.py:352
  20.4 12.8 %collective-permute-start.6 = (bf16[512,512]{1,0:T(8,128)(2,1)S(1)}, bf16[512,512]{1,0:T(8,128)(2,1)S(1)}, u32[]{:S(2)}, u32[]{:S(2)}) collective-permute-start(bf16[512,512]{1,0:T(8,128)(2,1)S(1)} %slice_bitcast_fusion.refs_0_), channel_id=1, source_target_pairs={{0,2},{1,3},{2,4},{3,5},{4,6},{5,7},{6,0},{7,1},{8,10},{9,11},{10,... | collective-permute-start | bytes 1572872 | tf_op jit(solution)/shard_map/ppermute | solution.py:351
  33.3 15.9 %collective-permute-start.11 = (bf16[3,512,512]{2,1,0:T(8,128)(2,1)S(1)}, bf16[3,512,512]{2,1,0:T(8,128)(2,1)S(1)}, u32[]{:S(2)}, u32[]{:S(2)}) collective-permute-start(bf16[3,512,512]{2,1,0:T(8,128)(2,1)S(1)} %hold.5.refs_10_), channel_id=1, source_target_pairs={{0,1},{1,0},{2,3},{3,2},{4,5},{5,4},{6,7},{7,6},{8,9},{9,8},{10,11... | collective-permute-start | bytes 4718600 | tf_op jit(solution)/shard_map/ppermute | solution.py:362
  33.4 14.3 %collective-permute-start.9 = (bf16[512,512]{1,0:T(8,128)(2,1)S(1)}, bf16[512,512]{1,0:T(8,128)(2,1)S(1)}, u32[]{:S(2)}, u32[]{:S(2)}) collective-permute-start(bf16[512,512]{1,0:T(8,128)(2,1)S(1)} %pad_maximum_fusion.1), channel_id=1, source_target_pairs={{0,6},{1,7},{2,0},{3,1},{4,2},{5,3},{6,4},{7,5},{8,14},{9,15},{10,... | collective-permute-start | bytes 1572872 | tf_op jit(solution)/shard_map/ppermute | solution.py:356
  35.3 14.0 %collective-permute-start.8 = (bf16[512,512]{1,0:T(8,128)(2,1)S(1)}, bf16[512,512]{1,0:T(8,128)(2,1)S(1)}, u32[]{:S(2)}, u32[]{:S(2)}) collective-permute-start(bf16[512,512]{1,0:T(8,128)(2,1)S(1)} %pad_maximum_fusion.1), channel_id=1, source_target_pairs={{0,2},{1,3},{2,4},{3,5},{4,6},{5,7},{6,0},{7,1},{8,10},{9,11},{10,... | collective-permute-start | bytes 1572872 | tf_op jit(solution)/shard_map/ppermute | solution.py:355
  35.6 5.7 %collective-permute-start.13 = (bf16[64,512]{1,0:T(8,128)(2,1)S(1)}, bf16[64,512]{1,0:T(8,128)(2,1)S(1)}, u32[]{:S(2)}, u32[]{:S(2)}) collective-permute-start(bf16[64,512]{1,0:T(8,128)(2,1)S(1)} %copy-done.48), channel_id=1, source_target_pairs={{192,128},{200,136},{208,144},{216,152},{224,160},{232,168},{240,1... | collective-permute-start | bytes 196616 | tf_op jit(solution)/shard_map/ppermute | solution.py:360
  36.2 5.0 %collective-permute-start.12 = (bf16[64,512]{1,0:T(8,128)(2,1)S(1)}, bf16[64,512]{1,0:T(8,128)(2,1)}, u32[]{:S(2)}, u32[]{:S(2)}) collective-permute-start(bf16[64,512]{1,0:T(8,128)(2,1)S(1)} %get-tuple-element.45), channel_id=1, source_target_pairs={{192,64},{200,72},{208,80},{216,88},{224,96},{232,104},{240,112},{... | collective-permute-start | bytes 196616 | tf_op jit(solution)/shard_map/ppermute | solution.py:360
  50.7 11.3 %collective-permute-start.18 = (bf16[3,512,512]{2,1,0:T(8,128)(2,1)S(1)}, bf16[3,512,512]{2,1,0:T(8,128)(2,1)S(1)}, u32[]{:S(2)}, u32[]{:S(2)}) collective-permute-start(bf16[3,512,512]{2,1,0:T(8,128)(2,1)S(1)} %pad_maximum_fusion.refs_4_.refs_0_.refs_6_), channel_id=1, source_target_pairs={{0,1},{1,0},{2,3},{3,2},{4,5},{5,4},{6,7},{7,6},{8,9},{9,8},{10,11... | collective-permute-start | bytes 4718600 | tf_op jit(solution)/shard_map/ppermute | solution.py:372
  50.8 9.0 %collective-permute-start.17 = (bf16[256,512]{1,0:T(8,128)(2,1)S(1)}, bf16[256,512]{1,0:T(8,128)(2,1)S(1)}, u32[]{:S(2)}, u32[]{:S(2)}) collective-permute-start(bf16[256,512]{1,0:T(8,128)(2,1)S(1)} %slice.65), channel_id=1, source_target_pairs={{0,6},{1,7},{2,0},{3,1},{4,2},{5,3},{6,4},{7,5},{8,14},{9,15},{10,... | collective-permute-start | bytes 786440 | tf_op jit(solution)/shard_map/ppermute | solution.py:371
  53.6 8.4 %collective-permute-start.16 = (bf16[256,512]{1,0:T(8,128)(2,1)S(1)}, bf16[256,512]{1,0:T(8,128)(2,1)S(1)}, u32[]{:S(2)}, u32[]{:S(2)}) collective-permute-start(bf16[256,512]{1,0:T(8,128)(2,1)S(1)} %slice.64), channel_id=1, source_target_pairs={{0,2},{1,3},{2,4},{3,5},{4,6},{5,7},{6,0},{7,1},{8,10},{9,11},{10,... | collective-permute-start | bytes 786440 | tf_op jit(solution)/shard_map/ppermute | solution.py:370
  62.8 11.1 %collective-permute-start.19 = (bf16[512,512]{1,0:T(8,128)(2,1)}, bf16[512,512]{1,0:T(8,128)(2,1)}, u32[]{:S(2)}, u32[]{:S(2)}) collective-permute-start(bf16[512,512]{1,0:T(8,128)(2,1)} %hold.7.refs_5_.refs_1_.refs_7_), channel_id=1, source_target_pairs={{0,1},{1,0},{2,3},{3,2},{4,5},{5,4},{6,7},{7,6},{8,9},{9,8},{10,11... | collective-permute-start | bytes 1572872 | tf_op jit(solution)/shard_map/ppermute | solution.py:375
  66.2 6.4 %collective-permute-start.14 = (bf16[64,512]{1,0:T(8,128)(2,1)S(1)}, bf16[64,512]{1,0:T(8,128)(2,1)S(1)}, u32[]{:S(2)}, u32[]{:S(2)}) collective-permute-start(bf16[64,512]{1,0:T(8,128)(2,1)S(1)} %first.1), channel_id=1, source_target_pairs={{0,8},{64,72},{128,136},{192,200},{1,9},{65,73},{129,137},{193,201... | collective-permute-start | bytes 196616 | tf_op jit(solution)/shard_map/ppermute | solution.py:387
  72.6 8.0 %collective-permute-start.15 = (bf16[1,64,512]{2,1,0:T(8,128)(2,1)S(1)}, bf16[1,64,512]{2,1,0:T(8,128)(2,1)S(1)}, u32[]{:S(2)}, u32[]{:S(2)}) collective-permute-start(bf16[1,64,512]{2,1,0:T(8,128)(2,1)S(1)} %bitcast.31), channel_id=1, source_target_pairs={{8,16},{72,80},{136,144},{200,208},{40,48},{9,17},{73,81},{137,145... | collective-permute-start | bytes 196616 | tf_op jit(solution)/shard_map/ppermute | solution.py:386
  79.0 3.4 %collective-permute-start.20 = (bf16[64,512]{1,0:T(8,128)(2,1)S(1)}, bf16[64,512]{1,0:T(8,128)(2,1)S(1)}, u32[]{:S(2)}, u32[]{:S(2)}) collective-permute-start(bf16[64,512]{1,0:T(8,128)(2,1)S(1)} %step.7), channel_id=1, source_target_pairs={{8,16},{72,80},{136,144},{200,208},{9,17},{73,81},{137,145},{201,2... | collective-permute-start | bytes 196616 | tf_op jit(solution)/shard_map/ppermute | solution.py:387
  82.5 3.0 %collective-permute-start.21 = (bf16[2,64,512]{2,1,0:T(8,128)(2,1)S(1)}, bf16[2,64,512]{2,1,0:T(8,128)(2,1)S(1)}, u32[]{:S(2)}, u32[]{:S(2)}) collective-permute-start(bf16[2,64,512]{2,1,0:T(8,128)(2,1)S(1)} %pad_maximum_fusion.6), channel_id=1, source_target_pairs={{16,24},{80,88},{144,152},{208,216},{48,56},{17,25},{81,89},{145,1... | collective-permute-start | bytes 393224 | tf_op jit(solution)/shard_map/ppermute | solution.py:386
  84.9 2.4 %collective-permute-start.22 = (bf16[64,512]{1,0:T(8,128)(2,1)S(1)}, bf16[64,512]{1,0:T(8,128)(2,1)S(1)}, u32[]{:S(2)}, u32[]{:S(2)}) collective-permute-start(bf16[64,512]{1,0:T(8,128)(2,1)S(1)} %step.8), channel_id=1, source_target_pairs={{16,24},{80,88},{144,152},{208,216},{17,25},{81,89},{145,153},{209... | collective-permute-start | bytes 196616 | tf_op jit(solution)/shard_map/ppermute | solution.py:387
  87.3 3.0 %collective-permute-start.23 = (bf16[3,64,512]{2,1,0:T(8,128)(2,1)S(1)}, bf16[3,64,512]{2,1,0:T(8,128)(2,1)S(1)}, u32[]{:S(2)}, u32[]{:S(2)}) collective-permute-start(bf16[3,64,512]{2,1,0:T(8,128)(2,1)S(1)} %pad_maximum_fusion.5), channel_id=1, source_target_pairs={{24,32},{88,96},{152,160},{216,224},{56,0},{25,33},{89,97},{153,16... | collective-permute-start | bytes 589832 | tf_op jit(solution)/shard_map/ppermute | solution.py:386
  89.7 2.8 %collective-permute-start.24 = (bf16[64,512]{1,0:T(8,128)(2,1)S(1)}, bf16[64,512]{1,0:T(8,128)(2,1)S(1)}, u32[]{:S(2)}, u32[]{:S(2)}) collective-permute-start(bf16[64,512]{1,0:T(8,128)(2,1)S(1)} %step.9), channel_id=1, source_target_pairs={{24,32},{88,96},{152,160},{216,224},{25,33},{89,97},{153,161},{217... | collective-permute-start | bytes 196616 | tf_op jit(solution)/shard_map/ppermute | solution.py:387
  92.5 13.5 %collective-permute-start.25 = (bf16[4,64,512]{2,1,0:T(8,128)(2,1)S(1)}, bf16[4,64,512]{2,1,0:T(8,128)(2,1)S(1)}, u32[]{:S(2)}, u32[]{:S(2)}) collective-permute-start(bf16[4,64,512]{2,1,0:T(8,128)(2,1)S(1)} %pad_maximum_fusion.4), channel_id=1, source_target_pairs={{32,40},{96,104},{160,168},{224,232},{0,8},{33,41},{97,105},{161,1... | collective-permute-start | bytes 786440 | tf_op jit(solution)/shard_map/ppermute | solution.py:386
  95.7 12.8 %collective-permute-start.26 = (bf16[64,512]{1,0:T(8,128)(2,1)S(1)}, bf16[64,512]{1,0:T(8,128)(2,1)S(1)}, u32[]{:S(2)}, u32[]{:S(2)}) collective-permute-start(bf16[64,512]{1,0:T(8,128)(2,1)S(1)} %step.10), channel_id=1, source_target_pairs={{32,40},{96,104},{160,168},{224,232},{33,41},{97,105},{161,169},{2... | collective-permute-start | bytes 196616 | tf_op jit(solution)/shard_map/ppermute | solution.py:387
  108.5 7.2 %collective-permute-start.27 = (bf16[5,64,512]{2,1,0:T(8,128)(2,1)S(1)}, bf16[5,64,512]{2,1,0:T(8,128)(2,1)S(1)}, u32[]{:S(2)}, u32[]{:S(2)}) collective-permute-start(bf16[5,64,512]{2,1,0:T(8,128)(2,1)S(1)} %pad_maximum_fusion.3), channel_id=1, source_target_pairs={{40,48},{104,112},{168,176},{232,240},{8,16},{41,49},{105,113},{16... | collective-permute-start | bytes 983048 | tf_op jit(solution)/shard_map/ppermute | solution.py:386
  111.5 6.8 %collective-permute-start.28 = (bf16[64,512]{1,0:T(8,128)(2,1)S(1)}, bf16[64,512]{1,0:T(8,128)(2,1)S(1)}, u32[]{:S(2)}, u32[]{:S(2)}) collective-permute-start(bf16[64,512]{1,0:T(8,128)(2,1)S(1)} %step.11), channel_id=1, source_target_pairs={{40,48},{104,112},{168,176},{232,240},{41,49},{105,113},{169,177},... | collective-permute-start | bytes 196616 | tf_op jit(solution)/shard_map/ppermute | solution.py:387
  119.1 7.0 %collective-permute-start.29 = (bf16[6,64,512]{2,1,0:T(8,128)(2,1)}, bf16[6,64,512]{2,1,0:T(8,128)(2,1)}, u32[]{:S(2)}, u32[]{:S(2)}) collective-permute-start(bf16[6,64,512]{2,1,0:T(8,128)(2,1)} %pad_maximum_fusion.2), channel_id=1, source_target_pairs={{48,56},{112,120},{176,184},{240,248},{16,24},{49,57},{113,121},{1... | collective-permute-start | bytes 1179656 | tf_op jit(solution)/shard_map/ppermute | solution.py:386
  122.8 7.5 %collective-permute-start.30 = (bf16[64,512]{1,0:T(8,128)(2,1)}, bf16[64,512]{1,0:T(8,128)(2,1)}, u32[]{:S(2)}, u32[]{:S(2)}) collective-permute-start(bf16[64,512]{1,0:T(8,128)(2,1)} %step.12), channel_id=1, source_target_pairs={{48,56},{112,120},{176,184},{240,248},{49,57},{113,121},{177,185},... | collective-permute-start | bytes 196616 | tf_op jit(solution)/shard_map/ppermute | solution.py:387
  124.1 28.5 %collective-permute-start.44 = (bf16[256,512]{1,0:T(8,128)(2,1)}, bf16[256,512]{1,0:T(8,128)(2,1)S(1)}, u32[]{:S(2)}, u32[]{:S(2)}) collective-permute-start(bf16[256,512]{1,0:T(8,128)(2,1)} %slice.60), channel_id=1, source_target_pairs={{0,2},{1,3},{2,4},{3,5},{4,6},{5,7},{6,0},{7,1},{8,10},{9,11},{10,... | collective-permute-start | bytes 786440 | tf_op jit(solution)/shard_map/ppermute | solution.py:394
  124.4 28.3 %collective-permute-start.45 = (bf16[256,512]{1,0:T(8,128)(2,1)}, bf16[256,512]{1,0:T(8,128)(2,1)S(1)}, u32[]{:S(2)}, u32[]{:S(2)}) collective-permute-start(bf16[256,512]{1,0:T(8,128)(2,1)} %slice.61), channel_id=1, source_target_pairs={{0,6},{1,7},{2,0},{3,1},{4,2},{5,3},{6,4},{7,5},{8,14},{9,15},{10,... | collective-permute-start | bytes 786440 | tf_op jit(solution)/shard_map/ppermute | solution.py:395
  132.3 8.8 %collective-permute-start.37 = (bf16[64,512]{1,0:T(8,128)(2,1)S(1)}, bf16[64,512]{1,0:T(8,128)(2,1)S(1)}, u32[]{:S(2)}, u32[]{:S(2)}) collective-permute-start(bf16[64,512]{1,0:T(8,128)(2,1)S(1)} %select_select_fusion.2.refs_7_.refs_0_), channel_id=1, source_target_pairs={{8,0},{16,8},{24,16},{32,24},{40,32},{48,40},{56,48},{72,64},{80,7... | collective-permute-start | bytes 196616 | tf_op jit(solution)/shard_map/ppermute | solution.py:406
  134.4 10.1 %collective-permute-start.36 = (bf16[64,512]{1,0:T(8,128)(2,1)S(1)}, bf16[64,512]{1,0:T(8,128)(2,1)S(1)}, u32[]{:S(2)}, u32[]{:S(2)}) collective-permute-start(bf16[64,512]{1,0:T(8,128)(2,1)S(1)} %select_select_fusion.2.refs_7_.refs_0_), channel_id=1, source_target_pairs={{16,0},{24,8},{32,16},{40,24},{48,32},{56,40},{80,64},{88,72},{96,... | collective-permute-start | bytes 196616 | tf_op jit(solution)/shard_map/ppermute | solution.py:406
  135.7 13.5 %collective-permute-start.35 = (bf16[64,512]{1,0:T(8,128)(2,1)S(1)}, bf16[64,512]{1,0:T(8,128)(2,1)S(1)}, u32[]{:S(2)}, u32[]{:S(2)}) collective-permute-start(bf16[64,512]{1,0:T(8,128)(2,1)S(1)} %select_select_fusion.2.refs_7_.refs_0_), channel_id=1, source_target_pairs={{24,0},{32,8},{40,16},{48,24},{56,32},{88,64},{96,72},{104,80},{11... | collective-permute-start | bytes 196616 | tf_op jit(solution)/shard_map/ppermute | solution.py:406
  150.5 25.1 %collective-permute-start.39 = (bf16[4,64,512]{2,1,0:T(8,128)(2,1)S(1)}, bf16[4,64,512]{2,1,0:T(8,128)(2,1)S(1)}, u32[]{:S(2)}, u32[]{:S(2)}) collective-permute-start(bf16[4,64,512]{2,1,0:T(8,128)(2,1)S(1)} %collect.3.refs_1_), channel_id=1, source_target_pairs={{0,192},{8,200},{16,208},{24,216},{32,224},{40,232},{48,240},{56,2... | collective-permute-start | bytes 786440 | tf_op jit(solution)/shard_map/ppermute | solution.py:411
  150.6 25.0 %collective-permute-start.38 = (bf16[4,64,512]{2,1,0:T(8,128)(2,1)S(1)}, bf16[4,64,512]{2,1,0:T(8,128)(2,1)S(1)}, u32[]{:S(2)}, u32[]{:S(2)}) collective-permute-start(bf16[4,64,512]{2,1,0:T(8,128)(2,1)S(1)} %collect.3.refs_1_), channel_id=1, source_target_pairs={{0,64},{8,72},{16,80},{24,88},{32,96},{40,104},{48,112},{56,120},{... | collective-permute-start | bytes 786440 | tf_op jit(solution)/shard_map/ppermute | solution.py:410
  152.7 41.1 %collective-permute-start.46 = (bf16[512,512]{1,0:T(8,128)(2,1)S(1)}, bf16[512,512]{1,0:T(8,128)(2,1)S(1)}, u32[]{:S(2)}, u32[]{:S(2)}) collective-permute-start(bf16[512,512]{1,0:T(8,128)(2,1)S(1)} %hold.9.refs_11_), channel_id=1, source_target_pairs={{0,1},{1,0},{2,3},{3,2},{4,5},{5,4},{6,7},{7,6},{8,9},{9,8},{10,11... | collective-permute-start | bytes 1572872 | tf_op jit(solution)/shard_map/ppermute | solution.py:403
  152.8 2.0 collective-permute-start.34
  153.4 11.0 %collective-permute-start.33 = (bf16[64,512]{1,0:T(8,128)(2,1)S(1)}, bf16[64,512]{1,0:T(8,128)(2,1)S(1)}, u32[]{:S(2)}, u32[]{:S(2)}) collective-permute-start(bf16[64,512]{1,0:T(8,128)(2,1)S(1)} %select_select_fusion.2.refs_7_.refs_0_), channel_id=1, source_target_pairs={{48,0},{56,8},{112,64},{120,72},{176,128},{184,136},{240,192},{248... | collective-permute-start | bytes 196616 | tf_op jit(solution)/shard_map/ppermute | solution.py:406
  154.7 11.0 %collective-permute-start.32 = (bf16[64,512]{1,0:T(8,128)(2,1)S(1)}, bf16[64,512]{1,0:T(8,128)(2,1)S(1)}, u32[]{:S(2)}, u32[]{:S(2)}) collective-permute-start(bf16[64,512]{1,0:T(8,128)(2,1)S(1)} %select_select_fusion.2.refs_7_.refs_0_), channel_id=1, source_target_pairs={{40,0},{48,8},{56,16},{104,64},{112,72},{120,80},{168,128},{176,13... | collective-permute-start | bytes 196616 | tf_op jit(solution)/shard_map/ppermute | solution.py:406
  164.4 10.1 %collective-permute-start.31 = (bf16[64,512]{1,0:T(8,128)(2,1)S(1)}, bf16[64,512]{1,0:T(8,128)(2,1)S(1)}, u32[]{:S(2)}, u32[]{:S(2)}) collective-permute-start(bf16[64,512]{1,0:T(8,128)(2,1)S(1)} %select_select_fusion.2.refs_7_.refs_0_), channel_id=1, source_target_pairs={{32,0},{40,8},{48,16},{56,24},{96,64},{104,72},{112,80},{120,88},{... | collective-permute-start | bytes 196616 | tf_op jit(solution)/shard_map/ppermute | solution.py:406
  175.6 13.1 %collective-permute-start.41 = (bf16[4,64,512]{2,1,0:T(8,128)(2,1)S(1)}, bf16[4,64,512]{2,1,0:T(8,128)(2,1)S(1)}, u32[]{:S(2)}, u32[]{:S(2)}) collective-permute-start(bf16[4,64,512]{2,1,0:T(8,128)(2,1)S(1)} %collect.2.refs_1_), channel_id=1, source_target_pairs={{0,64},{8,72},{16,80},{24,88},{32,96},{40,104},{48,112},{56,120},{... | collective-permute-start | bytes 786440 | tf_op jit(solution)/shard_map/ppermute | solution.py:222
  175.7 13.9 %collective-permute-start.40 = (bf16[4,64,512]{2,1,0:T(8,128)(2,1)S(1)}, bf16[4,64,512]{2,1,0:T(8,128)(2,1)S(1)}, u32[]{:S(2)}, u32[]{:S(2)}) collective-permute-start(bf16[4,64,512]{2,1,0:T(8,128)(2,1)S(1)} %collect.2.refs_1_), channel_id=1, source_target_pairs={{0,192},{8,200},{16,208},{24,216},{32,224},{40,232},{48,240},{56,2... | collective-permute-start | bytes 786440 | tf_op jit(solution)/shard_map/ppermute | solution.py:223
  178.9 14.8 %collective-permute-start.47 = (bf16[4,64,512]{2,1,0:T(8,128)(2,1)S(1)}, bf16[4,64,512]{2,1,0:T(8,128)(2,1)S(1)}, u32[]{:S(2)}, u32[]{:S(2)}) collective-permute-start(bf16[4,64,512]{2,1,0:T(8,128)(2,1)S(1)} %collect.3.refs_1_), channel_id=1, source_target_pairs={{0,128},{8,136},{16,144},{24,152},{32,160},{40,168},{48,176},{56,1... | collective-permute-start | bytes 786440 | tf_op jit(solution)/shard_map/ppermute | solution.py:412
  188.7 10.0 %collective-permute-start.42 = (bf16[2,64,512]{2,1,0:T(8,128)(2,1)S(1)}, bf16[2,64,512]{2,1,0:T(8,128)(2,1)S(1)}, u32[]{:S(2)}, u32[]{:S(2)}) collective-permute-start(bf16[2,64,512]{2,1,0:T(8,128)(2,1)S(1)} %slice.73), channel_id=1, source_target_pairs={{0,64},{8,72},{16,80},{24,88},{32,96},{40,104},{48,112},{56,120},{... | collective-permute-start | bytes 393224 | tf_op jit(solution)/shard_map/ppermute | solution.py:224
  189.6 9.1 %collective-permute-start.43 = (bf16[2,64,512]{2,1,0:T(8,128)(2,1)S(1)}, bf16[2,64,512]{2,1,0:T(8,128)(2,1)S(1)}, u32[]{:S(2)}, u32[]{:S(2)}) collective-permute-start(bf16[2,64,512]{2,1,0:T(8,128)(2,1)S(1)} %slice.74), channel_id=1, source_target_pairs={{0,192},{8,200},{16,208},{24,216},{32,224},{40,232},{48,240},{56,2... | collective-permute-start | bytes 393224 | tf_op jit(solution)/shard_map/ppermute | solution.py:225
  (51 other events, 630.1 us)
where the time goes:
time: 206 us; the launch traced here: 204 us
  waiting for transfers between devices  91.8 us (45%)
  starting transfers between devices  52.8 us (26%)
  Pallas kernels  40.7 us (20%)
  local copies, waits for them, and re-layouts  13.6 us (7%)
  other arithmetic  3.3 us (2%)
    ppermute x7, waiting for transfers between devices, on_device(): lax.ppermute(own_s, 'row', back_z(d, range(1 if d < 4 else 4, 8)))  29.4 us
    ppermute x6, waiting for transfers between devices, on_device(): sent = lax.ppermute(known, 'row', hop_z_early(t))  13.3 us
    pallas_call x6, Pallas kernels, early(): pl.pallas_call(early_kernel, out_shape=jax.ShapeDtypeStruct((c, b), F32),...  13.2 us
    pallas_call x7, Pallas kernels, step(): pl.pallas_call(lambda *refs: step_kernel(t, *refs), out_shape=jax.ShapeDt...  12.4 us
    pallas_call x2, Pallas kernels, final(): pl.pallas_call(lambda *refs: final_kernel(start, *refs), out_shape=(jax.S...  10.2 us
    ppermute x1, waiting for transfers between devices, spread_y(): before = lax.ppermute(rows, 'row', shift_y(1))  9.77 us
    ppermute x7, starting transfers between devices, on_device(): lax.ppermute(own_s, 'row', back_z(d, range(1 if d < 4 else 4, 8)))  9.17 us
    unnamed x103, local copies, waits for them, and re-layouts  9.12 us
  transfers between devices with their start and end apart: 48, of which 19 were waited for; matrix products, arithmetic and copies ran while one was open for 3% of the time, Pallas kernels for 17%

commit v1 on v0

--- a/solution.py
+++ b/solution.py
@@ -50,6 +50,7 @@
 
 VMEM = pl.BlockSpec(memory_space=pltpu.VMEM)
 SMEM = pl.BlockSpec(memory_space=pltpu.SMEM)
+ANY = pl.BlockSpec(memory_space=pl.ANY)
 LIMIT = 8 * 1024 * 1024
 PLACE, KIND, ROWS, AT_Z, PLANE = 0, 8, 16, 17, 18
 
@@ -69,8 +70,10 @@
             use(lax.dot_general(*pair, NT, preferred_element_type=F32))
 
 
-def early_kernel(sc, base, solved, *refs):
-    *blocks, out = refs
+def early_kernel(t, sc, base, solved, inverse, *refs):
+    *blocks, out, inv, sem = refs
+    fetch = pltpu.make_async_copy(inverse.at[t], inv, sem)
+    fetch.start()
     out[...] = base[...].astype(F32)
 
     def subtract(value):
@@ -80,21 +83,27 @@
     def _(j):
         times_block(sc, j, solved[j], blocks, subtract)
 
-
-def early(sc, base, solved, blocks):
+    fetch.wait()
+
+
+def early(t, sc, base, solved, inverse, blocks):
     n = solved.shape[0]
     c, b = base.shape
     return pl.pallas_call(
-        early_kernel,
-        out_shape=jax.ShapeDtypeStruct((c, b), F32),
-        in_specs=[SMEM] + [VMEM] * (2 + len(blocks)),
-        out_specs=VMEM,
+        lambda *refs: early_kernel(t, *refs),
+        out_shape=(
+            jax.ShapeDtypeStruct((c, b), F32),
+            jax.ShapeDtypeStruct((b, b), BF),
+        ),
+        in_specs=[SMEM, VMEM, VMEM, ANY] + [VMEM] * len(blocks),
+        out_specs=(VMEM, VMEM),
+        scratch_shapes=[pltpu.SemaphoreType.DMA],
         compiler_params=params(),
         cost_estimate=pl.CostEstimate(
             flops=2 * n * c * b * b, bytes_accessed=n * b * b, transcendentals=0
         ),
         name="early",
-    )(sc, base, solved, *blocks)
+    )(sc, base, solved, inverse, *blocks)
 
 
 def step_kernel(t, sc, acc, last, inv, *refs):
@@ -105,7 +114,7 @@
 
     times_block(sc, t - 1, last[...], blocks, subtract)
     out[...] = lax.dot_general(
-        base[...], inv[t], NT, preferred_element_type=F32
+        base[...], inv[...], NT, preferred_element_type=F32
     ).astype(BF)
 
 
@@ -125,21 +134,32 @@
     )(sc, acc, last, inv, *blocks)
 
 
-def first_kernel(base, inv, out):
+def first_kernel(base, inverse, out, inv, here, sems):
+    own = pltpu.make_async_copy(inverse.at[0], here, sems.at[0])
+    following = pltpu.make_async_copy(inverse.at[1], inv, sems.at[1])
+    own.start()
+    following.start()
+    own.wait()
     out[...] = lax.dot_general(
-        base[...], inv[0], NT, preferred_element_type=F32
+        base[...], here[...], NT, preferred_element_type=F32
     ).astype(BF)
-
-
-def first(base, inv):
+    following.wait()
+
+
+def first(base, inverse):
+    square = inverse.shape[1:]
     return pl.pallas_call(
         first_kernel,
-        out_shape=jax.ShapeDtypeStruct(base.shape, BF),
-        in_specs=[VMEM, VMEM],
-        out_specs=VMEM,
+        out_shape=(
+            jax.ShapeDtypeStruct(base.shape, BF),
+            jax.ShapeDtypeStruct(square, BF),
+        ),
+        in_specs=[VMEM, ANY],
+        out_specs=(VMEM, VMEM),
+        scratch_shapes=[pltpu.VMEM(square, BF), pltpu.SemaphoreType.DMA((2,))],
         compiler_params=params(),
         name="first",
-    )(base, inv)
+    )(base, inverse)
 
 
 def hold(parts, stack=False):
@@ -360,9 +380,8 @@
     zr = [lax.ppermute(ready[i], "row", from_plane(3, i)) for i in range(NY - 1)]
     near1 = hold([after(panel1, zr[0]), left1, right1], stack=True)
     near_other1 = lax.ppermute(near1, "col", SWAP)
-    inverse = hold([inverse])
-    left, right, near_other1, left1, right1, inverse, *zr = lax.optimization_barrier(
-        (left, right, near_other1, left1[:half], right1[half:], inverse, *zr)
+    left, right, near_other1, left1, right1, *zr = lax.optimization_barrier(
+        (left, right, near_other1, left1[:half], right1[half:], *zr)
     )
     base = by_plane(*zr, zq[3])
     far_a, far_b = left[:half], right[half:]
@@ -375,18 +394,19 @@
     far_other = hold([lax.ppermute(far, "col", SWAP)])
     blocks0 = [near, far, near_other, far_other]
 
-    fresh = first(base, inverse)
+    fresh, inv = first(base, inverse)
     own_s = fresh
     acc = base.astype(F32)
     known = None
     before = {0: []}
+    back_a = []
     for t in range(1, steps):
         sent = None
         if t > 1:
             sent = lax.ppermute(known, "row", hop_z_early(t))
         last = lax.ppermute(fresh, "row", hop_z(t))
         if t > 1:
-            acc = early(sc, base, after(sent, fresh), blocks0)
+            acc, inv = early(t, sc, base, after(sent, fresh), inverse, blocks0)
             last = after(last, acc)
         if t == 2:
             left1, right1 = after(left1, acc), after(right1, acc)
@@ -394,25 +414,30 @@
                 lax.ppermute(left1, "col", shift_x(1)),
                 lax.ppermute(right1, "col", shift_x(-1)),
             ]
-        fresh = step(t, sc, acc, last, inverse, blocks0)
+        if 4 <= t <= 6:
+            back_a.append(
+                lax.ppermute((back_a or [own_s])[-1], "row", back_z(1, range(1, 4)))
+            )
+        if t > 4:
+            last = after(last, back_a[t - 5])
+        if t == 7:
+            rows_a = collect(sc, range(4), own_s, {**before, 7: [sent]}, back_a)
+            acc, rows_a = lax.optimization_barrier((acc, rows_a))
+            before_a = lax.ppermute(rows_a, "row", shift_y(1))
+            behind_a = lax.ppermute(rows_a, "row", shift_y(-1))
+            far_a = lax.ppermute(rows_a, "row", shift_y(2))
+            pieces_a = (rows_a, behind_a, far_a, far_a, before_a)
+        fresh = step(t, sc, acc, last, inv, blocks0)
         own_s = jnp.where(z == t, fresh, own_s)
         before[t] = [last] if t == 1 else [sent, last]
         known = last[None] if t == 1 else jnp.concatenate([sent, last[None]])
 
-    far1 = hold([after(far1[0], fresh), far1[1]])
+    back = [lax.ppermute(own_s, "row", back_z(d, range(4, 8))) for d in range(1, 8)]
+    rows_b = collect(sc, range(4, 8), own_s, before, back)
+    far1 = hold([after(far1[0], rows_b), far1[1]])
     far_other1 = lax.ppermute(far1, "col", SWAP)
     blocks1 = [near1, far1, near_other1, far_other1]
-    back = [
-        lax.ppermute(own_s, "row", back_z(d, range(1 if d < 4 else 4, 8)))
-        for d in range(1, 8)
-    ]
-    rows_a = collect(sc, range(4), own_s, before, back)
-    before_a = lax.ppermute(rows_a, "row", shift_y(1))
-    behind_a = lax.ppermute(rows_a, "row", shift_y(-1))
-    far_a = lax.ppermute(rows_a, "row", shift_y(2))
-    pieces_a = (rows_a, behind_a, far_a, far_a, before_a)
     out_s, rest = final(0, sc, steps, pieces_a, blocks0, blocks1, rhs)
-    rows_b = collect(sc, range(4, 8), own_s, before, back)
     rows_b = after(rows_b, before_a, behind_a)
     pieces_b = spread_y(rows_b)
     return tuple(final(4, sc, steps, pieces_b, blocks0, blocks1, rest, out_s))

time: 206 us -> 210 us (1.019)
  the two profiles are of different devices: /device:TPU:34 before, /device:TPU:2 now
where the time goes in v1:
time: 210 us; the launch traced here: 206 us
  waiting for transfers between devices  84.8 us (40%)
  starting transfers between devices  57.4 us (27%)
  Pallas kernels  40.3 us (19%)
  local copies, waits for them, and re-layouts  18 us (9%)
  other arithmetic  3.97 us (2%)
    ppermute x7, waiting for transfers between devices, on_device(): lax.ppermute(own_s, 'row', back_z(d, range(4, 8)))  22.7 us
    pallas_call x6, Pallas kernels, early(): pl.pallas_call(lambda *refs: early_kernel(t, *refs), out_shape=(jax.Shape...  13.5 us
    unnamed x133, local copies, waits for them, and re-layouts  13.4 us
    ppermute x1, waiting for transfers between devices, spread_y(): before = lax.ppermute(rows, 'row', shift_y(1))  12.2 us
    pallas_call x7, Pallas kernels, step(): pl.pallas_call(lambda *refs: step_kernel(t, *refs), out_shape=jax.ShapeDt...  12 us
    ppermute x6, waiting for transfers between devices, on_device(): sent = lax.ppermute(known, 'row', hop_z_early(t))  11.8 us
    pallas_call x2, Pallas kernels, final(): pl.pallas_call(lambda *refs: final_kernel(start, *refs), out_shape=(jax.S...  10.2 us
    ppermute x1, waiting for transfers between devices, on_device(): right = lax.ppermute(window, 'col', shift_x(-1))  9.39 us
  transfers between devices with their start and end apart: 51, of which 15 were waited for; matrix products, arithmetic and copies ran while one was open for 3% of the time, Pallas kernels for 16%

profile of v1, /device:TPU:2, one launch (start us, length us, event | category | flops | bytes accessed | tf_op | source)
XLA Modules:
  0.0 206.5 jit_solution(15295101261195902678)
XLA Ops:
  1.8 1.3 collective-permute-start
  3.1 1.4 collective-permute-start.4
  4.5 4.3 %collective-permute-start.1 = (bf16[256,512]{1,0:T(8,128)(2,1)S(1)}, bf16[256,512]{1,0:T(8,128)(2,1)}, u32[]{:S(2)}, u32[]{:S(2)}) collective-permute-start(bf16[256,512]{1,0:T(8,128)(2,1)S(1)} %get-tuple-element.118), channel_id=1, source_target_pairs={{192,128},{200,136},{208,144},{216,152},{224,160},{232,168},{240,1... | collective-permute-start | bytes 786440 | tf_op jit(solution)/shard_map/ppermute | solution.py:357
  14.3 1.7 collective-permute-start.2
  16.1 1.4 collective-permute-start.5
  18.1 2.9 %collective-permute-done.10 = bf16[64,512]{1,0:T(8,128)(2,1)S(1)} collective-permute-done((bf16[64,512]{1,0:T(8,128)(2,1)S(1)}, bf16[64,512]{1,0:T(8,128)(2,1)S(1)}, u32[]{:S(2)}, u32[]{:S(2)}) %collective-permute-start.10) | collective-permute-done | bytes 65568 | tf_op jit(solution)/shard_map/ppermute | solution.py:380
  21.0 1.5 collective-permute-start.6
  23.8 6.9 %collective-permute-done.7.refs_2_ = bf16[512,512]{1,0:T(8,128)(2,1)S(1)} collective-permute-done((bf16[512,512]{1,0:T(8,128)(2,1)S(1)}, bf16[512,512]{1,0:T(8,128)(2,1)S(1)}, u32[]{:S(2)}, u32[]{:S(2)}) %collective-permute-start.7) | collective-permute-done | bytes 524320 | tf_op jit(solution)/shard_map/ppermute | solution.py:372
  30.7 3.0 %collective-permute-done.6.refs_1_ = bf16[512,512]{1,0:T(8,128)(2,1)S(1)} collective-permute-done((bf16[512,512]{1,0:T(8,128)(2,1)S(1)}, bf16[512,512]{1,0:T(8,128)(2,1)S(1)}, u32[]{:S(2)}, u32[]{:S(2)}) %collective-permute-start.6) | collective-permute-done | bytes 524320 | tf_op jit(solution)/shard_map/ppermute | solution.py:371
  33.9 1.6 collective-permute-start.9
  38.8 9.4 %collective-permute-done.9 = bf16[512,512]{1,0:T(8,128)(2,1)S(1)} collective-permute-done((bf16[512,512]{1,0:T(8,128)(2,1)S(1)}, bf16[512,512]{1,0:T(8,128)(2,1)S(1)}, u32[]{:S(2)}, u32[]{:S(2)}) %collective-permute-start.9) | collective-permute-done | bytes 524320 | tf_op jit(solution)/shard_map/ppermute | solution.py:376
  51.0 3.0 %collective-permute-start.17 = (bf16[256,512]{1,0:T(8,128)(2,1)S(1)}, bf16[256,512]{1,0:T(8,128)(2,1)S(1)}, u32[]{:S(2)}, u32[]{:S(2)}) collective-permute-start(bf16[256,512]{1,0:T(8,128)(2,1)S(1)} %slice.65), channel_id=1, source_target_pairs={{0,6},{1,7},{2,0},{3,1},{4,2},{5,3},{6,4},{7,5},{8,14},{9,15},{10,... | collective-permute-start | bytes 786440 | tf_op jit(solution)/shard_map/ppermute | solution.py:390
  54.0 6.1 %collective-permute-done.17.refs_1_ = bf16[256,512]{1,0:T(8,128)(2,1)S(1)} collective-permute-done((bf16[256,512]{1,0:T(8,128)(2,1)S(1)}, bf16[256,512]{1,0:T(8,128)(2,1)S(1)}, u32[]{:S(2)}, u32[]{:S(2)}) %collective-permute-start.17) | collective-permute-done | bytes 262176 | tf_op jit(solution)/shard_map/ppermute | solution.py:390
  60.2 2.2 %collective-permute-done.16.refs_0_ = bf16[256,512]{1,0:T(8,128)(2,1)S(1)} collective-permute-done((bf16[256,512]{1,0:T(8,128)(2,1)S(1)}, bf16[256,512]{1,0:T(8,128)(2,1)S(1)}, u32[]{:S(2)}, u32[]{:S(2)}) %collective-permute-start.16) | collective-permute-done | bytes 262176 | tf_op jit(solution)/shard_map/ppermute | solution.py:389
  64.2 2.2 %copy-done = bf16[8,512,512]{2,1,0:T(8,128)(2,1)S(1)} copy-done((bf16[8,512,512]{2,1,0:T(8,128)(2,1)S(1)}, bf16[8,512,512]{2,1,0:T(8,128)(2,1)}, u32[]{:S(2)}) %copy-start) | copy-done | bytes 4194328
  67.5 3.4 %collective-permute-start.14 = (bf16[64,512]{1,0:T(8,128)(2,1)S(1)}, bf16[64,512]{1,0:T(8,128)(2,1)S(1)}, u32[]{:S(2)}, u32[]{:S(2)}) collective-permute-start(bf16[64,512]{1,0:T(8,128)(2,1)S(1)} %get-tuple-element.68), channel_id=1, source_target_pairs={{0,8},{64,72},{128,136},{192,200},{1,9},{65,73},{129,137},{193,201... | collective-permute-start | bytes 196616 | tf_op jit(solution)/shard_map/ppermute | solution.py:407
  71.1 1.9 collective-permute-done.14.refs_2_.refs_4_
  76.0 1.8 step.7
  78.5 1.4 early.6
  80.7 1.6 step.8
  83.0 1.8 early.7
  86.8 1.6 step.9
  89.2 8.1 %collective-permute-done.23.refs_2_.refs_9_ = bf16[3,64,512]{2,1,0:T(8,128)(2,1)S(1)} collective-permute-done((bf16[3,64,512]{2,1,0:T(8,128)(2,1)}, bf16[3,64,512]{2,1,0:T(8,128)(2,1)S(1)}, u32[]{:S(2)}, u32[]{:S(2)}) %collective-permute-start.23) | collective-permute-done | bytes 196640 | tf_op jit(solution)/shard_map/ppermute | solution.py:406
  97.3 2.2 %copy-done.2 = bf16[8,512,512]{2,1,0:T(8,128)(2,1)S(1)} copy-done((bf16[8,512,512]{2,1,0:T(8,128)(2,1)S(1)}, bf16[8,512,512]{2,1,0:T(8,128)(2,1)}, u32[]{:S(2)}) %copy-start.2) | copy-done | bytes 4194328
  100.5 2.1 %early.8 = (f32[64,512]{1,0:T(8,128)S(1)}, bf16[512,512]{1,0:T(8,128)(2,1)S(1)}) custom-call(s32[22]{0:T(128)S(1)} %concatenate.21.refs_0_.sc, bf16[64,512]{1,0:T(8,128)(2,1)S(1)} %get-tuple-element.115.base.refs_1_, bf16[3,64,512]{2,1,0:T(8,128)(2,1)S(1)} %collective-permute-done.23.refs_2_.refs_9_, bf16[8,512,512]{2,1,0:T(8,128)(2,1)S(1)} %copy-done.2, ...), custom_call_target="tpu_custom_call" | custom-call | flops 100663296 | bytes 786432 | tf_op jit(solution)/shard_map/early/pallas_call | solution.py:92
  102.8 1.8 step.10
  105.5 1.3 collective-permute-start.25
  106.9 1.3 collective-permute-start.27
  108.2 3.7 %collective-permute-done.25.refs_2_.refs_11_ = bf16[4,64,512]{2,1,0:T(8,128)(2,1)S(1)} collective-permute-done((bf16[4,64,512]{2,1,0:T(8,128)(2,1)S(1)}, bf16[4,64,512]{2,1,0:T(8,128)(2,1)S(1)}, u32[]{:S(2)}, u32[]{:S(2)}) %collective-permute-start.25) | collective-permute-done | bytes 262176 | tf_op jit(solution)/shard_map/ppermute | solution.py:406
  111.8 2.4 %early.9 = (f32[64,512]{1,0:T(8,128)S(1)}, bf16[512,512]{1,0:T(8,128)(2,1)S(1)}) custom-call(s32[22]{0:T(128)S(1)} %concatenate.21.refs_0_.sc, bf16[64,512]{1,0:T(8,128)(2,1)S(1)} %get-tuple-element.115.base.refs_1_, bf16[4,64,512]{2,1,0:T(8,128)(2,1)S(1)} %collective-permute-done.25.refs_2_.refs_11_, bf16[8,512,512]{2,1,0:T(8,128)(2,1)S(1)} %copy-done.3, ...), custom_call_target="tpu_custom_call" | custom-call | flops 134217728 | bytes 1048576 | tf_op jit(solution)/shard_map/early/pallas_call | solution.py:92
  115.1 1.6 step.11
  117.4 1.3 collective-permute-start.30
  118.7 2.6 %early.10 = (f32[64,512]{1,0:T(8,128)S(1)}, bf16[512,512]{1,0:T(8,128)(2,1)S(1)}) custom-call(s32[22]{0:T(128)S(1)} %concatenate.21.refs_0_.sc, bf16[64,512]{1,0:T(8,128)(2,1)S(1)} %get-tuple-element.115.base.refs_1_, bf16[5,64,512]{2,1,0:T(8,128)(2,1)S(1)} %collective-permute-done.28.refs_2_.refs_12_.refs_9_, bf16[8,512,512]{2,1,0:T(8,128)(2,1)S(1)} %copy-done.3, ...), custom_call_target="tpu_custom_call" | custom-call | flops 167772160 | bytes 1310720 | tf_op jit(solution)/shard_map/early/pallas_call | solution.py:92
  121.4 3.2 %collective-permute-done.30.refs_2_ = bf16[64,512]{1,0:T(8,128)(2,1)S(1)} collective-permute-done((bf16[64,512]{1,0:T(8,128)(2,1)S(1)}, bf16[64,512]{1,0:T(8,128)(2,1)S(1)}, u32[]{:S(2)}, u32[]{:S(2)}) %collective-permute-start.30) | collective-permute-done | bytes 65568 | tf_op jit(solution)/shard_map/ppermute | solution.py:419
  126.1 1.4 collective-permute-start.31
  127.8 1.7 collective-permute-start.48
  134.7 1.8 step.12
  137.3 3.1 %early.11 = (f32[64,512]{1,0:T(8,128)S(1)}, bf16[512,512]{1,0:T(8,128)(2,1)S(1)}) custom-call(s32[22]{0:T(128)S(1)} %concatenate.21.refs_0_.sc, bf16[64,512]{1,0:T(8,128)(2,1)S(1)} %get-tuple-element.115.base.refs_1_, bf16[6,64,512]{2,1,0:T(8,128)(2,1)} %collective-permute-done.31.refs_2_.refs_13_.refs_11_, bf16[8,512,512]{2,1,0:T(8,128)(2,1)S(1)} %copy-done.4, ...), custom_call_target="tpu_custom_call" | custom-call | flops 201326592 | bytes 1572864 | tf_op jit(solution)/shard_map/early/pallas_call | solution.py:92
  141.7 1.7 step.13
  145.8 1.3 collective-permute-start.37
  149.7 16.0 %collective-permute-done.37.refs_3_ = bf16[64,512]{1,0:T(8,128)(2,1)S(1)} collective-permute-done((bf16[64,512]{1,0:T(8,128)(2,1)S(1)}, bf16[64,512]{1,0:T(8,128)(2,1)S(1)}, u32[]{:S(2)}, u32[]{:S(2)}) %collective-permute-start.37) | collective-permute-done | bytes 65568 | tf_op jit(solution)/shard_map/ppermute | solution.py:435
  167.1 2.0 collective-permute-start.41
  169.2 6.6 %collective-permute-done.34.refs_0_ = bf16[64,512]{1,0:T(8,128)(2,1)S(1)} collective-permute-done((bf16[64,512]{1,0:T(8,128)(2,1)S(1)}, bf16[64,512]{1,0:T(8,128)(2,1)S(1)}, u32[]{:S(2)}, u32[]{:S(2)}) %collective-permute-start.34) | collective-permute-done | bytes 65568 | tf_op jit(solution)/shard_map/ppermute | solution.py:435
  177.2 3.2 %collective-permute-start.43 = (bf16[4,64,512]{2,1,0:T(8,128)(2,1)S(1)}, bf16[4,64,512]{2,1,0:T(8,128)(2,1)S(1)}, u32[]{:S(2)}, u32[]{:S(2)}) collective-permute-start(bf16[4,64,512]{2,1,0:T(8,128)(2,1)S(1)} %collect.3.refs_1_), channel_id=1, source_target_pairs={{0,192},{8,200},{16,208},{24,216},{32,224},{40,232},{48,240},{56,2... | collective-permute-start | bytes 786440 | tf_op jit(solution)/shard_map/ppermute | solution.py:243
  180.4 12.2 %collective-permute-done.44.refs_5_ = bf16[4,64,512]{2,1,0:T(8,128)(2,1)S(1)} collective-permute-done((bf16[4,64,512]{2,1,0:T(8,128)(2,1)S(1)}, bf16[4,64,512]{2,1,0:T(8,128)(2,1)S(1)}, u32[]{:S(2)}, u32[]{:S(2)}) %collective-permute-start.44) | collective-permute-done | bytes 262176 | tf_op jit(solution)/shard_map/ppermute | solution.py:242
  192.7 3.5 %collective-permute-start.46 = (bf16[2,64,512]{2,1,0:T(8,128)(2,1)S(1)}, bf16[2,64,512]{2,1,0:T(8,128)(2,1)S(1)}, u32[]{:S(2)}, u32[]{:S(2)}) collective-permute-start(bf16[2,64,512]{2,1,0:T(8,128)(2,1)S(1)} %slice.74), channel_id=1, source_target_pairs={{0,192},{8,200},{16,208},{24,216},{32,224},{40,232},{48,240},{56,2... | collective-permute-start | bytes 393224 | tf_op jit(solution)/shard_map/ppermute | solution.py:245
  196.3 4.9 %final.2 = (f32[8,512,256]{2,1,0:T(8,128)}, f32[2,1,512,256]{3,2,1,0:T(8,128)S(1)}) custom-call(s32[22]{0:T(128)S(1)} %concatenate.21.refs_0_.sc, bf16[4,64,512]{2,1,0:T(8,128)(2,1)S(1)} %collect.2.refs_1_, bf16[4,64,512]{2,1,0:T(8,128)(2,1)S(1)} %collective-permute-done.42.refs_2_, bf16[4,64,512]{2,1,0:T(8,128)(2,1)S(1)} %collective-permute-done.50.refs_3_.refs_4_, ...), custom_call_target="tpu_custom_call" | custom-call | flops 1610612736 | bytes 2097152 | tf_op jit(solution)/shard_map/final/pallas_call | solution.py:308
  201.2 5.3 %final.3 = (f32[8,512,256]{2,1,0:T(8,128)}, f32[2,1,512,256]{3,2,1,0:T(8,128)}) custom-call(s32[22]{0:T(128)S(1)} %concatenate.21.refs_0_.sc, bf16[4,64,512]{2,1,0:T(8,128)(2,1)S(1)} %collect.3.refs_1_, bf16[4,64,512]{2,1,0:T(8,128)(2,1)S(1)} %collective-permute-done.43.refs_2_, ...), custom_call_target="tpu_custom_call", output_to_operand_aliasing={{0}: (15, {})} | custom-call | flops 1610612736 | bytes 2097152 | tf_op jit(solution)/shard_map/final/pallas_call | solution.py:308
  (234 shorter events, 45.2 us)
Async XLA Ops:
  1.8 11.3 %collective-permute-start = (bf16[256,512]{1,0:T(8,128)(2,1)S(1)}, bf16[256,512]{1,0:T(8,128)(2,1)}, u32[]{:S(2)}, u32[]{:S(2)}) collective-permute-start(bf16[256,512]{1,0:T(8,128)(2,1)S(1)} %get-tuple-element.118), channel_id=1, source_target_pairs={{192,0},{200,8},{208,16},{216,24},{224,32},{232,40},{240,48},{248,... | collective-permute-start | bytes 786440 | tf_op jit(solution)/shard_map/ppermute | solution.py:354
  3.1 13.0 %collective-permute-start.4 = (bf16[256,512]{1,0:T(8,128)(2,1)S(1)}, bf16[256,512]{1,0:T(8,128)(2,1)}, u32[]{:S(2)}, u32[]{:S(2)}) collective-permute-start(bf16[256,512]{1,0:T(8,128)(2,1)S(1)} %get-tuple-element.119), channel_id=1, source_target_pairs={{192,128},{200,136},{208,144},{216,152},{224,160},{232,168},{240,1... | collective-permute-start | bytes 786440 | tf_op jit(solution)/shard_map/ppermute | solution.py:355
  4.5 13.0 %collective-permute-start.1 = (bf16[256,512]{1,0:T(8,128)(2,1)S(1)}, bf16[256,512]{1,0:T(8,128)(2,1)}, u32[]{:S(2)}, u32[]{:S(2)}) collective-permute-start(bf16[256,512]{1,0:T(8,128)(2,1)S(1)} %get-tuple-element.118), channel_id=1, source_target_pairs={{192,128},{200,136},{208,144},{216,152},{224,160},{232,168},{240,1... | collective-permute-start | bytes 786440 | tf_op jit(solution)/shard_map/ppermute | solution.py:357
  8.8 13.8 %collective-permute-start.3 = (bf16[256,512]{1,0:T(8,128)(2,1)S(1)}, bf16[256,512]{1,0:T(8,128)(2,1)}, u32[]{:S(2)}, u32[]{:S(2)}) collective-permute-start(bf16[256,512]{1,0:T(8,128)(2,1)S(1)} %get-tuple-element.119), channel_id=1, source_target_pairs={{192,0},{200,8},{208,16},{216,24},{224,32},{232,40},{240,48},{248,... | collective-permute-start | bytes 786440 | tf_op jit(solution)/shard_map/ppermute | solution.py:356
  13.1 8.0 %collective-permute-start.10 = (bf16[64,512]{1,0:T(8,128)(2,1)S(1)}, bf16[64,512]{1,0:T(8,128)(2,1)S(1)}, u32[]{:S(2)}, u32[]{:S(2)}) collective-permute-start(bf16[64,512]{1,0:T(8,128)(2,1)S(1)} %get-tuple-element.59), channel_id=1, source_target_pairs={{192,0},{200,8},{208,16},{216,24},{224,32},{232,40},{240,48},{248,... | collective-permute-start | bytes 196616 | tf_op jit(solution)/shard_map/ppermute | solution.py:380
  14.3 8.2 %collective-permute-start.2 = (bf16[256,512]{1,0:T(8,128)(2,1)}, bf16[256,512]{1,0:T(8,128)(2,1)S(1)}, u32[]{:S(2)}, u32[]{:S(2)}) collective-permute-start(bf16[256,512]{1,0:T(8,128)(2,1)} %collective-permute-done), channel_id=1, source_target_pairs={{0,64},{8,72},{16,80},{24,88},{32,96},{40,104},{48,112},{56,120},{... | collective-permute-start | bytes 786440 | tf_op jit(solution)/shard_map/ppermute | solution.py:358
  16.1 6.4 %collective-permute-start.5 = (bf16[256,512]{1,0:T(8,128)(2,1)}, bf16[256,512]{1,0:T(8,128)(2,1)}, u32[]{:S(2)}, u32[]{:S(2)}) collective-permute-start(bf16[256,512]{1,0:T(8,128)(2,1)} %collective-permute-done.4), channel_id=1, source_target_pairs={{128,64},{136,72},{144,80},{152,88},{160,96},{168,104},{176,112},{... | collective-permute-start | bytes 786440 | tf_op jit(solution)/shard_map/ppermute | solution.py:359
  17.5 13.2 %collective-permute-start.7 = (bf16[512,512]{1,0:T(8,128)(2,1)S(1)}, bf16[512,512]{1,0:T(8,128)(2,1)S(1)}, u32[]{:S(2)}, u32[]{:S(2)}) collective-permute-start(bf16[512,512]{1,0:T(8,128)(2,1)S(1)} %slice_bitcast_fusion.refs_0_), channel_id=1, source_target_pairs={{0,6},{1,7},{2,0},{3,1},{4,2},{5,3},{6,4},{7,5},{8,14},{9,15},{10,... | collective-permute-start | bytes 1572872 | tf_op jit(solution)/shard_map/ppermute | solution.py:372
  21.0 12.6 %collective-permute-start.6 = (bf16[512,512]{1,0:T(8,128)(2,1)S(1)}, bf16[512,512]{1,0:T(8,128)(2,1)S(1)}, u32[]{:S(2)}, u32[]{:S(2)}) collective-permute-start(bf16[512,512]{1,0:T(8,128)(2,1)S(1)} %slice_bitcast_fusion.refs_0_), channel_id=1, source_target_pairs={{0,2},{1,3},{2,4},{3,5},{4,6},{5,7},{6,0},{7,1},{8,10},{9,11},{10,... | collective-permute-start | bytes 1572872 | tf_op jit(solution)/shard_map/ppermute | solution.py:371
  33.8 15.7 %collective-permute-start.11 = (bf16[3,512,512]{2,1,0:T(8,128)(2,1)S(1)}, bf16[3,512,512]{2,1,0:T(8,128)(2,1)S(1)}, u32[]{:S(2)}, u32[]{:S(2)}) collective-permute-start(bf16[3,512,512]{2,1,0:T(8,128)(2,1)S(1)} %hold.4.refs_10_), channel_id=1, source_target_pairs={{0,1},{1,0},{2,3},{3,2},{4,5},{5,4},{6,7},{7,6},{8,9},{9,8},{10,11... | collective-permute-start | bytes 4718600 | tf_op jit(solution)/shard_map/ppermute | solution.py:382
  33.9 14.3 %collective-permute-start.9 = (bf16[512,512]{1,0:T(8,128)(2,1)S(1)}, bf16[512,512]{1,0:T(8,128)(2,1)S(1)}, u32[]{:S(2)}, u32[]{:S(2)}) collective-permute-start(bf16[512,512]{1,0:T(8,128)(2,1)S(1)} %pad_maximum_fusion.1), channel_id=1, source_target_pairs={{0,6},{1,7},{2,0},{3,1},{4,2},{5,3},{6,4},{7,5},{8,14},{9,15},{10,... | collective-permute-start | bytes 1572872 | tf_op jit(solution)/shard_map/ppermute | solution.py:376
  35.5 14.0 %collective-permute-start.8 = (bf16[512,512]{1,0:T(8,128)(2,1)S(1)}, bf16[512,512]{1,0:T(8,128)(2,1)S(1)}, u32[]{:S(2)}, u32[]{:S(2)}) collective-permute-start(bf16[512,512]{1,0:T(8,128)(2,1)S(1)} %pad_maximum_fusion.1), channel_id=1, source_target_pairs={{0,2},{1,3},{2,4},{3,5},{4,6},{5,7},{6,0},{7,1},{8,10},{9,11},{10,... | collective-permute-start | bytes 1572872 | tf_op jit(solution)/shard_map/ppermute | solution.py:375
  36.0 2.8 %collective-permute-start.13 = (bf16[64,512]{1,0:T(8,128)(2,1)S(1)}, bf16[64,512]{1,0:T(8,128)(2,1)S(1)}, u32[]{:S(2)}, u32[]{:S(2)}) collective-permute-start(bf16[64,512]{1,0:T(8,128)(2,1)S(1)} %copy-done.62), channel_id=1, source_target_pairs={{192,128},{200,136},{208,144},{216,152},{224,160},{232,168},{240,1... | collective-permute-start | bytes 196616 | tf_op jit(solution)/shard_map/ppermute | solution.py:380
  50.9 11.5 %collective-permute-start.18 = (bf16[3,512,512]{2,1,0:T(8,128)(2,1)S(1)}, bf16[3,512,512]{2,1,0:T(8,128)(2,1)S(1)}, u32[]{:S(2)}, u32[]{:S(2)}) collective-permute-start(bf16[3,512,512]{2,1,0:T(8,128)(2,1)S(1)} %pad_maximum_fusion.refs_4_.refs_6_), channel_id=1, source_target_pairs={{0,1},{1,0},{2,3},{3,2},{4,5},{5,4},{6,7},{7,6},{8,9},{9,8},{10,11... | collective-permute-start | bytes 4718600 | tf_op jit(solution)/shard_map/ppermute | solution.py:391
  51.0 9.2 %collective-permute-start.17 = (bf16[256,512]{1,0:T(8,128)(2,1)S(1)}, bf16[256,512]{1,0:T(8,128)(2,1)S(1)}, u32[]{:S(2)}, u32[]{:S(2)}) collective-permute-start(bf16[256,512]{1,0:T(8,128)(2,1)S(1)} %slice.65), channel_id=1, source_target_pairs={{0,6},{1,7},{2,0},{3,1},{4,2},{5,3},{6,4},{7,5},{8,14},{9,15},{10,... | collective-permute-start | bytes 786440 | tf_op jit(solution)/shard_map/ppermute | solution.py:390
  54.0 8.4 %collective-permute-start.16 = (bf16[256,512]{1,0:T(8,128)(2,1)S(1)}, bf16[256,512]{1,0:T(8,128)(2,1)S(1)}, u32[]{:S(2)}, u32[]{:S(2)}) collective-permute-start(bf16[256,512]{1,0:T(8,128)(2,1)S(1)} %slice.64), channel_id=1, source_target_pairs={{0,2},{1,3},{2,4},{3,5},{4,6},{5,7},{6,0},{7,1},{8,10},{9,11},{10,... | collective-permute-start | bytes 786440 | tf_op jit(solution)/shard_map/ppermute | solution.py:389
  63.2 10.4 %collective-permute-start.19 = (bf16[512,512]{1,0:T(8,128)(2,1)}, bf16[512,512]{1,0:T(8,128)(2,1)}, u32[]{:S(2)}, u32[]{:S(2)}) collective-permute-start(bf16[512,512]{1,0:T(8,128)(2,1)} %hold.5.refs_5_.refs_7_), channel_id=1, source_target_pairs={{0,1},{1,0},{2,3},{3,2},{4,5},{5,4},{6,7},{7,6},{8,9},{9,8},{10,11... | collective-permute-start | bytes 1572872 | tf_op jit(solution)/shard_map/ppermute | solution.py:394
  67.5 5.5 %collective-permute-start.14 = (bf16[64,512]{1,0:T(8,128)(2,1)S(1)}, bf16[64,512]{1,0:T(8,128)(2,1)S(1)}, u32[]{:S(2)}, u32[]{:S(2)}) collective-permute-start(bf16[64,512]{1,0:T(8,128)(2,1)S(1)} %get-tuple-element.68), channel_id=1, source_target_pairs={{0,8},{64,72},{128,136},{192,200},{1,9},{65,73},{129,137},{193,201... | collective-permute-start | bytes 196616 | tf_op jit(solution)/shard_map/ppermute | solution.py:407
  73.0 5.5 %collective-permute-start.15 = (bf16[1,64,512]{2,1,0:T(8,128)(2,1)S(1)}, bf16[1,64,512]{2,1,0:T(8,128)(2,1)S(1)}, u32[]{:S(2)}, u32[]{:S(2)}) collective-permute-start(bf16[1,64,512]{2,1,0:T(8,128)(2,1)S(1)} %bitcast.31), channel_id=1, source_target_pairs={{8,16},{72,80},{136,144},{200,208},{40,48},{9,17},{73,81},{137,145... | collective-permute-start | bytes 196616 | tf_op jit(solution)/shard_map/ppermute | solution.py:406
  80.0 3.0 %collective-permute-start.21 = (bf16[2,64,512]{2,1,0:T(8,128)(2,1)S(1)}, bf16[2,64,512]{2,1,0:T(8,128)(2,1)S(1)}, u32[]{:S(2)}, u32[]{:S(2)}) collective-permute-start(bf16[2,64,512]{2,1,0:T(8,128)(2,1)S(1)} %pad_maximum_fusion.6), channel_id=1, source_target_pairs={{16,24},{80,88},{144,152},{208,216},{48,56},{17,25},{81,89},{145,1... | collective-permute-start | bytes 393224 | tf_op jit(solution)/shard_map/ppermute | solution.py:406
  82.3 2.5 %collective-permute-start.22 = (bf16[64,512]{1,0:T(8,128)(2,1)S(1)}, bf16[64,512]{1,0:T(8,128)(2,1)S(1)}, u32[]{:S(2)}, u32[]{:S(2)}) collective-permute-start(bf16[64,512]{1,0:T(8,128)(2,1)S(1)} %step.8), channel_id=1, source_target_pairs={{16,24},{80,88},{144,152},{208,216},{17,25},{81,89},{145,153},{209... | collective-permute-start | bytes 196616 | tf_op jit(solution)/shard_map/ppermute | solution.py:407
  85.5 11.8 %collective-permute-start.23 = (bf16[3,64,512]{2,1,0:T(8,128)(2,1)}, bf16[3,64,512]{2,1,0:T(8,128)(2,1)S(1)}, u32[]{:S(2)}, u32[]{:S(2)}) collective-permute-start(bf16[3,64,512]{2,1,0:T(8,128)(2,1)} %pad_maximum_fusion.5), channel_id=1, source_target_pairs={{24,32},{88,96},{152,160},{216,224},{56,0},{25,33},{89,97},{153,16... | collective-permute-start | bytes 589832 | tf_op jit(solution)/shard_map/ppermute | solution.py:406
  88.5 14.2 %collective-permute-start.24 = (bf16[64,512]{1,0:T(8,128)(2,1)S(1)}, bf16[64,512]{1,0:T(8,128)(2,1)S(1)}, u32[]{:S(2)}, u32[]{:S(2)}) collective-permute-start(bf16[64,512]{1,0:T(8,128)(2,1)S(1)} %step.9), channel_id=1, source_target_pairs={{24,32},{88,96},{152,160},{216,224},{25,33},{89,97},{153,161},{217... | collective-permute-start | bytes 196616 | tf_op jit(solution)/shard_map/ppermute | solution.py:407
  104.6 9.7 %collective-permute-start.26 = (bf16[64,512]{1,0:T(8,128)(2,1)S(1)}, bf16[64,512]{1,0:T(8,128)(2,1)S(1)}, u32[]{:S(2)}, u32[]{:S(2)}) collective-permute-start(bf16[64,512]{1,0:T(8,128)(2,1)S(1)} %step.10), channel_id=1, source_target_pairs={{32,40},{96,104},{160,168},{224,232},{33,41},{97,105},{161,169},{2... | collective-permute-start | bytes 196616 | tf_op jit(solution)/shard_map/ppermute | solution.py:407
  105.5 6.4 %collective-permute-start.25 = (bf16[4,64,512]{2,1,0:T(8,128)(2,1)S(1)}, bf16[4,64,512]{2,1,0:T(8,128)(2,1)S(1)}, u32[]{:S(2)}, u32[]{:S(2)}) collective-permute-start(bf16[4,64,512]{2,1,0:T(8,128)(2,1)S(1)} %pad_maximum_fusion.4), channel_id=1, source_target_pairs={{32,40},{96,104},{160,168},{224,232},{0,8},{33,41},{97,105},{161,1... | collective-permute-start | bytes 786440 | tf_op jit(solution)/shard_map/ppermute | solution.py:406
  106.9 7.5 %collective-permute-start.27 = (bf16[64,512]{1,0:T(8,128)(2,1)S(1)}, bf16[64,512]{1,0:T(8,128)(2,1)S(1)}, u32[]{:S(2)}, u32[]{:S(2)}) collective-permute-start(bf16[64,512]{1,0:T(8,128)(2,1)S(1)} %select_select_fusion.3), channel_id=1, source_target_pairs={{8,0},{16,8},{24,16},{72,64},{80,72},{88,80},{136,128},{144,136},{... | collective-permute-start | bytes 196616 | tf_op jit(solution)/shard_map/ppermute | solution.py:419
  114.4 4.3 %collective-permute-start.28 = (bf16[5,64,512]{2,1,0:T(8,128)(2,1)S(1)}, bf16[5,64,512]{2,1,0:T(8,128)(2,1)S(1)}, u32[]{:S(2)}, u32[]{:S(2)}) collective-permute-start(bf16[5,64,512]{2,1,0:T(8,128)(2,1)S(1)} %pad_maximum_fusion.3), channel_id=1, source_target_pairs={{40,48},{104,112},{168,176},{232,240},{8,16},{41,49},{105,113},{16... | collective-permute-start | bytes 983048 | tf_op jit(solution)/shard_map/ppermute | solution.py:406
  116.7 4.7 %collective-permute-start.29 = (bf16[64,512]{1,0:T(8,128)(2,1)S(1)}, bf16[64,512]{1,0:T(8,128)(2,1)S(1)}, u32[]{:S(2)}, u32[]{:S(2)}) collective-permute-start(bf16[64,512]{1,0:T(8,128)(2,1)S(1)} %step.11), channel_id=1, source_target_pairs={{40,48},{104,112},{168,176},{232,240},{41,49},{105,113},{169,177},... | collective-permute-start | bytes 196616 | tf_op jit(solution)/shard_map/ppermute | solution.py:407
  117.4 7.3 %collective-permute-start.30 = (bf16[64,512]{1,0:T(8,128)(2,1)S(1)}, bf16[64,512]{1,0:T(8,128)(2,1)S(1)}, u32[]{:S(2)}, u32[]{:S(2)}) collective-permute-start(bf16[64,512]{1,0:T(8,128)(2,1)S(1)} %collective-permute-done.27.refs_1_), channel_id=1, source_target_pairs={{8,0},{16,8},{24,16},{72,64},{80,72},{88,80},{136,128},{144,136},{... | collective-permute-start | bytes 196616 | tf_op jit(solution)/shard_map/ppermute | solution.py:419
  126.1 11.2 %collective-permute-start.31 = (bf16[6,64,512]{2,1,0:T(8,128)(2,1)}, bf16[6,64,512]{2,1,0:T(8,128)(2,1)}, u32[]{:S(2)}, u32[]{:S(2)}) collective-permute-start(bf16[6,64,512]{2,1,0:T(8,128)(2,1)} %pad_maximum_fusion.2), channel_id=1, source_target_pairs={{48,56},{112,120},{176,184},{240,248},{16,24},{49,57},{113,121},{1... | collective-permute-start | bytes 1179656 | tf_op jit(solution)/shard_map/ppermute | solution.py:406
  127.5 49.4 %collective-permute-start.47 = (bf16[256,512]{1,0:T(8,128)(2,1)}, bf16[256,512]{1,0:T(8,128)(2,1)S(1)}, u32[]{:S(2)}, u32[]{:S(2)}) collective-permute-start(bf16[256,512]{1,0:T(8,128)(2,1)} %slice.60), channel_id=1, source_target_pairs={{0,2},{1,3},{2,4},{3,5},{4,6},{5,7},{6,0},{7,1},{8,10},{9,11},{10,... | collective-permute-start | bytes 786440 | tf_op jit(solution)/shard_map/ppermute | solution.py:414
  127.8 49.1 %collective-permute-start.48 = (bf16[256,512]{1,0:T(8,128)(2,1)}, bf16[256,512]{1,0:T(8,128)(2,1)S(1)}, u32[]{:S(2)}, u32[]{:S(2)}) collective-permute-start(bf16[256,512]{1,0:T(8,128)(2,1)} %slice.61), channel_id=1, source_target_pairs={{0,6},{1,7},{2,0},{3,1},{4,2},{5,3},{6,4},{7,5},{8,14},{9,15},{10,... | collective-permute-start | bytes 786440 | tf_op jit(solution)/shard_map/ppermute | solution.py:415
  129.5 11.0 %collective-permute-start.32 = (bf16[64,512]{1,0:T(8,128)(2,1)}, bf16[64,512]{1,0:T(8,128)(2,1)S(1)}, u32[]{:S(2)}, u32[]{:S(2)}) collective-permute-start(bf16[64,512]{1,0:T(8,128)(2,1)} %copy-done.56), channel_id=1, source_target_pairs={{8,0},{16,8},{24,16},{72,64},{80,72},{88,80},{136,128},{144,136},{... | collective-permute-start | bytes 196616 | tf_op jit(solution)/shard_map/ppermute | solution.py:419
  136.5 4.0 %collective-permute-start.33 = (bf16[64,512]{1,0:T(8,128)(2,1)S(1)}, bf16[64,512]{1,0:T(8,128)(2,1)S(1)}, u32[]{:S(2)}, u32[]{:S(2)}) collective-permute-start(bf16[64,512]{1,0:T(8,128)(2,1)S(1)} %step.12), channel_id=1, source_target_pairs={{48,56},{112,120},{176,184},{240,248},{49,57},{113,121},{177,185},... | collective-permute-start | bytes 196616 | tf_op jit(solution)/shard_map/ppermute | solution.py:407
  144.3 2.8 %collective-permute-start.39 = (bf16[64,512]{1,0:T(8,128)(2,1)S(1)}, bf16[64,512]{1,0:T(8,128)(2,1)S(1)}, u32[]{:S(2)}, u32[]{:S(2)}) collective-permute-start(bf16[64,512]{1,0:T(8,128)(2,1)S(1)} %broadcast_select_fusion.refs_7_), channel_id=1, source_target_pairs={{32,16},{40,24},{48,32},{56,40},{96,80},{104,88},{112,96},{120,104... | collective-permute-start | bytes 196616 | tf_op jit(solution)/shard_map/ppermute | solution.py:435
  145.1 3.3 %collective-permute-start.38 = (bf16[64,512]{1,0:T(8,128)(2,1)S(1)}, bf16[64,512]{1,0:T(8,128)(2,1)S(1)}, u32[]{:S(2)}, u32[]{:S(2)}) collective-permute-start(bf16[64,512]{1,0:T(8,128)(2,1)S(1)} %broadcast_select_fusion.refs_7_), channel_id=1, source_target_pairs={{32,8},{40,16},{48,24},{56,32},{96,72},{104,80},{112,88},{120,96},... | collective-permute-start | bytes 196616 | tf_op jit(solution)/shard_map/ppermute | solution.py:435
  145.8 20.0 %collective-permute-start.37 = (bf16[64,512]{1,0:T(8,128)(2,1)S(1)}, bf16[64,512]{1,0:T(8,128)(2,1)S(1)}, u32[]{:S(2)}, u32[]{:S(2)}) collective-permute-start(bf16[64,512]{1,0:T(8,128)(2,1)S(1)} %broadcast_select_fusion.refs_7_), channel_id=1, source_target_pairs={{56,0},{120,64},{184,128},{248,192},{57,1},{121,65},{185,129},{249... | collective-permute-start | bytes 196616 | tf_op jit(solution)/shard_map/ppermute | solution.py:435
  147.1 19.9 %collective-permute-start.36 = (bf16[64,512]{1,0:T(8,128)(2,1)S(1)}, bf16[64,512]{1,0:T(8,128)(2,1)S(1)}, u32[]{:S(2)}, u32[]{:S(2)}) collective-permute-start(bf16[64,512]{1,0:T(8,128)(2,1)S(1)} %broadcast_select_fusion.refs_7_), channel_id=1, source_target_pairs={{48,0},{56,8},{112,64},{120,72},{176,128},{184,136},{240,192},{248... | collective-permute-start | bytes 196616 | tf_op jit(solution)/shard_map/ppermute | solution.py:435
  148.4 18.7 %collective-permute-start.35 = (bf16[64,512]{1,0:T(8,128)(2,1)S(1)}, bf16[64,512]{1,0:T(8,128)(2,1)S(1)}, u32[]{:S(2)}, u32[]{:S(2)}) collective-permute-start(bf16[64,512]{1,0:T(8,128)(2,1)S(1)} %broadcast_select_fusion.refs_7_), channel_id=1, source_target_pairs={{40,0},{48,8},{56,16},{104,64},{112,72},{120,80},{168,128},{176,13... | collective-permute-start | bytes 196616 | tf_op jit(solution)/shard_map/ppermute | solution.py:435
  165.7 10.1 %collective-permute-start.34 = (bf16[64,512]{1,0:T(8,128)(2,1)S(1)}, bf16[64,512]{1,0:T(8,128)(2,1)S(1)}, u32[]{:S(2)}, u32[]{:S(2)}) collective-permute-start(bf16[64,512]{1,0:T(8,128)(2,1)S(1)} %broadcast_select_fusion.refs_7_), channel_id=1, source_target_pairs={{32,0},{40,8},{48,16},{56,24},{96,64},{104,72},{112,80},{120,88},{... | collective-permute-start | bytes 196616 | tf_op jit(solution)/shard_map/ppermute | solution.py:435
  167.0 10.0 %collective-permute-start.42 = (bf16[4,64,512]{2,1,0:T(8,128)(2,1)S(1)}, bf16[4,64,512]{2,1,0:T(8,128)(2,1)S(1)}, u32[]{:S(2)}, u32[]{:S(2)}) collective-permute-start(bf16[4,64,512]{2,1,0:T(8,128)(2,1)S(1)} %collect.2.refs_1_), channel_id=1, source_target_pairs={{0,192},{8,200},{16,208},{24,216},{32,224},{40,232},{48,240},{56,2... | collective-permute-start | bytes 786440 | tf_op jit(solution)/shard_map/ppermute | solution.py:427
  167.1 9.9 %collective-permute-start.41 = (bf16[4,64,512]{2,1,0:T(8,128)(2,1)S(1)}, bf16[4,64,512]{2,1,0:T(8,128)(2,1)S(1)}, u32[]{:S(2)}, u32[]{:S(2)}) collective-permute-start(bf16[4,64,512]{2,1,0:T(8,128)(2,1)S(1)} %collect.2.refs_1_), channel_id=1, source_target_pairs={{0,64},{8,72},{16,80},{24,88},{32,96},{40,104},{48,112},{56,120},{... | collective-permute-start | bytes 786440 | tf_op jit(solution)/shard_map/ppermute | solution.py:426
  177.0 19.3 %collective-permute-start.49 = (bf16[512,512]{1,0:T(8,128)(2,1)S(1)}, bf16[512,512]{1,0:T(8,128)(2,1)S(1)}, u32[]{:S(2)}, u32[]{:S(2)}) collective-permute-start(bf16[512,512]{1,0:T(8,128)(2,1)S(1)} %hold.7.refs_11_), channel_id=1, source_target_pairs={{0,1},{1,0},{2,3},{3,2},{4,5},{5,4},{6,7},{7,6},{8,9},{9,8},{10,11... | collective-permute-start | bytes 1572872 | tf_op jit(solution)/shard_map/ppermute | solution.py:438
  177.1 15.5 %collective-permute-start.44 = (bf16[4,64,512]{2,1,0:T(8,128)(2,1)S(1)}, bf16[4,64,512]{2,1,0:T(8,128)(2,1)S(1)}, u32[]{:S(2)}, u32[]{:S(2)}) collective-permute-start(bf16[4,64,512]{2,1,0:T(8,128)(2,1)S(1)} %collect.3.refs_1_), channel_id=1, source_target_pairs={{0,64},{8,72},{16,80},{24,88},{32,96},{40,104},{48,112},{56,120},{... | collective-permute-start | bytes 786440 | tf_op jit(solution)/shard_map/ppermute | solution.py:242
  177.2 15.5 %collective-permute-start.43 = (bf16[4,64,512]{2,1,0:T(8,128)(2,1)S(1)}, bf16[4,64,512]{2,1,0:T(8,128)(2,1)S(1)}, u32[]{:S(2)}, u32[]{:S(2)}) collective-permute-start(bf16[4,64,512]{2,1,0:T(8,128)(2,1)S(1)} %collect.3.refs_1_), channel_id=1, source_target_pairs={{0,192},{8,200},{16,208},{24,216},{32,224},{40,232},{48,240},{56,2... | collective-permute-start | bytes 786440 | tf_op jit(solution)/shard_map/ppermute | solution.py:243
  180.4 15.9 %collective-permute-start.50 = (bf16[4,64,512]{2,1,0:T(8,128)(2,1)S(1)}, bf16[4,64,512]{2,1,0:T(8,128)(2,1)S(1)}, u32[]{:S(2)}, u32[]{:S(2)}) collective-permute-start(bf16[4,64,512]{2,1,0:T(8,128)(2,1)S(1)} %collect.2.refs_1_), channel_id=1, source_target_pairs={{0,128},{8,136},{16,144},{24,152},{32,160},{40,168},{48,176},{56,1... | collective-permute-start | bytes 786440 | tf_op jit(solution)/shard_map/ppermute | solution.py:428
  192.6 8.6 %collective-permute-start.45 = (bf16[2,64,512]{2,1,0:T(8,128)(2,1)S(1)}, bf16[2,64,512]{2,1,0:T(8,128)(2,1)S(1)}, u32[]{:S(2)}, u32[]{:S(2)}) collective-permute-start(bf16[2,64,512]{2,1,0:T(8,128)(2,1)S(1)} %slice.73), channel_id=1, source_target_pairs={{0,64},{8,72},{16,80},{24,88},{32,96},{40,104},{48,112},{56,120},{... | collective-permute-start | bytes 393224 | tf_op jit(solution)/shard_map/ppermute | solution.py:244
  192.7 8.5 %collective-permute-start.46 = (bf16[2,64,512]{2,1,0:T(8,128)(2,1)S(1)}, bf16[2,64,512]{2,1,0:T(8,128)(2,1)S(1)}, u32[]{:S(2)}, u32[]{:S(2)}) collective-permute-start(bf16[2,64,512]{2,1,0:T(8,128)(2,1)S(1)} %slice.74), channel_id=1, source_target_pairs={{0,192},{8,200},{16,208},{24,216},{32,224},{40,232},{48,240},{56,2... | collective-permute-start | bytes 393224 | tf_op jit(solution)/shard_map/ppermute | solution.py:245
  (69 other events, 514.0 us)

commit v2 on v1

--- a/solution.py
+++ b/solution.py
@@ -51,6 +51,7 @@
 VMEM = pl.BlockSpec(memory_space=pltpu.VMEM)
 SMEM = pl.BlockSpec(memory_space=pltpu.SMEM)
 ANY = pl.BlockSpec(memory_space=pl.ANY)
+HBM = pl.BlockSpec(memory_space=pltpu.HBM)
 LIMIT = 8 * 1024 * 1024
 PLACE, KIND, ROWS, AT_Z, PLANE = 0, 8, 16, 17, 18
 
@@ -95,7 +96,7 @@
             jax.ShapeDtypeStruct((c, b), F32),
             jax.ShapeDtypeStruct((b, b), BF),
         ),
-        in_specs=[SMEM, VMEM, VMEM, ANY] + [VMEM] * len(blocks),
+        in_specs=[SMEM, VMEM, VMEM, HBM] + [VMEM] * len(blocks),
         out_specs=(VMEM, VMEM),
         scratch_shapes=[pltpu.SemaphoreType.DMA],
         compiler_params=params(),
@@ -154,7 +155,7 @@
             jax.ShapeDtypeStruct(base.shape, BF),
             jax.ShapeDtypeStruct(square, BF),
         ),
-        in_specs=[VMEM, ANY],
+        in_specs=[VMEM, HBM],
         out_specs=(VMEM, VMEM),
         scratch_shapes=[pltpu.VMEM(square, BF), pltpu.SemaphoreType.DMA((2,))],
         compiler_params=params(),
@@ -185,6 +186,45 @@
         ),
         name="hold",
     )(*parts)
+
+
+def append(known, last):
+    n, c, b = known.shape
+
+    def kernel(known, last, out):
+        out[:n] = known[...]
+        out[n] = last[...]
+
+    return pl.pallas_call(
+        kernel,
+        out_shape=jax.ShapeDtypeStruct((n + 1, c, b), BF),
+        in_specs=[VMEM, VMEM],
+        out_specs=VMEM,
+        compiler_params=params(),
+        cost_estimate=pl.CostEstimate(
+            flops=0, bytes_accessed=4 * (n + 1) * c * b, transcendentals=0
+        ),
+        name="append",
+    )(known, last)
+
+
+def own_row(sc, solved):
+    def kernel(sc, *refs):
+        *ins, out = refs
+        for z, ref in enumerate(ins):
+
+            @pl.when((sc[AT_Z] == z) if z + 1 < len(ins) else (sc[AT_Z] >= z))
+            def _():
+                out[...] = ref[...]
+
+    return pl.pallas_call(
+        kernel,
+        out_shape=jax.ShapeDtypeStruct(solved[0].shape, BF),
+        in_specs=[SMEM] + [VMEM] * len(solved),
+        out_specs=VMEM,
+        compiler_params=params(),
+        name="own_row",
+    )(sc, *solved)
 
 
 def collect(sc, rows, own, before, after_own):
@@ -395,7 +435,7 @@
     blocks0 = [near, far, near_other, far_other]
 
     fresh, inv = first(base, inverse)
-    own_s = fresh
+    solved = [fresh]
     acc = base.astype(F32)
     known = None
     before = {0: []}
@@ -414,6 +454,8 @@
                 lax.ppermute(left1, "col", shift_x(1)),
                 lax.ppermute(right1, "col", shift_x(-1)),
             ]
+        if t == 4:
+            own_s = own_row(sc, solved)
         if 4 <= t <= 6:
             back_a.append(
                 lax.ppermute((back_a or [own_s])[-1], "row", back_z(1, range(1, 4)))
@@ -428,10 +470,11 @@
             far_a = lax.ppermute(rows_a, "row", shift_y(2))
             pieces_a = (rows_a, behind_a, far_a, far_a, before_a)
         fresh = step(t, sc, acc, last, inv, blocks0)
-        own_s = jnp.where(z == t, fresh, own_s)
+        solved.append(fresh)
         before[t] = [last] if t == 1 else [sent, last]
-        known = last[None] if t == 1 else jnp.concatenate([sent, last[None]])
-
+        known = last[None] if t == 1 else append(sent, last)
+
+    own_s = own_row(sc, solved)
     back = [lax.ppermute(own_s, "row", back_z(d, range(4, 8))) for d in range(1, 8)]
     rows_b = collect(sc, range(4, 8), own_s, before, back)
     far1 = hold([after(far1[0], rows_b), far1[1]])

time: 210 us -> 196 us (0.933)
  the two profiles are of different devices: /device:TPU:2 before, /device:TPU:1 now
where the time goes in v2:
time: 196 us; the launch traced here: 195 us
  waiting for transfers between devices  70.7 us (36%)
  starting transfers between devices  70.3 us (36%)
  Pallas kernels  40 us (20%)
  local copies, waits for them, and re-layouts  9.91 us (5%)
  other arithmetic  2.32 us (1%)
    ppermute x7, waiting for transfers between devices, on_device(): lax.ppermute(own_s, 'row', back_z(d, range(4, 8)))  18.7 us
    pallas_call x6, Pallas kernels, early(): pl.pallas_call(lambda *refs: early_kernel(t, *refs), out_shape=(jax.Shape...  13.1 us
    ppermute x1, waiting for transfers between devices, spread_y(): before = lax.ppermute(rows, 'row', shift_y(1))  11.9 us
    pallas_call x7, Pallas kernels, step(): pl.pallas_call(lambda *refs: step_kernel(t, *refs), out_shape=jax.ShapeDt...  11.8 us
    pallas_call x2, Pallas kernels, final(): pl.pallas_call(lambda *refs: final_kernel(start, *refs), out_shape=(jax.S...  10.2 us
    ppermute x1, waiting for transfers between devices, on_device(): right = lax.ppermute(window, 'col', shift_x(-1))  9.14 us
    ppermute x1, starting transfers between devices, on_device(): far_other1 = lax.ppermute(far1, 'col', SWAP)  8.72 us
    ppermute x6, waiting for transfers between devices, on_device(): sent = lax.ppermute(known, 'row', hop_z_early(t))  7.53 us
  transfers between devices with their start and end apart: 51, of which 14 were waited for; matrix products, arithmetic and copies ran while one was open for 3% of the time, Pallas kernels for 17%

profile of v2, /device:TPU:1, one launch (start us, length us, event | category | flops | bytes accessed | tf_op | source)
XLA Modules:
  0.0 194.7 jit_solution(6909095098793275844)
XLA Ops:
  1.8 1.3 collective-permute-start
  3.1 1.4 collective-permute-start.4
  4.5 3.4 %collective-permute-start.1 = (bf16[256,512]{1,0:T(8,128)(2,1)S(1)}, bf16[256,512]{1,0:T(8,128)(2,1)S(1)}, u32[]{:S(2)}, u32[]{:S(2)}) collective-permute-start(bf16[256,512]{1,0:T(8,128)(2,1)S(1)} %get-tuple-element.118), channel_id=1, source_target_pairs={{192,128},{200,136},{208,144},{216,152},{224,160},{232,168},{240,1... | collective-permute-start | bytes 786440 | tf_op jit(solution)/shard_map/ppermute | solution.py:397
  7.9 1.3 collective-permute-start.3
  12.4 3.9 %collective-permute-start.2 = (bf16[256,512]{1,0:T(8,128)(2,1)S(1)}, bf16[256,512]{1,0:T(8,128)(2,1)}, u32[]{:S(2)}, u32[]{:S(2)}) collective-permute-start(bf16[256,512]{1,0:T(8,128)(2,1)S(1)} %collective-permute-done), channel_id=1, source_target_pairs={{0,64},{8,72},{16,80},{24,88},{32,96},{40,104},{48,112},{56,120},{... | collective-permute-start | bytes 786440 | tf_op jit(solution)/shard_map/ppermute | solution.py:398
  16.3 1.4 collective-permute-start.5
  17.8 2.6 %collective-permute-start.7 = (bf16[512,512]{1,0:T(8,128)(2,1)S(1)}, bf16[512,512]{1,0:T(8,128)(2,1)S(1)}, u32[]{:S(2)}, u32[]{:S(2)}) collective-permute-start(bf16[512,512]{1,0:T(8,128)(2,1)S(1)} %slice_bitcast_fusion.refs_0_), channel_id=1, source_target_pairs={{0,6},{1,7},{2,0},{3,1},{4,2},{5,3},{6,4},{7,5},{8,14},{9,15},{10,... | collective-permute-start | bytes 1572872 | tf_op jit(solution)/shard_map/ppermute | solution.py:412
  22.7 7.2 %collective-permute-done.7.refs_2_ = bf16[512,512]{1,0:T(8,128)(2,1)S(1)} collective-permute-done((bf16[512,512]{1,0:T(8,128)(2,1)S(1)}, bf16[512,512]{1,0:T(8,128)(2,1)S(1)}, u32[]{:S(2)}, u32[]{:S(2)}) %collective-permute-start.7) | collective-permute-done | bytes 524320 | tf_op jit(solution)/shard_map/ppermute | solution.py:412
  29.9 3.1 %collective-permute-done.6.refs_1_ = bf16[512,512]{1,0:T(8,128)(2,1)S(1)} collective-permute-done((bf16[512,512]{1,0:T(8,128)(2,1)S(1)}, bf16[512,512]{1,0:T(8,128)(2,1)S(1)}, u32[]{:S(2)}, u32[]{:S(2)}) %collective-permute-start.6) | collective-permute-done | bytes 524320 | tf_op jit(solution)/shard_map/ppermute | solution.py:411
  33.1 3.0 %collective-permute-start.11 = (bf16[3,512,512]{2,1,0:T(8,128)(2,1)S(1)}, bf16[3,512,512]{2,1,0:T(8,128)(2,1)S(1)}, u32[]{:S(2)}, u32[]{:S(2)}) collective-permute-start(bf16[3,512,512]{2,1,0:T(8,128)(2,1)S(1)} %hold.4.refs_10_), channel_id=1, source_target_pairs={{0,1},{1,0},{2,3},{3,2},{4,5},{5,4},{6,7},{7,6},{8,9},{9,8},{10,11... | collective-permute-start | bytes 4718600 | tf_op jit(solution)/shard_map/ppermute | solution.py:422
  40.3 9.1 %collective-permute-done.9 = bf16[512,512]{1,0:T(8,128)(2,1)S(1)} collective-permute-done((bf16[512,512]{1,0:T(8,128)(2,1)S(1)}, bf16[512,512]{1,0:T(8,128)(2,1)S(1)}, u32[]{:S(2)}, u32[]{:S(2)}) %collective-permute-start.9) | collective-permute-done | bytes 524320 | tf_op jit(solution)/shard_map/ppermute | solution.py:416
  49.5 2.1 %collective-permute-done.8 = bf16[512,512]{1,0:T(8,128)(2,1)S(1)} collective-permute-done((bf16[512,512]{1,0:T(8,128)(2,1)S(1)}, bf16[512,512]{1,0:T(8,128)(2,1)S(1)}, u32[]{:S(2)}, u32[]{:S(2)}) %collective-permute-start.8) | collective-permute-done | bytes 524320 | tf_op jit(solution)/shard_map/ppermute | solution.py:415
  53.0 1.3 collective-permute-start.17
  54.3 1.5 collective-permute-start.15
  55.8 6.3 %collective-permute-done.16.refs_1_ = bf16[256,512]{1,0:T(8,128)(2,1)S(1)} collective-permute-done((bf16[256,512]{1,0:T(8,128)(2,1)S(1)}, bf16[256,512]{1,0:T(8,128)(2,1)S(1)}, u32[]{:S(2)}, u32[]{:S(2)}) %collective-permute-start.16) | collective-permute-done | bytes 262176 | tf_op jit(solution)/shard_map/ppermute | solution.py:430
  66.0 2.2 %copy-done = bf16[8,512,512]{2,1,0:T(8,128)(2,1)S(1)} copy-done((bf16[8,512,512]{2,1,0:T(8,128)(2,1)S(1)}, bf16[8,512,512]{2,1,0:T(8,128)(2,1)}, u32[]{:S(2)}) %copy-start) | copy-done | bytes 4194328
  69.3 3.5 %collective-permute-start.14 = (bf16[64,512]{1,0:T(8,128)(2,1)S(1)}, bf16[64,512]{1,0:T(8,128)(2,1)S(1)}, u32[]{:S(2)}, u32[]{:S(2)}) collective-permute-start(bf16[64,512]{1,0:T(8,128)(2,1)S(1)} %get-tuple-element.68.refs_0_), channel_id=1, source_target_pairs={{0,8},{64,72},{128,136},{192,200},{1,9},{65,73},{129,137},{193,201... | collective-permute-start | bytes 196616 | tf_op jit(solution)/shard_map/ppermute | solution.py:447
  73.0 1.3 collective-permute-done.14.refs_2_.refs_4_
  77.1 1.8 step.7.refs_1_
  79.6 1.4 early.6
  81.7 1.6 step.8.refs_2_
  84.0 1.7 early.7
  85.8 1.3 collective-permute-start.23
  87.1 1.6 step.9.refs_3_
  89.4 7.4 %collective-permute-done.23.refs_2_.known.refs_9_ = bf16[3,64,512]{2,1,0:T(8,128)(2,1)S(1)} collective-permute-done((bf16[3,64,512]{2,1,0:T(8,128)(2,1)S(1)}, bf16[3,64,512]{2,1,0:T(8,128)(2,1)S(1)}, u32[]{:S(2)}, u32[]{:S(2)}) %collective-permute-start.23) | collective-permute-done | bytes 196640 | tf_op jit(solution)/shard_map/ppermute | solution.py:446
  96.8 2.0 %early.8 = (f32[64,512]{1,0:T(8,128)S(1)}, bf16[512,512]{1,0:T(8,128)(2,1)S(1)}) custom-call(s32[22]{0:T(128)S(1)} %concatenate.6.refs_0_.sc, bf16[64,512]{1,0:T(8,128)(2,1)S(1)} %get-tuple-element.115.base.refs_1_, bf16[3,64,512]{2,1,0:T(8,128)(2,1)S(1)} %collective-permute-done.23.refs_2_.known.refs_9_, bf16[8,512,512]{2,1,0:T(8,128)(2,1)S(1)} %copy-done.1, ...), custom_call_target="tpu_custom_call" | custom-call | flops 100663296 | bytes 786432 | tf_op jit(solution)/shard_map/early/pallas_call | solution.py:93
  98.9 1.3 collective-permute-start.25
  100.2 1.6 step.10.refs_4_
  103.1 1.5 collective-permute-start.27
  104.7 2.3 %early.9 = (f32[64,512]{1,0:T(8,128)S(1)}, bf16[512,512]{1,0:T(8,128)(2,1)S(1)}) custom-call(s32[22]{0:T(128)S(1)} %concatenate.6.refs_0_.sc, bf16[64,512]{1,0:T(8,128)(2,1)S(1)} %get-tuple-element.115.base.refs_1_, bf16[4,64,512]{2,1,0:T(8,128)(2,1)S(1)} %collective-permute-done.25.refs_2_.known.refs_11_, bf16[8,512,512]{2,1,0:T(8,128)(2,1)S(1)} %copy-done.1, ...), custom_call_target="tpu_custom_call" | custom-call | flops 134217728 | bytes 1048576 | tf_op jit(solution)/shard_map/early/pallas_call | solution.py:93
  108.8 1.6 step.11.refs_5_
  111.1 1.3 collective-permute-start.30
  112.4 2.6 %early.10 = (f32[64,512]{1,0:T(8,128)S(1)}, bf16[512,512]{1,0:T(8,128)(2,1)S(1)}) custom-call(s32[22]{0:T(128)S(1)} %concatenate.6.refs_0_.sc, bf16[64,512]{1,0:T(8,128)(2,1)S(1)} %get-tuple-element.115.base.refs_1_, bf16[5,64,512]{2,1,0:T(8,128)(2,1)S(1)} %collective-permute-done.28.refs_2_.known.refs_12_.refs_9_, bf16[8,512,512]{2,1,0:T(8,128)(2,1)S(1)} %copy-done.1, ...), custom_call_target="tpu_custom_call" | custom-call | flops 167772160 | bytes 1310720 | tf_op jit(solution)/shard_map/early/pallas_call | solution.py:93
  115.1 1.3 collective-permute-done.30.refs_2_
  117.2 1.7 step.12.refs_6_
  121.2 2.4 %collective-permute-start.48 = (bf16[256,512]{1,0:T(8,128)(2,1)S(1)}, bf16[256,512]{1,0:T(8,128)(2,1)S(1)}, u32[]{:S(2)}, u32[]{:S(2)}) collective-permute-start(bf16[256,512]{1,0:T(8,128)(2,1)S(1)} %copy-done.11), channel_id=1, source_target_pairs={{0,6},{1,7},{2,0},{3,1},{4,2},{5,3},{6,4},{7,5},{8,14},{9,15},{10,... | collective-permute-start | bytes 786440 | tf_op jit(solution)/shard_map/ppermute | solution.py:455
  123.6 2.9 %early.11 = (f32[64,512]{1,0:T(8,128)S(1)}, bf16[512,512]{1,0:T(8,128)(2,1)S(1)}) custom-call(s32[22]{0:T(128)S(1)} %concatenate.6.refs_0_.sc, bf16[64,512]{1,0:T(8,128)(2,1)S(1)} %get-tuple-element.115.base.refs_1_, bf16[6,64,512]{2,1,0:T(8,128)(2,1)S(1)} %collective-permute-done.31.refs_2_.refs_13_.refs_11_, bf16[8,512,512]{2,1,0:T(8,128)(2,1)S(1)} %copy-done.1, ...), custom_call_target="tpu_custom_call" | custom-call | flops 201326592 | bytes 1572864 | tf_op jit(solution)/shard_map/early/pallas_call | solution.py:93
  127.2 1.7 step.13.refs_7_
  134.5 1.3 collective-permute-start.35
  135.8 12.6 %collective-permute-done.37.refs_3_ = bf16[64,512]{1,0:T(8,128)(2,1)S(1)} collective-permute-done((bf16[64,512]{1,0:T(8,128)(2,1)S(1)}, bf16[64,512]{1,0:T(8,128)(2,1)S(1)}, u32[]{:S(2)}, u32[]{:S(2)}) %collective-permute-start.37) | collective-permute-done | bytes 65568 | tf_op jit(solution)/shard_map/ppermute | solution.py:478
  149.8 1.4 collective-permute-start.41
  151.3 6.1 %collective-permute-done.34.refs_0_ = bf16[64,512]{1,0:T(8,128)(2,1)S(1)} collective-permute-done((bf16[64,512]{1,0:T(8,128)(2,1)S(1)}, bf16[64,512]{1,0:T(8,128)(2,1)S(1)}, u32[]{:S(2)}, u32[]{:S(2)}) %collective-permute-start.34) | collective-permute-done | bytes 65568 | tf_op jit(solution)/shard_map/ppermute | solution.py:478
  158.0 8.7 %collective-permute-start.49 = (bf16[512,512]{1,0:T(8,128)(2,1)S(1)}, bf16[512,512]{1,0:T(8,128)(2,1)S(1)}, u32[]{:S(2)}, u32[]{:S(2)}) collective-permute-start(bf16[512,512]{1,0:T(8,128)(2,1)S(1)} %hold.7.refs_11_), channel_id=1, source_target_pairs={{0,1},{1,0},{2,3},{3,2},{4,5},{5,4},{6,7},{7,6},{8,9},{9,8},{10,11... | collective-permute-start | bytes 1572872 | tf_op jit(solution)/shard_map/ppermute | solution.py:481
  166.8 2.7 %collective-permute-start.43 = (bf16[4,64,512]{2,1,0:T(8,128)(2,1)S(1)}, bf16[4,64,512]{2,1,0:T(8,128)(2,1)S(1)}, u32[]{:S(2)}, u32[]{:S(2)}) collective-permute-start(bf16[4,64,512]{2,1,0:T(8,128)(2,1)S(1)} %collect.3.refs_1_), channel_id=1, source_target_pairs={{0,192},{8,200},{16,208},{24,216},{32,224},{40,232},{48,240},{56,2... | collective-permute-start | bytes 786440 | tf_op jit(solution)/shard_map/ppermute | solution.py:283
  169.4 11.9 %collective-permute-done.44.refs_5_ = bf16[4,64,512]{2,1,0:T(8,128)(2,1)S(1)} collective-permute-done((bf16[4,64,512]{2,1,0:T(8,128)(2,1)S(1)}, bf16[4,64,512]{2,1,0:T(8,128)(2,1)S(1)}, u32[]{:S(2)}, u32[]{:S(2)}) %collective-permute-start.44) | collective-permute-done | bytes 262176 | tf_op jit(solution)/shard_map/ppermute | solution.py:282
  181.5 2.9 %collective-permute-start.46 = (bf16[2,64,512]{2,1,0:T(8,128)(2,1)S(1)}, bf16[2,64,512]{2,1,0:T(8,128)(2,1)S(1)}, u32[]{:S(2)}, u32[]{:S(2)}) collective-permute-start(bf16[2,64,512]{2,1,0:T(8,128)(2,1)S(1)} %slice.74), channel_id=1, source_target_pairs={{0,192},{8,200},{16,208},{24,216},{32,224},{40,232},{48,240},{56,2... | collective-permute-start | bytes 393224 | tf_op jit(solution)/shard_map/ppermute | solution.py:285
  184.5 4.9 %final.2 = (f32[8,512,256]{2,1,0:T(8,128)}, f32[2,1,512,256]{3,2,1,0:T(8,128)S(1)}) custom-call(s32[22]{0:T(128)S(1)} %concatenate.6.refs_0_.sc, bf16[4,64,512]{2,1,0:T(8,128)(2,1)S(1)} %collect.2.refs_1_, bf16[4,64,512]{2,1,0:T(8,128)(2,1)S(1)} %collective-permute-done.42.refs_2_, bf16[4,64,512]{2,1,0:T(8,128)(2,1)S(1)} %collective-permute-done.50.refs_3_.refs_4_, ...), custom_call_target="tpu_custom_call" | custom-call | flops 1610612736 | bytes 2097152 | tf_op jit(solution)/shard_map/final/pallas_call | solution.py:348
  189.4 5.3 %final.3 = (f32[8,512,256]{2,1,0:T(8,128)}, f32[2,1,512,256]{3,2,1,0:T(8,128)}) custom-call(s32[22]{0:T(128)S(1)} %concatenate.6.refs_0_.sc, bf16[4,64,512]{2,1,0:T(8,128)(2,1)S(1)} %collect.3.refs_1_, bf16[4,64,512]{2,1,0:T(8,128)(2,1)S(1)} %collective-permute-done.43.refs_2_, ...), custom_call_target="tpu_custom_call", output_to_operand_aliasing={{0}: (15, {})} | custom-call | flops 1610612736 | bytes 2097152 | tf_op jit(solution)/shard_map/final/pallas_call | solution.py:348
  (129 shorter events, 38.2 us)
Async XLA Ops:
  1.8 9.3 %collective-permute-start = (bf16[256,512]{1,0:T(8,128)(2,1)S(1)}, bf16[256,512]{1,0:T(8,128)(2,1)S(1)}, u32[]{:S(2)}, u32[]{:S(2)}) collective-permute-start(bf16[256,512]{1,0:T(8,128)(2,1)S(1)} %get-tuple-element.118), channel_id=1, source_target_pairs={{192,0},{200,8},{208,16},{216,24},{224,32},{232,40},{240,48},{248,... | collective-permute-start | bytes 786440 | tf_op jit(solution)/shard_map/ppermute | solution.py:394
  3.1 13.2 %collective-permute-start.4 = (bf16[256,512]{1,0:T(8,128)(2,1)S(1)}, bf16[256,512]{1,0:T(8,128)(2,1)}, u32[]{:S(2)}, u32[]{:S(2)}) collective-permute-start(bf16[256,512]{1,0:T(8,128)(2,1)S(1)} %get-tuple-element.119), channel_id=1, source_target_pairs={{192,128},{200,136},{208,144},{216,152},{224,160},{232,168},{240,1... | collective-permute-start | bytes 786440 | tf_op jit(solution)/shard_map/ppermute | solution.py:395
  4.5 13.3 %collective-permute-start.1 = (bf16[256,512]{1,0:T(8,128)(2,1)S(1)}, bf16[256,512]{1,0:T(8,128)(2,1)S(1)}, u32[]{:S(2)}, u32[]{:S(2)}) collective-permute-start(bf16[256,512]{1,0:T(8,128)(2,1)S(1)} %get-tuple-element.118), channel_id=1, source_target_pairs={{192,128},{200,136},{208,144},{216,152},{224,160},{232,168},{240,1... | collective-permute-start | bytes 786440 | tf_op jit(solution)/shard_map/ppermute | solution.py:397
  7.9 13.6 %collective-permute-start.3 = (bf16[256,512]{1,0:T(8,128)(2,1)S(1)}, bf16[256,512]{1,0:T(8,128)(2,1)}, u32[]{:S(2)}, u32[]{:S(2)}) collective-permute-start(bf16[256,512]{1,0:T(8,128)(2,1)S(1)} %get-tuple-element.119), channel_id=1, source_target_pairs={{192,0},{200,8},{208,16},{216,24},{224,32},{232,40},{240,48},{248,... | collective-permute-start | bytes 786440 | tf_op jit(solution)/shard_map/ppermute | solution.py:396
  11.1 9.2 %collective-permute-start.10 = (bf16[64,512]{1,0:T(8,128)(2,1)S(1)}, bf16[64,512]{1,0:T(8,128)(2,1)S(1)}, u32[]{:S(2)}, u32[]{:S(2)}) collective-permute-start(bf16[64,512]{1,0:T(8,128)(2,1)S(1)} %get-tuple-element.59), channel_id=1, source_target_pairs={{192,0},{200,8},{208,16},{216,24},{224,32},{232,40},{240,48},{248,... | collective-permute-start | bytes 196616 | tf_op jit(solution)/shard_map/ppermute | solution.py:420
  12.4 9.0 %collective-permute-start.2 = (bf16[256,512]{1,0:T(8,128)(2,1)S(1)}, bf16[256,512]{1,0:T(8,128)(2,1)}, u32[]{:S(2)}, u32[]{:S(2)}) collective-permute-start(bf16[256,512]{1,0:T(8,128)(2,1)S(1)} %collective-permute-done), channel_id=1, source_target_pairs={{0,64},{8,72},{16,80},{24,88},{32,96},{40,104},{48,112},{56,120},{... | collective-permute-start | bytes 786440 | tf_op jit(solution)/shard_map/ppermute | solution.py:398
  16.3 5.1 %collective-permute-start.5 = (bf16[256,512]{1,0:T(8,128)(2,1)}, bf16[256,512]{1,0:T(8,128)(2,1)}, u32[]{:S(2)}, u32[]{:S(2)}) collective-permute-start(bf16[256,512]{1,0:T(8,128)(2,1)} %collective-permute-done.4), channel_id=1, source_target_pairs={{128,64},{136,72},{144,80},{152,88},{160,96},{168,104},{176,112},{... | collective-permute-start | bytes 786440 | tf_op jit(solution)/shard_map/ppermute | solution.py:399
  17.8 12.1 %collective-permute-start.7 = (bf16[512,512]{1,0:T(8,128)(2,1)S(1)}, bf16[512,512]{1,0:T(8,128)(2,1)S(1)}, u32[]{:S(2)}, u32[]{:S(2)}) collective-permute-start(bf16[512,512]{1,0:T(8,128)(2,1)S(1)} %slice_bitcast_fusion.refs_0_), channel_id=1, source_target_pairs={{0,6},{1,7},{2,0},{3,1},{4,2},{5,3},{6,4},{7,5},{8,14},{9,15},{10,... | collective-permute-start | bytes 1572872 | tf_op jit(solution)/shard_map/ppermute | solution.py:412
  20.3 12.7 %collective-permute-start.6 = (bf16[512,512]{1,0:T(8,128)(2,1)S(1)}, bf16[512,512]{1,0:T(8,128)(2,1)S(1)}, u32[]{:S(2)}, u32[]{:S(2)}) collective-permute-start(bf16[512,512]{1,0:T(8,128)(2,1)S(1)} %slice_bitcast_fusion.refs_0_), channel_id=1, source_target_pairs={{0,2},{1,3},{2,4},{3,5},{4,6},{5,7},{6,0},{7,1},{8,10},{9,11},{10,... | collective-permute-start | bytes 1572872 | tf_op jit(solution)/shard_map/ppermute | solution.py:411
  33.1 18.4 %collective-permute-start.11 = (bf16[3,512,512]{2,1,0:T(8,128)(2,1)S(1)}, bf16[3,512,512]{2,1,0:T(8,128)(2,1)S(1)}, u32[]{:S(2)}, u32[]{:S(2)}) collective-permute-start(bf16[3,512,512]{2,1,0:T(8,128)(2,1)S(1)} %hold.4.refs_10_), channel_id=1, source_target_pairs={{0,1},{1,0},{2,3},{3,2},{4,5},{5,4},{6,7},{7,6},{8,9},{9,8},{10,11... | collective-permute-start | bytes 4718600 | tf_op jit(solution)/shard_map/ppermute | solution.py:422
  36.1 13.4 %collective-permute-start.9 = (bf16[512,512]{1,0:T(8,128)(2,1)S(1)}, bf16[512,512]{1,0:T(8,128)(2,1)S(1)}, u32[]{:S(2)}, u32[]{:S(2)}) collective-permute-start(bf16[512,512]{1,0:T(8,128)(2,1)S(1)} %pad_maximum_fusion.1), channel_id=1, source_target_pairs={{0,6},{1,7},{2,0},{3,1},{4,2},{5,3},{6,4},{7,5},{8,14},{9,15},{10,... | collective-permute-start | bytes 1572872 | tf_op jit(solution)/shard_map/ppermute | solution.py:416
  37.2 14.3 %collective-permute-start.8 = (bf16[512,512]{1,0:T(8,128)(2,1)S(1)}, bf16[512,512]{1,0:T(8,128)(2,1)S(1)}, u32[]{:S(2)}, u32[]{:S(2)}) collective-permute-start(bf16[512,512]{1,0:T(8,128)(2,1)S(1)} %pad_maximum_fusion.1), channel_id=1, source_target_pairs={{0,2},{1,3},{2,4},{3,5},{4,6},{5,7},{6,0},{7,1},{8,10},{9,11},{10,... | collective-permute-start | bytes 1572872 | tf_op jit(solution)/shard_map/ppermute | solution.py:415
  37.6 2.8 %collective-permute-start.13 = (bf16[64,512]{1,0:T(8,128)(2,1)S(1)}, bf16[64,512]{1,0:T(8,128)(2,1)S(1)}, u32[]{:S(2)}, u32[]{:S(2)}) collective-permute-start(bf16[64,512]{1,0:T(8,128)(2,1)S(1)} %copy-done.13), channel_id=1, source_target_pairs={{192,128},{200,136},{208,144},{216,152},{224,160},{232,168},{240,1... | collective-permute-start | bytes 196616 | tf_op jit(solution)/shard_map/ppermute | solution.py:420
  53.0 10.0 %collective-permute-start.17 = (bf16[3,512,512]{2,1,0:T(8,128)(2,1)S(1)}, bf16[3,512,512]{2,1,0:T(8,128)(2,1)S(1)}, u32[]{:S(2)}, u32[]{:S(2)}) collective-permute-start(bf16[3,512,512]{2,1,0:T(8,128)(2,1)S(1)} %pad_maximum_fusion.refs_4_.refs_6_), channel_id=1, source_target_pairs={{0,1},{1,0},{2,3},{3,2},{4,5},{5,4},{6,7},{7,6},{8,9},{9,8},{10,11... | collective-permute-start | bytes 4718600 | tf_op jit(solution)/shard_map/ppermute | solution.py:431
  54.3 7.8 %collective-permute-start.16 = (bf16[256,512]{1,0:T(8,128)(2,1)S(1)}, bf16[256,512]{1,0:T(8,128)(2,1)S(1)}, u32[]{:S(2)}, u32[]{:S(2)}) collective-permute-start(bf16[256,512]{1,0:T(8,128)(2,1)S(1)} %slice.65), channel_id=1, source_target_pairs={{0,6},{1,7},{2,0},{3,1},{4,2},{5,3},{6,4},{7,5},{8,14},{9,15},{10,... | collective-permute-start | bytes 786440 | tf_op jit(solution)/shard_map/ppermute | solution.py:430
  54.3 8.7 %collective-permute-start.15 = (bf16[256,512]{1,0:T(8,128)(2,1)S(1)}, bf16[256,512]{1,0:T(8,128)(2,1)S(1)}, u32[]{:S(2)}, u32[]{:S(2)}) collective-permute-start(bf16[256,512]{1,0:T(8,128)(2,1)S(1)} %slice.64), channel_id=1, source_target_pairs={{0,2},{1,3},{2,4},{3,5},{4,6},{5,7},{6,0},{7,1},{8,10},{9,11},{10,... | collective-permute-start | bytes 786440 | tf_op jit(solution)/shard_map/ppermute | solution.py:429
  63.8 11.1 %collective-permute-start.18 = (bf16[512,512]{1,0:T(8,128)(2,1)}, bf16[512,512]{1,0:T(8,128)(2,1)}, u32[]{:S(2)}, u32[]{:S(2)}) collective-permute-start(bf16[512,512]{1,0:T(8,128)(2,1)} %hold.5.refs_5_.refs_7_), channel_id=1, source_target_pairs={{0,1},{1,0},{2,3},{3,2},{4,5},{5,4},{6,7},{7,6},{8,9},{9,8},{10,11... | collective-permute-start | bytes 1572872 | tf_op jit(solution)/shard_map/ppermute | solution.py:434
  69.3 5.0 %collective-permute-start.14 = (bf16[64,512]{1,0:T(8,128)(2,1)S(1)}, bf16[64,512]{1,0:T(8,128)(2,1)S(1)}, u32[]{:S(2)}, u32[]{:S(2)}) collective-permute-start(bf16[64,512]{1,0:T(8,128)(2,1)S(1)} %get-tuple-element.68.refs_0_), channel_id=1, source_target_pairs={{0,8},{64,72},{128,136},{192,200},{1,9},{65,73},{129,137},{193,201... | collective-permute-start | bytes 196616 | tf_op jit(solution)/shard_map/ppermute | solution.py:447
  74.3 5.3 %collective-permute-start.19 = (bf16[1,64,512]{2,1,0:T(8,128)(2,1)S(1)}, bf16[1,64,512]{2,1,0:T(8,128)(2,1)S(1)}, u32[]{:S(2)}, u32[]{:S(2)}) collective-permute-start(bf16[1,64,512]{2,1,0:T(8,128)(2,1)S(1)} %bitcast.21), channel_id=1, source_target_pairs={{8,16},{72,80},{136,144},{200,208},{40,48},{9,17},{73,81},{137,145... | collective-permute-start | bytes 196616 | tf_op jit(solution)/shard_map/ppermute | solution.py:446
  81.0 3.0 %collective-permute-start.21 = (bf16[2,64,512]{2,1,0:T(8,128)(2,1)S(1)}, bf16[2,64,512]{2,1,0:T(8,128)(2,1)S(1)}, u32[]{:S(2)}, u32[]{:S(2)}) collective-permute-start(bf16[2,64,512]{2,1,0:T(8,128)(2,1)S(1)} %append.5), channel_id=1, source_target_pairs={{16,24},{80,88},{144,152},{208,216},{48,56},{17,25},{81,89},{145,1... | collective-permute-start | bytes 393224 | tf_op jit(solution)/shard_map/ppermute | solution.py:446
  83.3 2.4 %collective-permute-start.22 = (bf16[64,512]{1,0:T(8,128)(2,1)S(1)}, bf16[64,512]{1,0:T(8,128)(2,1)S(1)}, u32[]{:S(2)}, u32[]{:S(2)}) collective-permute-start(bf16[64,512]{1,0:T(8,128)(2,1)S(1)} %step.8.refs_2_), channel_id=1, source_target_pairs={{16,24},{80,88},{144,152},{208,216},{17,25},{81,89},{145,153},{209... | collective-permute-start | bytes 196616 | tf_op jit(solution)/shard_map/ppermute | solution.py:447
  85.8 11.0 %collective-permute-start.23 = (bf16[3,64,512]{2,1,0:T(8,128)(2,1)S(1)}, bf16[3,64,512]{2,1,0:T(8,128)(2,1)S(1)}, u32[]{:S(2)}, u32[]{:S(2)}) collective-permute-start(bf16[3,64,512]{2,1,0:T(8,128)(2,1)S(1)} %append.6), channel_id=1, source_target_pairs={{24,32},{88,96},{152,160},{216,224},{56,0},{25,33},{89,97},{153,16... | collective-permute-start | bytes 589832 | tf_op jit(solution)/shard_map/ppermute | solution.py:446
  88.7 10.1 %collective-permute-start.24 = (bf16[64,512]{1,0:T(8,128)(2,1)S(1)}, bf16[64,512]{1,0:T(8,128)(2,1)S(1)}, u32[]{:S(2)}, u32[]{:S(2)}) collective-permute-start(bf16[64,512]{1,0:T(8,128)(2,1)S(1)} %step.9.refs_3_), channel_id=1, source_target_pairs={{24,32},{88,96},{152,160},{216,224},{25,33},{89,97},{153,161},{217... | collective-permute-start | bytes 196616 | tf_op jit(solution)/shard_map/ppermute | solution.py:447
  98.9 5.8 %collective-permute-start.25 = (bf16[4,64,512]{2,1,0:T(8,128)(2,1)S(1)}, bf16[4,64,512]{2,1,0:T(8,128)(2,1)S(1)}, u32[]{:S(2)}, u32[]{:S(2)}) collective-permute-start(bf16[4,64,512]{2,1,0:T(8,128)(2,1)S(1)} %append.7), channel_id=1, source_target_pairs={{32,40},{96,104},{160,168},{224,232},{0,8},{33,41},{97,105},{161,1... | collective-permute-start | bytes 786440 | tf_op jit(solution)/shard_map/ppermute | solution.py:446
  101.8 5.2 %collective-permute-start.26 = (bf16[64,512]{1,0:T(8,128)(2,1)S(1)}, bf16[64,512]{1,0:T(8,128)(2,1)S(1)}, u32[]{:S(2)}, u32[]{:S(2)}) collective-permute-start(bf16[64,512]{1,0:T(8,128)(2,1)S(1)} %step.10.refs_4_), channel_id=1, source_target_pairs={{32,40},{96,104},{160,168},{224,232},{33,41},{97,105},{161,169},{2... | collective-permute-start | bytes 196616 | tf_op jit(solution)/shard_map/ppermute | solution.py:447
  103.1 5.0 %collective-permute-start.27 = (bf16[64,512]{1,0:T(8,128)(2,1)S(1)}, bf16[64,512]{1,0:T(8,128)(2,1)S(1)}, u32[]{:S(2)}, u32[]{:S(2)}) collective-permute-start(bf16[64,512]{1,0:T(8,128)(2,1)S(1)} %own_row.2.refs_0_), channel_id=1, source_target_pairs={{8,0},{16,8},{24,16},{72,64},{80,72},{88,80},{136,128},{144,136},{... | collective-permute-start | bytes 196616 | tf_op jit(solution)/shard_map/ppermute | solution.py:461
  108.1 4.3 %collective-permute-start.28 = (bf16[5,64,512]{2,1,0:T(8,128)(2,1)S(1)}, bf16[5,64,512]{2,1,0:T(8,128)(2,1)S(1)}, u32[]{:S(2)}, u32[]{:S(2)}) collective-permute-start(bf16[5,64,512]{2,1,0:T(8,128)(2,1)S(1)} %append.8), channel_id=1, source_target_pairs={{40,48},{104,112},{168,176},{232,240},{8,16},{41,49},{105,113},{16... | collective-permute-start | bytes 983048 | tf_op jit(solution)/shard_map/ppermute | solution.py:446
  110.5 4.6 %collective-permute-start.29 = (bf16[64,512]{1,0:T(8,128)(2,1)S(1)}, bf16[64,512]{1,0:T(8,128)(2,1)S(1)}, u32[]{:S(2)}, u32[]{:S(2)}) collective-permute-start(bf16[64,512]{1,0:T(8,128)(2,1)S(1)} %step.11.refs_5_), channel_id=1, source_target_pairs={{40,48},{104,112},{168,176},{232,240},{41,49},{105,113},{169,177},... | collective-permute-start | bytes 196616 | tf_op jit(solution)/shard_map/ppermute | solution.py:447
  111.1 5.3 %collective-permute-start.30 = (bf16[64,512]{1,0:T(8,128)(2,1)S(1)}, bf16[64,512]{1,0:T(8,128)(2,1)S(1)}, u32[]{:S(2)}, u32[]{:S(2)}) collective-permute-start(bf16[64,512]{1,0:T(8,128)(2,1)S(1)} %collective-permute-done.27.refs_1_), channel_id=1, source_target_pairs={{8,0},{16,8},{24,16},{72,64},{80,72},{88,80},{136,128},{144,136},{... | collective-permute-start | bytes 196616 | tf_op jit(solution)/shard_map/ppermute | solution.py:461
  116.5 7.1 %collective-permute-start.31 = (bf16[6,64,512]{2,1,0:T(8,128)(2,1)S(1)}, bf16[6,64,512]{2,1,0:T(8,128)(2,1)S(1)}, u32[]{:S(2)}, u32[]{:S(2)}) collective-permute-start(bf16[6,64,512]{2,1,0:T(8,128)(2,1)S(1)} %append.9), channel_id=1, source_target_pairs={{48,56},{112,120},{176,184},{240,248},{16,24},{49,57},{113,121},{1... | collective-permute-start | bytes 1179656 | tf_op jit(solution)/shard_map/ppermute | solution.py:446
  118.9 7.7 %collective-permute-start.33 = (bf16[64,512]{1,0:T(8,128)(2,1)S(1)}, bf16[64,512]{1,0:T(8,128)(2,1)S(1)}, u32[]{:S(2)}, u32[]{:S(2)}) collective-permute-start(bf16[64,512]{1,0:T(8,128)(2,1)S(1)} %step.12.refs_6_), channel_id=1, source_target_pairs={{48,56},{112,120},{176,184},{240,248},{49,57},{113,121},{177,185},... | collective-permute-start | bytes 196616 | tf_op jit(solution)/shard_map/ppermute | solution.py:447
  119.6 7.0 %collective-permute-start.32 = (bf16[64,512]{1,0:T(8,128)(2,1)S(1)}, bf16[64,512]{1,0:T(8,128)(2,1)S(1)}, u32[]{:S(2)}, u32[]{:S(2)}) collective-permute-start(bf16[64,512]{1,0:T(8,128)(2,1)S(1)} %collective-permute-done.30.refs_2_), channel_id=1, source_target_pairs={{8,0},{16,8},{24,16},{72,64},{80,72},{88,80},{136,128},{144,136},{... | collective-permute-start | bytes 196616 | tf_op jit(solution)/shard_map/ppermute | solution.py:461
  120.9 37.1 %collective-permute-start.47 = (bf16[256,512]{1,0:T(8,128)(2,1)S(1)}, bf16[256,512]{1,0:T(8,128)(2,1)S(1)}, u32[]{:S(2)}, u32[]{:S(2)}) collective-permute-start(bf16[256,512]{1,0:T(8,128)(2,1)S(1)} %copy-done.12), channel_id=1, source_target_pairs={{0,2},{1,3},{2,4},{3,5},{4,6},{5,7},{6,0},{7,1},{8,10},{9,11},{10,... | collective-permute-start | bytes 786440 | tf_op jit(solution)/shard_map/ppermute | solution.py:454
  121.2 36.8 %collective-permute-start.48 = (bf16[256,512]{1,0:T(8,128)(2,1)S(1)}, bf16[256,512]{1,0:T(8,128)(2,1)S(1)}, u32[]{:S(2)}, u32[]{:S(2)}) collective-permute-start(bf16[256,512]{1,0:T(8,128)(2,1)S(1)} %copy-done.11), channel_id=1, source_target_pairs={{0,6},{1,7},{2,0},{3,1},{4,2},{5,3},{6,4},{7,5},{8,14},{9,15},{10,... | collective-permute-start | bytes 786440 | tf_op jit(solution)/shard_map/ppermute | solution.py:455
  130.4 2.8 %collective-permute-start.39 = (bf16[64,512]{1,0:T(8,128)(2,1)S(1)}, bf16[64,512]{1,0:T(8,128)(2,1)S(1)}, u32[]{:S(2)}, u32[]{:S(2)}) collective-permute-start(bf16[64,512]{1,0:T(8,128)(2,1)S(1)} %own_row.3.refs_7_), channel_id=1, source_target_pairs={{32,16},{40,24},{48,32},{56,40},{96,80},{104,88},{112,96},{120,104... | collective-permute-start | bytes 196616 | tf_op jit(solution)/shard_map/ppermute | solution.py:478
  131.2 3.3 %collective-permute-start.38 = (bf16[64,512]{1,0:T(8,128)(2,1)S(1)}, bf16[64,512]{1,0:T(8,128)(2,1)S(1)}, u32[]{:S(2)}, u32[]{:S(2)}) collective-permute-start(bf16[64,512]{1,0:T(8,128)(2,1)S(1)} %own_row.3.refs_7_), channel_id=1, source_target_pairs={{32,8},{40,16},{48,24},{56,32},{96,72},{104,80},{112,88},{120,96},... | collective-permute-start | bytes 196616 | tf_op jit(solution)/shard_map/ppermute | solution.py:478
  131.9 16.5 %collective-permute-start.37 = (bf16[64,512]{1,0:T(8,128)(2,1)S(1)}, bf16[64,512]{1,0:T(8,128)(2,1)S(1)}, u32[]{:S(2)}, u32[]{:S(2)}) collective-permute-start(bf16[64,512]{1,0:T(8,128)(2,1)S(1)} %own_row.3.refs_7_), channel_id=1, source_target_pairs={{56,0},{120,64},{184,128},{248,192},{57,1},{121,65},{185,129},{249... | collective-permute-start | bytes 196616 | tf_op jit(solution)/shard_map/ppermute | solution.py:478
  133.2 16.5 %collective-permute-start.36 = (bf16[64,512]{1,0:T(8,128)(2,1)S(1)}, bf16[64,512]{1,0:T(8,128)(2,1)S(1)}, u32[]{:S(2)}, u32[]{:S(2)}) collective-permute-start(bf16[64,512]{1,0:T(8,128)(2,1)S(1)} %own_row.3.refs_7_), channel_id=1, source_target_pairs={{48,0},{56,8},{112,64},{120,72},{176,128},{184,136},{240,192},{248... | collective-permute-start | bytes 196616 | tf_op jit(solution)/shard_map/ppermute | solution.py:478
  134.5 15.3 %collective-permute-start.35 = (bf16[64,512]{1,0:T(8,128)(2,1)S(1)}, bf16[64,512]{1,0:T(8,128)(2,1)S(1)}, u32[]{:S(2)}, u32[]{:S(2)}) collective-permute-start(bf16[64,512]{1,0:T(8,128)(2,1)S(1)} %own_row.3.refs_7_), channel_id=1, source_target_pairs={{40,0},{48,8},{56,16},{104,64},{112,72},{120,80},{168,128},{176,13... | collective-permute-start | bytes 196616 | tf_op jit(solution)/shard_map/ppermute | solution.py:478
  148.4 8.9 %collective-permute-start.34 = (bf16[64,512]{1,0:T(8,128)(2,1)S(1)}, bf16[64,512]{1,0:T(8,128)(2,1)S(1)}, u32[]{:S(2)}, u32[]{:S(2)}) collective-permute-start(bf16[64,512]{1,0:T(8,128)(2,1)S(1)} %own_row.3.refs_7_), channel_id=1, source_target_pairs={{32,0},{40,8},{48,16},{56,24},{96,64},{104,72},{112,80},{120,88},{... | collective-permute-start | bytes 196616 | tf_op jit(solution)/shard_map/ppermute | solution.py:478
  149.7 17.0 %collective-permute-start.42 = (bf16[4,64,512]{2,1,0:T(8,128)(2,1)S(1)}, bf16[4,64,512]{2,1,0:T(8,128)(2,1)S(1)}, u32[]{:S(2)}, u32[]{:S(2)}) collective-permute-start(bf16[4,64,512]{2,1,0:T(8,128)(2,1)S(1)} %collect.2.refs_1_), channel_id=1, source_target_pairs={{0,192},{8,200},{16,208},{24,216},{32,224},{40,232},{48,240},{56,2... | collective-permute-start | bytes 786440 | tf_op jit(solution)/shard_map/ppermute | solution.py:469
  149.8 16.9 %collective-permute-start.41 = (bf16[4,64,512]{2,1,0:T(8,128)(2,1)S(1)}, bf16[4,64,512]{2,1,0:T(8,128)(2,1)S(1)}, u32[]{:S(2)}, u32[]{:S(2)}) collective-permute-start(bf16[4,64,512]{2,1,0:T(8,128)(2,1)S(1)} %collect.2.refs_1_), channel_id=1, source_target_pairs={{0,64},{8,72},{16,80},{24,88},{32,96},{40,104},{48,112},{56,120},{... | collective-permute-start | bytes 786440 | tf_op jit(solution)/shard_map/ppermute | solution.py:468
  158.0 26.4 %collective-permute-start.49 = (bf16[512,512]{1,0:T(8,128)(2,1)S(1)}, bf16[512,512]{1,0:T(8,128)(2,1)S(1)}, u32[]{:S(2)}, u32[]{:S(2)}) collective-permute-start(bf16[512,512]{1,0:T(8,128)(2,1)S(1)} %hold.7.refs_11_), channel_id=1, source_target_pairs={{0,1},{1,0},{2,3},{3,2},{4,5},{5,4},{6,7},{7,6},{8,9},{9,8},{10,11... | collective-permute-start | bytes 1572872 | tf_op jit(solution)/shard_map/ppermute | solution.py:481
  166.8 14.6 %collective-permute-start.44 = (bf16[4,64,512]{2,1,0:T(8,128)(2,1)S(1)}, bf16[4,64,512]{2,1,0:T(8,128)(2,1)S(1)}, u32[]{:S(2)}, u32[]{:S(2)}) collective-permute-start(bf16[4,64,512]{2,1,0:T(8,128)(2,1)S(1)} %collect.3.refs_1_), channel_id=1, source_target_pairs={{0,64},{8,72},{16,80},{24,88},{32,96},{40,104},{48,112},{56,120},{... | collective-permute-start | bytes 786440 | tf_op jit(solution)/shard_map/ppermute | solution.py:282
  166.8 14.7 %collective-permute-start.43 = (bf16[4,64,512]{2,1,0:T(8,128)(2,1)S(1)}, bf16[4,64,512]{2,1,0:T(8,128)(2,1)S(1)}, u32[]{:S(2)}, u32[]{:S(2)}) collective-permute-start(bf16[4,64,512]{2,1,0:T(8,128)(2,1)S(1)} %collect.3.refs_1_), channel_id=1, source_target_pairs={{0,192},{8,200},{16,208},{24,216},{32,224},{40,232},{48,240},{56,2... | collective-permute-start | bytes 786440 | tf_op jit(solution)/shard_map/ppermute | solution.py:283
  169.4 15.0 %collective-permute-start.50 = (bf16[4,64,512]{2,1,0:T(8,128)(2,1)S(1)}, bf16[4,64,512]{2,1,0:T(8,128)(2,1)S(1)}, u32[]{:S(2)}, u32[]{:S(2)}) collective-permute-start(bf16[4,64,512]{2,1,0:T(8,128)(2,1)S(1)} %collect.2.refs_1_), channel_id=1, source_target_pairs={{0,128},{8,136},{16,144},{24,152},{32,160},{40,168},{48,176},{56,1... | collective-permute-start | bytes 786440 | tf_op jit(solution)/shard_map/ppermute | solution.py:470
  181.4 8.0 %collective-permute-start.45 = (bf16[2,64,512]{2,1,0:T(8,128)(2,1)S(1)}, bf16[2,64,512]{2,1,0:T(8,128)(2,1)S(1)}, u32[]{:S(2)}, u32[]{:S(2)}) collective-permute-start(bf16[2,64,512]{2,1,0:T(8,128)(2,1)S(1)} %slice.73), channel_id=1, source_target_pairs={{0,64},{8,72},{16,80},{24,88},{32,96},{40,104},{48,112},{56,120},{... | collective-permute-start | bytes 393224 | tf_op jit(solution)/shard_map/ppermute | solution.py:284
  181.5 7.9 %collective-permute-start.46 = (bf16[2,64,512]{2,1,0:T(8,128)(2,1)S(1)}, bf16[2,64,512]{2,1,0:T(8,128)(2,1)S(1)}, u32[]{:S(2)}, u32[]{:S(2)}) collective-permute-start(bf16[2,64,512]{2,1,0:T(8,128)(2,1)S(1)} %slice.74), channel_id=1, source_target_pairs={{0,192},{8,200},{16,208},{24,216},{32,224},{40,232},{48,240},{56,2... | collective-permute-start | bytes 393224 | tf_op jit(solution)/shard_map/ppermute | solution.py:285
  (17 other events, 247.8 us)

commit v3 on v2

--- a/solution.py
+++ b/solution.py
@@ -73,18 +73,21 @@
 
 def early_kernel(t, sc, base, solved, inverse, *refs):
     *blocks, out, inv, sem = refs
-    fetch = pltpu.make_async_copy(inverse.at[t], inv, sem)
-    fetch.start()
-    out[...] = base[...].astype(F32)
-
-    def subtract(value):
-        out[...] -= value
-
-    @pl.loop(0, solved.shape[0])
-    def _(j):
-        times_block(sc, j, solved[j], blocks, subtract)
-
-    fetch.wait()
+
+    @pl.when(sc[AT_Z] == t)
+    def _():
+        fetch = pltpu.make_async_copy(inverse.at[t], inv, sem)
+        fetch.start()
+        out[...] = base[...].astype(F32)
+
+        def subtract(value):
+            out[...] -= value
+
+        @pl.loop(0, solved.shape[0])
+        def _(j):
+            times_block(sc, j, solved[j], blocks, subtract)
+
+        fetch.wait()
 
 
 def early(t, sc, base, solved, inverse, blocks):
@@ -113,10 +116,12 @@
     def subtract(value):
         base[...] = (acc[...] - value).astype(BF)
 
-    times_block(sc, t - 1, last[...], blocks, subtract)
-    out[...] = lax.dot_general(
-        base[...], inv[...], NT, preferred_element_type=F32
-    ).astype(BF)
+    @pl.when(sc[AT_Z] == t)
+    def _():
+        times_block(sc, t - 1, last[...], blocks, subtract)
+        out[...] = lax.dot_general(
+            base[...], inv[...], NT, preferred_element_type=F32
+        ).astype(BF)
 
 
 def step(t, sc, acc, last, inv, blocks):
@@ -188,24 +193,26 @@
     )(*parts)
 
 
-def append(known, last):
+def append(sc, known, last):
     n, c, b = known.shape
 
-    def kernel(known, last, out):
-        out[:n] = known[...]
-        out[n] = last[...]
+    def kernel(sc, known, last, out):
+        @pl.when(sc[AT_Z] == n + 1)
+        def _():
+            out[:n] = known[...]
+            out[n] = last[...]
 
     return pl.pallas_call(
         kernel,
         out_shape=jax.ShapeDtypeStruct((n + 1, c, b), BF),
-        in_specs=[VMEM, VMEM],
+        in_specs=[SMEM, VMEM, VMEM],
         out_specs=VMEM,
         compiler_params=params(),
         cost_estimate=pl.CostEstimate(
             flops=0, bytes_accessed=4 * (n + 1) * c * b, transcendentals=0
         ),
         name="append",
-    )(known, last)
+    )(sc, known, last)
 
 
 def own_row(sc, solved):
@@ -472,7 +479,7 @@
         fresh = step(t, sc, acc, last, inv, blocks0)
         solved.append(fresh)
         before[t] = [last] if t == 1 else [sent, last]
-        known = last[None] if t == 1 else append(sent, last)
+        known = last[None] if t == 1 else append(sc, sent, last)
 
     own_s = own_row(sc, solved)
     back = [lax.ppermute(own_s, "row", back_z(d, range(4, 8))) for d in range(1, 8)]

time: 196 us -> 190 us (0.969)
  the two profiles are of different devices: /device:TPU:1 before, /device:TPU:2 now
where the time goes in v3:
time: 190 us; the launch traced here: 187 us
  waiting for transfers between devices  85.3 us (45%)
  starting transfers between devices  55.8 us (29%)
  Pallas kernels  31.9 us (17%)
  local copies, waits for them, and re-layouts  10.2 us (5%)
  other arithmetic  2.32 us (1%)
    ppermute x7, waiting for transfers between devices, on_device(): lax.ppermute(own_s, 'row', back_z(d, range(4, 8)))  18.5 us
    ppermute x1, waiting for transfers between devices, spread_y(): before = lax.ppermute(rows, 'row', shift_y(1))  11.8 us
    ppermute x6, waiting for transfers between devices, on_device(): sent = lax.ppermute(known, 'row', hop_z_early(t))  10.4 us
    pallas_call x2, Pallas kernels, final(): pl.pallas_call(lambda *refs: final_kernel(start, *refs), out_shape=(jax.S...  10.2 us
    ppermute x1, waiting for transfers between devices, on_device(): right = lax.ppermute(window, 'col', shift_x(-1))  9.44 us
    ppermute x3, waiting for transfers between devices, on_device(): lax.ppermute((back_a or [own_s])[-1], 'row', back_z(1, range(1, 4)))  8.91 us
    ppermute x7, starting transfers between devices, on_device(): last = lax.ppermute(fresh, 'row', hop_z(t))  7.93 us
    pallas_call x7, Pallas kernels, step(): pl.pallas_call(lambda *refs: step_kernel(t, *refs), out_shape=jax.ShapeDt...  7.72 us
  transfers between devices with their start and end apart: 51, of which 18 were waited for; matrix products, arithmetic and copies ran while one was open for 3% of the time, Pallas kernels for 12%

profile of v3, /device:TPU:2, one launch (start us, length us, event | category | flops | bytes accessed | tf_op | source)
XLA Modules:
  0.0 187.1 jit_solution(2205247254160214981)
XLA Ops:
  0.6 1.2 slice_bitcast_fusion.2
  1.8 1.3 collective-permute-start
  3.1 1.4 collective-permute-start.4
  4.5 2.9 %collective-permute-start.1 = (bf16[256,512]{1,0:T(8,128)(2,1)S(1)}, bf16[256,512]{1,0:T(8,128)(2,1)S(1)}, u32[]{:S(2)}, u32[]{:S(2)}) collective-permute-start(bf16[256,512]{1,0:T(8,128)(2,1)S(1)} %get-tuple-element.118), channel_id=1, source_target_pairs={{192,128},{200,136},{208,144},{216,152},{224,160},{232,168},{240,1... | collective-permute-start | bytes 786440 | tf_op jit(solution)/shard_map/ppermute | solution.py:404
  7.3 1.3 collective-permute-start.3
  10.6 2.7 %collective-permute-done = bf16[256,512]{1,0:T(8,128)(2,1)S(1)} collective-permute-done((bf16[256,512]{1,0:T(8,128)(2,1)S(1)}, bf16[256,512]{1,0:T(8,128)(2,1)S(1)}, u32[]{:S(2)}, u32[]{:S(2)}) %collective-permute-start) | collective-permute-done | bytes 262176 | tf_op jit(solution)/shard_map/ppermute | solution.py:401
  13.3 1.3 collective-permute-start.10
  14.6 2.0 %collective-permute-start.2 = (bf16[256,512]{1,0:T(8,128)(2,1)S(1)}, bf16[256,512]{1,0:T(8,128)(2,1)}, u32[]{:S(2)}, u32[]{:S(2)}) collective-permute-start(bf16[256,512]{1,0:T(8,128)(2,1)S(1)} %collective-permute-done), channel_id=1, source_target_pairs={{0,64},{8,72},{16,80},{24,88},{32,96},{40,104},{48,112},{56,120},{... | collective-permute-start | bytes 786440 | tf_op jit(solution)/shard_map/ppermute | solution.py:405
  16.6 1.4 collective-permute-start.5
  18.7 1.9 %collective-permute-done.10 = bf16[64,512]{1,0:T(8,128)(2,1)S(1)} collective-permute-done((bf16[64,512]{1,0:T(8,128)(2,1)S(1)}, bf16[64,512]{1,0:T(8,128)(2,1)S(1)}, u32[]{:S(2)}, u32[]{:S(2)}) %collective-permute-start.10) | collective-permute-done | bytes 65568 | tf_op jit(solution)/shard_map/ppermute | solution.py:427
  20.7 1.5 collective-permute-start.6
  22.2 1.2 select_select_fusion.1
  23.4 7.3 %collective-permute-done.7.refs_2_ = bf16[512,512]{1,0:T(8,128)(2,1)S(1)} collective-permute-done((bf16[512,512]{1,0:T(8,128)(2,1)S(1)}, bf16[512,512]{1,0:T(8,128)(2,1)S(1)}, u32[]{:S(2)}, u32[]{:S(2)}) %collective-permute-start.7) | collective-permute-done | bytes 524320 | tf_op jit(solution)/shard_map/ppermute | solution.py:419
  30.7 2.4 %collective-permute-done.6.refs_1_ = bf16[512,512]{1,0:T(8,128)(2,1)S(1)} collective-permute-done((bf16[512,512]{1,0:T(8,128)(2,1)S(1)}, bf16[512,512]{1,0:T(8,128)(2,1)S(1)}, u32[]{:S(2)}, u32[]{:S(2)}) %collective-permute-start.6) | collective-permute-done | bytes 524320 | tf_op jit(solution)/shard_map/ppermute | solution.py:418
  33.3 1.9 %collective-permute-start.9 = (bf16[512,512]{1,0:T(8,128)(2,1)S(1)}, bf16[512,512]{1,0:T(8,128)(2,1)S(1)}, u32[]{:S(2)}, u32[]{:S(2)}) collective-permute-start(bf16[512,512]{1,0:T(8,128)(2,1)S(1)} %pad_maximum_fusion.1), channel_id=1, source_target_pairs={{0,6},{1,7},{2,0},{3,1},{4,2},{5,3},{6,4},{7,5},{8,14},{9,15},{10,... | collective-permute-start | bytes 1572872 | tf_op jit(solution)/shard_map/ppermute | solution.py:423
  38.2 9.4 %collective-permute-done.9 = bf16[512,512]{1,0:T(8,128)(2,1)S(1)} collective-permute-done((bf16[512,512]{1,0:T(8,128)(2,1)S(1)}, bf16[512,512]{1,0:T(8,128)(2,1)S(1)}, u32[]{:S(2)}, u32[]{:S(2)}) %collective-permute-start.9) | collective-permute-done | bytes 524320 | tf_op jit(solution)/shard_map/ppermute | solution.py:423
  47.6 1.6 collective-permute-done.8
  49.2 1.2 copy-done.4
  50.7 2.7 %collective-permute-start.16 = (bf16[256,512]{1,0:T(8,128)(2,1)S(1)}, bf16[256,512]{1,0:T(8,128)(2,1)S(1)}, u32[]{:S(2)}, u32[]{:S(2)}) collective-permute-start(bf16[256,512]{1,0:T(8,128)(2,1)S(1)} %slice.65), channel_id=1, source_target_pairs={{0,6},{1,7},{2,0},{3,1},{4,2},{5,3},{6,4},{7,5},{8,14},{9,15},{10,... | collective-permute-start | bytes 786440 | tf_op jit(solution)/shard_map/ppermute | solution.py:437
  53.4 6.1 %collective-permute-done.16.refs_1_ = bf16[256,512]{1,0:T(8,128)(2,1)S(1)} collective-permute-done((bf16[256,512]{1,0:T(8,128)(2,1)S(1)}, bf16[256,512]{1,0:T(8,128)(2,1)S(1)}, u32[]{:S(2)}, u32[]{:S(2)}) %collective-permute-start.16) | collective-permute-done | bytes 262176 | tf_op jit(solution)/shard_map/ppermute | solution.py:437
  59.6 2.2 %collective-permute-done.15.refs_0_ = bf16[256,512]{1,0:T(8,128)(2,1)S(1)} collective-permute-done((bf16[256,512]{1,0:T(8,128)(2,1)S(1)}, bf16[256,512]{1,0:T(8,128)(2,1)S(1)}, u32[]{:S(2)}, u32[]{:S(2)}) %collective-permute-start.15) | collective-permute-done | bytes 262176 | tf_op jit(solution)/shard_map/ppermute | solution.py:436
  63.5 2.2 %copy-done = bf16[8,512,512]{2,1,0:T(8,128)(2,1)S(1)} copy-done((bf16[8,512,512]{2,1,0:T(8,128)(2,1)S(1)}, bf16[8,512,512]{2,1,0:T(8,128)(2,1)}, u32[]{:S(2)}) %copy-start) | copy-done | bytes 4194328
  66.9 3.8 %collective-permute-start.14 = (bf16[64,512]{1,0:T(8,128)(2,1)S(1)}, bf16[64,512]{1,0:T(8,128)(2,1)S(1)}, u32[]{:S(2)}, u32[]{:S(2)}) collective-permute-start(bf16[64,512]{1,0:T(8,128)(2,1)S(1)} %get-tuple-element.68.refs_0_), channel_id=1, source_target_pairs={{0,8},{64,72},{128,136},{192,200},{1,9},{65,73},{129,137},{193,201... | collective-permute-start | bytes 196616 | tf_op jit(solution)/shard_map/ppermute | solution.py:454
  70.8 1.9 %collective-permute-done.14.refs_2_.refs_4_ = bf16[64,512]{1,0:T(8,128)(2,1)S(1)} collective-permute-done((bf16[64,512]{1,0:T(8,128)(2,1)S(1)}, bf16[64,512]{1,0:T(8,128)(2,1)S(1)}, u32[]{:S(2)}, u32[]{:S(2)}) %collective-permute-start.14) | collective-permute-done | bytes 65568 | tf_op jit(solution)/shard_map/ppermute | solution.py:454
  75.5 1.2 step.7.refs_1_
  83.6 1.3 collective-permute-start.23
  86.6 9.1 %collective-permute-done.23.refs_2_.known.refs_9_ = bf16[3,64,512]{2,1,0:T(8,128)(2,1)S(1)} collective-permute-done((bf16[3,64,512]{2,1,0:T(8,128)(2,1)S(1)}, bf16[3,64,512]{2,1,0:T(8,128)(2,1)S(1)}, u32[]{:S(2)}, u32[]{:S(2)}) %collective-permute-start.23) | collective-permute-done | bytes 196640 | tf_op jit(solution)/shard_map/ppermute | solution.py:453
  97.4 1.3 collective-permute-start.25
  101.0 1.5 collective-permute-start.27
  102.5 1.2 collective-permute-done.25.refs_2_.known.refs_11_
  104.8 2.5 %collective-permute-done.27.refs_1_ = bf16[64,512]{1,0:T(8,128)(2,1)S(1)} collective-permute-done((bf16[64,512]{1,0:T(8,128)(2,1)S(1)}, bf16[64,512]{1,0:T(8,128)(2,1)S(1)}, u32[]{:S(2)}, u32[]{:S(2)}) %collective-permute-start.27) | collective-permute-done | bytes 65568 | tf_op jit(solution)/shard_map/ppermute | solution.py:468
  110.3 1.3 collective-permute-start.30
  112.7 4.7 %collective-permute-done.30.refs_2_ = bf16[64,512]{1,0:T(8,128)(2,1)S(1)} collective-permute-done((bf16[64,512]{1,0:T(8,128)(2,1)S(1)}, bf16[64,512]{1,0:T(8,128)(2,1)S(1)}, u32[]{:S(2)}, u32[]{:S(2)}) %collective-permute-start.30) | collective-permute-done | bytes 65568 | tf_op jit(solution)/shard_map/ppermute | solution.py:468
  120.5 1.3 collective-permute-start.32
  122.2 1.7 collective-permute-start.48
  125.0 1.7 collective-permute-done.32.refs_3_
  131.4 1.3 collective-permute-start.37
  132.7 1.3 collective-permute-start.36
  134.0 1.3 collective-permute-start.35
  135.3 11.4 %collective-permute-done.37.refs_3_ = bf16[64,512]{1,0:T(8,128)(2,1)S(1)} collective-permute-done((bf16[64,512]{1,0:T(8,128)(2,1)S(1)}, bf16[64,512]{1,0:T(8,128)(2,1)S(1)}, u32[]{:S(2)}, u32[]{:S(2)}) %collective-permute-start.37) | collective-permute-done | bytes 65568 | tf_op jit(solution)/shard_map/ppermute | solution.py:485
  146.8 1.3 collective-permute-start.34
  148.1 1.5 collective-permute-start.42
  150.2 6.6 %collective-permute-done.34.refs_0_ = bf16[64,512]{1,0:T(8,128)(2,1)S(1)} collective-permute-done((bf16[64,512]{1,0:T(8,128)(2,1)S(1)}, bf16[64,512]{1,0:T(8,128)(2,1)S(1)}, u32[]{:S(2)}, u32[]{:S(2)}) %collective-permute-start.34) | collective-permute-done | bytes 65568 | tf_op jit(solution)/shard_map/ppermute | solution.py:485
  157.7 3.2 %collective-permute-start.43 = (bf16[4,64,512]{2,1,0:T(8,128)(2,1)S(1)}, bf16[4,64,512]{2,1,0:T(8,128)(2,1)S(1)}, u32[]{:S(2)}, u32[]{:S(2)}) collective-permute-start(bf16[4,64,512]{2,1,0:T(8,128)(2,1)S(1)} %collect.3.refs_1_), channel_id=1, source_target_pairs={{0,192},{8,200},{16,208},{24,216},{32,224},{40,232},{48,240},{56,2... | collective-permute-start | bytes 786440 | tf_op jit(solution)/shard_map/ppermute | solution.py:290
  161.4 11.8 %collective-permute-done.44.refs_5_ = bf16[4,64,512]{2,1,0:T(8,128)(2,1)S(1)} collective-permute-done((bf16[4,64,512]{2,1,0:T(8,128)(2,1)S(1)}, bf16[4,64,512]{2,1,0:T(8,128)(2,1)S(1)}, u32[]{:S(2)}, u32[]{:S(2)}) %collective-permute-start.44) | collective-permute-done | bytes 262176 | tf_op jit(solution)/shard_map/ppermute | solution.py:289
  173.3 3.5 %collective-permute-start.46 = (bf16[2,64,512]{2,1,0:T(8,128)(2,1)S(1)}, bf16[2,64,512]{2,1,0:T(8,128)(2,1)S(1)}, u32[]{:S(2)}, u32[]{:S(2)}) collective-permute-start(bf16[2,64,512]{2,1,0:T(8,128)(2,1)S(1)} %slice.74), channel_id=1, source_target_pairs={{0,192},{8,200},{16,208},{24,216},{32,224},{40,232},{48,240},{56,2... | collective-permute-start | bytes 393224 | tf_op jit(solution)/shard_map/ppermute | solution.py:292
  176.8 4.9 %final.2 = (f32[8,512,256]{2,1,0:T(8,128)}, f32[2,1,512,256]{3,2,1,0:T(8,128)S(1)}) custom-call(s32[22]{0:T(128)S(1)} %concatenate.6.refs_0_.sc, bf16[4,64,512]{2,1,0:T(8,128)(2,1)S(1)} %collect.2.refs_1_, bf16[4,64,512]{2,1,0:T(8,128)(2,1)S(1)} %collective-permute-done.42.refs_2_, bf16[4,64,512]{2,1,0:T(8,128)(2,1)S(1)} %collective-permute-done.50.refs_3_.refs_4_, ...), custom_call_target="tpu_custom_call" | custom-call | flops 1610612736 | bytes 2097152 | tf_op jit(solution)/shard_map/final/pallas_call | solution.py:355
  181.8 5.3 %final.3 = (f32[8,512,256]{2,1,0:T(8,128)}, f32[2,1,512,256]{3,2,1,0:T(8,128)}) custom-call(s32[22]{0:T(128)S(1)} %concatenate.6.refs_0_.sc, bf16[4,64,512]{2,1,0:T(8,128)(2,1)S(1)} %collect.3.refs_1_, bf16[4,64,512]{2,1,0:T(8,128)(2,1)S(1)} %collective-permute-done.43.refs_2_, ...), custom_call_target="tpu_custom_call", output_to_operand_aliasing={{0}: (15, {})} | custom-call | flops 1610612736 | bytes 2097152 | tf_op jit(solution)/shard_map/final/pallas_call | solution.py:355
  (129 shorter events, 40.4 us)
Async XLA Ops:
  1.8 11.5 %collective-permute-start = (bf16[256,512]{1,0:T(8,128)(2,1)S(1)}, bf16[256,512]{1,0:T(8,128)(2,1)S(1)}, u32[]{:S(2)}, u32[]{:S(2)}) collective-permute-start(bf16[256,512]{1,0:T(8,128)(2,1)S(1)} %get-tuple-element.118), channel_id=1, source_target_pairs={{192,0},{200,8},{208,16},{216,24},{224,32},{232,40},{240,48},{248,... | collective-permute-start | bytes 786440 | tf_op jit(solution)/shard_map/ppermute | solution.py:401
  3.1 13.5 %collective-permute-start.4 = (bf16[256,512]{1,0:T(8,128)(2,1)S(1)}, bf16[256,512]{1,0:T(8,128)(2,1)}, u32[]{:S(2)}, u32[]{:S(2)}) collective-permute-start(bf16[256,512]{1,0:T(8,128)(2,1)S(1)} %get-tuple-element.119), channel_id=1, source_target_pairs={{192,128},{200,136},{208,144},{216,152},{224,160},{232,168},{240,1... | collective-permute-start | bytes 786440 | tf_op jit(solution)/shard_map/ppermute | solution.py:402
  4.5 13.6 %collective-permute-start.1 = (bf16[256,512]{1,0:T(8,128)(2,1)S(1)}, bf16[256,512]{1,0:T(8,128)(2,1)S(1)}, u32[]{:S(2)}, u32[]{:S(2)}) collective-permute-start(bf16[256,512]{1,0:T(8,128)(2,1)S(1)} %get-tuple-element.118), channel_id=1, source_target_pairs={{192,128},{200,136},{208,144},{216,152},{224,160},{232,168},{240,1... | collective-permute-start | bytes 786440 | tf_op jit(solution)/shard_map/ppermute | solution.py:404
  7.3 14.8 %collective-permute-start.3 = (bf16[256,512]{1,0:T(8,128)(2,1)S(1)}, bf16[256,512]{1,0:T(8,128)(2,1)}, u32[]{:S(2)}, u32[]{:S(2)}) collective-permute-start(bf16[256,512]{1,0:T(8,128)(2,1)S(1)} %get-tuple-element.119), channel_id=1, source_target_pairs={{192,0},{200,8},{208,16},{216,24},{224,32},{232,40},{240,48},{248,... | collective-permute-start | bytes 786440 | tf_op jit(solution)/shard_map/ppermute | solution.py:403
  13.3 7.4 %collective-permute-start.10 = (bf16[64,512]{1,0:T(8,128)(2,1)S(1)}, bf16[64,512]{1,0:T(8,128)(2,1)S(1)}, u32[]{:S(2)}, u32[]{:S(2)}) collective-permute-start(bf16[64,512]{1,0:T(8,128)(2,1)S(1)} %get-tuple-element.59), channel_id=1, source_target_pairs={{192,0},{200,8},{208,16},{216,24},{224,32},{232,40},{240,48},{248,... | collective-permute-start | bytes 196616 | tf_op jit(solution)/shard_map/ppermute | solution.py:427
  14.6 7.6 %collective-permute-start.2 = (bf16[256,512]{1,0:T(8,128)(2,1)S(1)}, bf16[256,512]{1,0:T(8,128)(2,1)}, u32[]{:S(2)}, u32[]{:S(2)}) collective-permute-start(bf16[256,512]{1,0:T(8,128)(2,1)S(1)} %collective-permute-done), channel_id=1, source_target_pairs={{0,64},{8,72},{16,80},{24,88},{32,96},{40,104},{48,112},{56,120},{... | collective-permute-start | bytes 786440 | tf_op jit(solution)/shard_map/ppermute | solution.py:405
  16.6 5.6 %collective-permute-start.5 = (bf16[256,512]{1,0:T(8,128)(2,1)}, bf16[256,512]{1,0:T(8,128)(2,1)}, u32[]{:S(2)}, u32[]{:S(2)}) collective-permute-start(bf16[256,512]{1,0:T(8,128)(2,1)} %collective-permute-done.4), channel_id=1, source_target_pairs={{128,64},{136,72},{144,80},{152,88},{160,96},{168,104},{176,112},{... | collective-permute-start | bytes 786440 | tf_op jit(solution)/shard_map/ppermute | solution.py:406
  18.0 12.7 %collective-permute-start.7 = (bf16[512,512]{1,0:T(8,128)(2,1)S(1)}, bf16[512,512]{1,0:T(8,128)(2,1)S(1)}, u32[]{:S(2)}, u32[]{:S(2)}) collective-permute-start(bf16[512,512]{1,0:T(8,128)(2,1)S(1)} %slice_bitcast_fusion.refs_0_), channel_id=1, source_target_pairs={{0,6},{1,7},{2,0},{3,1},{4,2},{5,3},{6,4},{7,5},{8,14},{9,15},{10,... | collective-permute-start | bytes 1572872 | tf_op jit(solution)/shard_map/ppermute | solution.py:419
  20.7 12.4 %collective-permute-start.6 = (bf16[512,512]{1,0:T(8,128)(2,1)S(1)}, bf16[512,512]{1,0:T(8,128)(2,1)S(1)}, u32[]{:S(2)}, u32[]{:S(2)}) collective-permute-start(bf16[512,512]{1,0:T(8,128)(2,1)S(1)} %slice_bitcast_fusion.refs_0_), channel_id=1, source_target_pairs={{0,2},{1,3},{2,4},{3,5},{4,6},{5,7},{6,0},{7,1},{8,10},{9,11},{10,... | collective-permute-start | bytes 1572872 | tf_op jit(solution)/shard_map/ppermute | solution.py:418
  33.2 16.0 %collective-permute-start.11 = (bf16[3,512,512]{2,1,0:T(8,128)(2,1)S(1)}, bf16[3,512,512]{2,1,0:T(8,128)(2,1)S(1)}, u32[]{:S(2)}, u32[]{:S(2)}) collective-permute-start(bf16[3,512,512]{2,1,0:T(8,128)(2,1)S(1)} %hold.4.refs_10_), channel_id=1, source_target_pairs={{0,1},{1,0},{2,3},{3,2},{4,5},{5,4},{6,7},{7,6},{8,9},{9,8},{10,11... | collective-permute-start | bytes 4718600 | tf_op jit(solution)/shard_map/ppermute | solution.py:429
  33.3 14.3 %collective-permute-start.9 = (bf16[512,512]{1,0:T(8,128)(2,1)S(1)}, bf16[512,512]{1,0:T(8,128)(2,1)S(1)}, u32[]{:S(2)}, u32[]{:S(2)}) collective-permute-start(bf16[512,512]{1,0:T(8,128)(2,1)S(1)} %pad_maximum_fusion.1), channel_id=1, source_target_pairs={{0,6},{1,7},{2,0},{3,1},{4,2},{5,3},{6,4},{7,5},{8,14},{9,15},{10,... | collective-permute-start | bytes 1572872 | tf_op jit(solution)/shard_map/ppermute | solution.py:423
  35.2 14.0 %collective-permute-start.8 = (bf16[512,512]{1,0:T(8,128)(2,1)S(1)}, bf16[512,512]{1,0:T(8,128)(2,1)S(1)}, u32[]{:S(2)}, u32[]{:S(2)}) collective-permute-start(bf16[512,512]{1,0:T(8,128)(2,1)S(1)} %pad_maximum_fusion.1), channel_id=1, source_target_pairs={{0,2},{1,3},{2,4},{3,5},{4,6},{5,7},{6,0},{7,1},{8,10},{9,11},{10,... | collective-permute-start | bytes 1572872 | tf_op jit(solution)/shard_map/ppermute | solution.py:422
  35.4 2.8 %collective-permute-start.13 = (bf16[64,512]{1,0:T(8,128)(2,1)S(1)}, bf16[64,512]{1,0:T(8,128)(2,1)S(1)}, u32[]{:S(2)}, u32[]{:S(2)}) collective-permute-start(bf16[64,512]{1,0:T(8,128)(2,1)S(1)} %copy-done.13), channel_id=1, source_target_pairs={{192,128},{200,136},{208,144},{216,152},{224,160},{232,168},{240,1... | collective-permute-start | bytes 196616 | tf_op jit(solution)/shard_map/ppermute | solution.py:427
  50.6 11.2 %collective-permute-start.17 = (bf16[3,512,512]{2,1,0:T(8,128)(2,1)S(1)}, bf16[3,512,512]{2,1,0:T(8,128)(2,1)S(1)}, u32[]{:S(2)}, u32[]{:S(2)}) collective-permute-start(bf16[3,512,512]{2,1,0:T(8,128)(2,1)S(1)} %pad_maximum_fusion.refs_4_.refs_6_), channel_id=1, source_target_pairs={{0,1},{1,0},{2,3},{3,2},{4,5},{5,4},{6,7},{7,6},{8,9},{9,8},{10,11... | collective-permute-start | bytes 4718600 | tf_op jit(solution)/shard_map/ppermute | solution.py:438
  50.7 8.9 %collective-permute-start.16 = (bf16[256,512]{1,0:T(8,128)(2,1)S(1)}, bf16[256,512]{1,0:T(8,128)(2,1)S(1)}, u32[]{:S(2)}, u32[]{:S(2)}) collective-permute-start(bf16[256,512]{1,0:T(8,128)(2,1)S(1)} %slice.65), channel_id=1, source_target_pairs={{0,6},{1,7},{2,0},{3,1},{4,2},{5,3},{6,4},{7,5},{8,14},{9,15},{10,... | collective-permute-start | bytes 786440 | tf_op jit(solution)/shard_map/ppermute | solution.py:437
  53.4 8.4 %collective-permute-start.15 = (bf16[256,512]{1,0:T(8,128)(2,1)S(1)}, bf16[256,512]{1,0:T(8,128)(2,1)S(1)}, u32[]{:S(2)}, u32[]{:S(2)}) collective-permute-start(bf16[256,512]{1,0:T(8,128)(2,1)S(1)} %slice.64), channel_id=1, source_target_pairs={{0,2},{1,3},{2,4},{3,5},{4,6},{5,7},{6,0},{7,1},{8,10},{9,11},{10,... | collective-permute-start | bytes 786440 | tf_op jit(solution)/shard_map/ppermute | solution.py:436
  62.6 10.7 %collective-permute-start.18 = (bf16[512,512]{1,0:T(8,128)(2,1)}, bf16[512,512]{1,0:T(8,128)(2,1)}, u32[]{:S(2)}, u32[]{:S(2)}) collective-permute-start(bf16[512,512]{1,0:T(8,128)(2,1)} %hold.5.refs_5_.refs_7_), channel_id=1, source_target_pairs={{0,1},{1,0},{2,3},{3,2},{4,5},{5,4},{6,7},{7,6},{8,9},{9,8},{10,11... | collective-permute-start | bytes 1572872 | tf_op jit(solution)/shard_map/ppermute | solution.py:441
  66.9 5.8 %collective-permute-start.14 = (bf16[64,512]{1,0:T(8,128)(2,1)S(1)}, bf16[64,512]{1,0:T(8,128)(2,1)S(1)}, u32[]{:S(2)}, u32[]{:S(2)}) collective-permute-start(bf16[64,512]{1,0:T(8,128)(2,1)S(1)} %get-tuple-element.68.refs_0_), channel_id=1, source_target_pairs={{0,8},{64,72},{128,136},{192,200},{1,9},{65,73},{129,137},{193,201... | collective-permute-start | bytes 196616 | tf_op jit(solution)/shard_map/ppermute | solution.py:454
  72.7 4.8 %collective-permute-start.19 = (bf16[1,64,512]{2,1,0:T(8,128)(2,1)S(1)}, bf16[1,64,512]{2,1,0:T(8,128)(2,1)S(1)}, u32[]{:S(2)}, u32[]{:S(2)}) collective-permute-start(bf16[1,64,512]{2,1,0:T(8,128)(2,1)S(1)} %bitcast.21), channel_id=1, source_target_pairs={{8,16},{72,80},{136,144},{200,208},{40,48},{9,17},{73,81},{137,145... | collective-permute-start | bytes 196616 | tf_op jit(solution)/shard_map/ppermute | solution.py:453
  79.5 2.4 %collective-permute-start.21 = (bf16[2,64,512]{2,1,0:T(8,128)(2,1)S(1)}, bf16[2,64,512]{2,1,0:T(8,128)(2,1)S(1)}, u32[]{:S(2)}, u32[]{:S(2)}) collective-permute-start(bf16[2,64,512]{2,1,0:T(8,128)(2,1)S(1)} %append.5), channel_id=1, source_target_pairs={{16,24},{80,88},{144,152},{208,216},{48,56},{17,25},{81,89},{145,1... | collective-permute-start | bytes 393224 | tf_op jit(solution)/shard_map/ppermute | solution.py:453
  83.6 12.2 %collective-permute-start.23 = (bf16[3,64,512]{2,1,0:T(8,128)(2,1)S(1)}, bf16[3,64,512]{2,1,0:T(8,128)(2,1)S(1)}, u32[]{:S(2)}, u32[]{:S(2)}) collective-permute-start(bf16[3,64,512]{2,1,0:T(8,128)(2,1)S(1)} %append.6), channel_id=1, source_target_pairs={{24,32},{88,96},{152,160},{216,224},{56,0},{25,33},{89,97},{153,16... | collective-permute-start | bytes 589832 | tf_op jit(solution)/shard_map/ppermute | solution.py:453
  85.9 10.9 %collective-permute-start.24 = (bf16[64,512]{1,0:T(8,128)(2,1)S(1)}, bf16[64,512]{1,0:T(8,128)(2,1)S(1)}, u32[]{:S(2)}, u32[]{:S(2)}) collective-permute-start(bf16[64,512]{1,0:T(8,128)(2,1)S(1)} %step.9.refs_3_), channel_id=1, source_target_pairs={{24,32},{88,96},{152,160},{216,224},{25,33},{89,97},{153,161},{217... | collective-permute-start | bytes 196616 | tf_op jit(solution)/shard_map/ppermute | solution.py:454
  97.4 6.4 %collective-permute-start.25 = (bf16[4,64,512]{2,1,0:T(8,128)(2,1)S(1)}, bf16[4,64,512]{2,1,0:T(8,128)(2,1)S(1)}, u32[]{:S(2)}, u32[]{:S(2)}) collective-permute-start(bf16[4,64,512]{2,1,0:T(8,128)(2,1)S(1)} %append.7), channel_id=1, source_target_pairs={{32,40},{96,104},{160,168},{224,232},{0,8},{33,41},{97,105},{161,1... | collective-permute-start | bytes 786440 | tf_op jit(solution)/shard_map/ppermute | solution.py:453
  99.8 5.1 %collective-permute-start.26 = (bf16[64,512]{1,0:T(8,128)(2,1)S(1)}, bf16[64,512]{1,0:T(8,128)(2,1)S(1)}, u32[]{:S(2)}, u32[]{:S(2)}) collective-permute-start(bf16[64,512]{1,0:T(8,128)(2,1)S(1)} %step.10.refs_4_), channel_id=1, source_target_pairs={{32,40},{96,104},{160,168},{224,232},{33,41},{97,105},{161,169},{2... | collective-permute-start | bytes 196616 | tf_op jit(solution)/shard_map/ppermute | solution.py:454
  101.0 6.3 %collective-permute-start.27 = (bf16[64,512]{1,0:T(8,128)(2,1)S(1)}, bf16[64,512]{1,0:T(8,128)(2,1)S(1)}, u32[]{:S(2)}, u32[]{:S(2)}) collective-permute-start(bf16[64,512]{1,0:T(8,128)(2,1)S(1)} %own_row.2.refs_0_), channel_id=1, source_target_pairs={{8,0},{16,8},{24,16},{72,64},{80,72},{88,80},{136,128},{144,136},{... | collective-permute-start | bytes 196616 | tf_op jit(solution)/shard_map/ppermute | solution.py:468
  107.9 3.7 %collective-permute-start.28 = (bf16[5,64,512]{2,1,0:T(8,128)(2,1)S(1)}, bf16[5,64,512]{2,1,0:T(8,128)(2,1)S(1)}, u32[]{:S(2)}, u32[]{:S(2)}) collective-permute-start(bf16[5,64,512]{2,1,0:T(8,128)(2,1)S(1)} %append.8), channel_id=1, source_target_pairs={{40,48},{104,112},{168,176},{232,240},{8,16},{41,49},{105,113},{16... | collective-permute-start | bytes 983048 | tf_op jit(solution)/shard_map/ppermute | solution.py:453
  109.7 3.1 %collective-permute-start.29 = (bf16[64,512]{1,0:T(8,128)(2,1)S(1)}, bf16[64,512]{1,0:T(8,128)(2,1)S(1)}, u32[]{:S(2)}, u32[]{:S(2)}) collective-permute-start(bf16[64,512]{1,0:T(8,128)(2,1)S(1)} %step.11.refs_5_), channel_id=1, source_target_pairs={{40,48},{104,112},{168,176},{232,240},{41,49},{105,113},{169,177},... | collective-permute-start | bytes 196616 | tf_op jit(solution)/shard_map/ppermute | solution.py:454
  110.3 7.1 %collective-permute-start.30 = (bf16[64,512]{1,0:T(8,128)(2,1)S(1)}, bf16[64,512]{1,0:T(8,128)(2,1)S(1)}, u32[]{:S(2)}, u32[]{:S(2)}) collective-permute-start(bf16[64,512]{1,0:T(8,128)(2,1)S(1)} %collective-permute-done.27.refs_1_), channel_id=1, source_target_pairs={{8,0},{16,8},{24,16},{72,64},{80,72},{88,80},{136,128},{144,136},{... | collective-permute-start | bytes 196616 | tf_op jit(solution)/shard_map/ppermute | solution.py:468
  118.0 5.9 %collective-permute-start.31 = (bf16[6,64,512]{2,1,0:T(8,128)(2,1)S(1)}, bf16[6,64,512]{2,1,0:T(8,128)(2,1)S(1)}, u32[]{:S(2)}, u32[]{:S(2)}) collective-permute-start(bf16[6,64,512]{2,1,0:T(8,128)(2,1)S(1)} %append.9), channel_id=1, source_target_pairs={{48,56},{112,120},{176,184},{240,248},{16,24},{49,57},{113,121},{1... | collective-permute-start | bytes 1179656 | tf_op jit(solution)/shard_map/ppermute | solution.py:453
  119.9 5.2 %collective-permute-start.33 = (bf16[64,512]{1,0:T(8,128)(2,1)S(1)}, bf16[64,512]{1,0:T(8,128)(2,1)S(1)}, u32[]{:S(2)}, u32[]{:S(2)}) collective-permute-start(bf16[64,512]{1,0:T(8,128)(2,1)S(1)} %step.12.refs_6_), channel_id=1, source_target_pairs={{48,56},{112,120},{176,184},{240,248},{49,57},{113,121},{177,185},... | collective-permute-start | bytes 196616 | tf_op jit(solution)/shard_map/ppermute | solution.py:454
  120.5 6.2 %collective-permute-start.32 = (bf16[64,512]{1,0:T(8,128)(2,1)S(1)}, bf16[64,512]{1,0:T(8,128)(2,1)S(1)}, u32[]{:S(2)}, u32[]{:S(2)}) collective-permute-start(bf16[64,512]{1,0:T(8,128)(2,1)S(1)} %collective-permute-done.30.refs_2_), channel_id=1, source_target_pairs={{8,0},{16,8},{24,16},{72,64},{80,72},{88,80},{136,128},{144,136},{... | collective-permute-start | bytes 196616 | tf_op jit(solution)/shard_map/ppermute | solution.py:468
  121.8 35.6 %collective-permute-start.47 = (bf16[256,512]{1,0:T(8,128)(2,1)S(1)}, bf16[256,512]{1,0:T(8,128)(2,1)S(1)}, u32[]{:S(2)}, u32[]{:S(2)}) collective-permute-start(bf16[256,512]{1,0:T(8,128)(2,1)S(1)} %copy-done.12), channel_id=1, source_target_pairs={{0,2},{1,3},{2,4},{3,5},{4,6},{5,7},{6,0},{7,1},{8,10},{9,11},{10,... | collective-permute-start | bytes 786440 | tf_op jit(solution)/shard_map/ppermute | solution.py:461
  122.2 35.3 %collective-permute-start.48 = (bf16[256,512]{1,0:T(8,128)(2,1)S(1)}, bf16[256,512]{1,0:T(8,128)(2,1)S(1)}, u32[]{:S(2)}, u32[]{:S(2)}) collective-permute-start(bf16[256,512]{1,0:T(8,128)(2,1)S(1)} %copy-done.11), channel_id=1, source_target_pairs={{0,6},{1,7},{2,0},{3,1},{4,2},{5,3},{6,4},{7,5},{8,14},{9,15},{10,... | collective-permute-start | bytes 786440 | tf_op jit(solution)/shard_map/ppermute | solution.py:462
  129.1 2.3 %collective-permute-start.40 = (bf16[64,512]{1,0:T(8,128)(2,1)S(1)}, bf16[64,512]{1,0:T(8,128)(2,1)S(1)}, u32[]{:S(2)}, u32[]{:S(2)}) collective-permute-start(bf16[64,512]{1,0:T(8,128)(2,1)S(1)} %own_row.3.refs_7_), channel_id=1, source_target_pairs={{32,24},{40,32},{48,40},{56,48},{96,88},{104,96},{112,104},{120,11... | collective-permute-start | bytes 196616 | tf_op jit(solution)/shard_map/ppermute | solution.py:485
  129.9 2.8 %collective-permute-start.39 = (bf16[64,512]{1,0:T(8,128)(2,1)S(1)}, bf16[64,512]{1,0:T(8,128)(2,1)S(1)}, u32[]{:S(2)}, u32[]{:S(2)}) collective-permute-start(bf16[64,512]{1,0:T(8,128)(2,1)S(1)} %own_row.3.refs_7_), channel_id=1, source_target_pairs={{32,16},{40,24},{48,32},{56,40},{96,80},{104,88},{112,96},{120,104... | collective-permute-start | bytes 196616 | tf_op jit(solution)/shard_map/ppermute | solution.py:485
  130.7 3.3 %collective-permute-start.38 = (bf16[64,512]{1,0:T(8,128)(2,1)S(1)}, bf16[64,512]{1,0:T(8,128)(2,1)S(1)}, u32[]{:S(2)}, u32[]{:S(2)}) collective-permute-start(bf16[64,512]{1,0:T(8,128)(2,1)S(1)} %own_row.3.refs_7_), channel_id=1, source_target_pairs={{32,8},{40,16},{48,24},{56,32},{96,72},{104,80},{112,88},{120,96},... | collective-permute-start | bytes 196616 | tf_op jit(solution)/shard_map/ppermute | solution.py:485
  131.4 15.4 %collective-permute-start.37 = (bf16[64,512]{1,0:T(8,128)(2,1)S(1)}, bf16[64,512]{1,0:T(8,128)(2,1)S(1)}, u32[]{:S(2)}, u32[]{:S(2)}) collective-permute-start(bf16[64,512]{1,0:T(8,128)(2,1)S(1)} %own_row.3.refs_7_), channel_id=1, source_target_pairs={{56,0},{120,64},{184,128},{248,192},{57,1},{121,65},{185,129},{249... | collective-permute-start | bytes 196616 | tf_op jit(solution)/shard_map/ppermute | solution.py:485
  132.7 15.3 %collective-permute-start.36 = (bf16[64,512]{1,0:T(8,128)(2,1)S(1)}, bf16[64,512]{1,0:T(8,128)(2,1)S(1)}, u32[]{:S(2)}, u32[]{:S(2)}) collective-permute-start(bf16[64,512]{1,0:T(8,128)(2,1)S(1)} %own_row.3.refs_7_), channel_id=1, source_target_pairs={{48,0},{56,8},{112,64},{120,72},{176,128},{184,136},{240,192},{248... | collective-permute-start | bytes 196616 | tf_op jit(solution)/shard_map/ppermute | solution.py:485
  134.0 16.0 %collective-permute-start.35 = (bf16[64,512]{1,0:T(8,128)(2,1)S(1)}, bf16[64,512]{1,0:T(8,128)(2,1)S(1)}, u32[]{:S(2)}, u32[]{:S(2)}) collective-permute-start(bf16[64,512]{1,0:T(8,128)(2,1)S(1)} %own_row.3.refs_7_), channel_id=1, source_target_pairs={{40,0},{48,8},{56,16},{104,64},{112,72},{120,80},{168,128},{176,13... | collective-permute-start | bytes 196616 | tf_op jit(solution)/shard_map/ppermute | solution.py:485
  146.8 10.1 %collective-permute-start.34 = (bf16[64,512]{1,0:T(8,128)(2,1)S(1)}, bf16[64,512]{1,0:T(8,128)(2,1)S(1)}, u32[]{:S(2)}, u32[]{:S(2)}) collective-permute-start(bf16[64,512]{1,0:T(8,128)(2,1)S(1)} %own_row.3.refs_7_), channel_id=1, source_target_pairs={{32,0},{40,8},{48,16},{56,24},{96,64},{104,72},{112,80},{120,88},{... | collective-permute-start | bytes 196616 | tf_op jit(solution)/shard_map/ppermute | solution.py:485
  148.1 9.5 %collective-permute-start.42 = (bf16[4,64,512]{2,1,0:T(8,128)(2,1)S(1)}, bf16[4,64,512]{2,1,0:T(8,128)(2,1)S(1)}, u32[]{:S(2)}, u32[]{:S(2)}) collective-permute-start(bf16[4,64,512]{2,1,0:T(8,128)(2,1)S(1)} %collect.2.refs_1_), channel_id=1, source_target_pairs={{0,192},{8,200},{16,208},{24,216},{32,224},{40,232},{48,240},{56,2... | collective-permute-start | bytes 786440 | tf_op jit(solution)/shard_map/ppermute | solution.py:476
  150.0 7.6 %collective-permute-start.41 = (bf16[4,64,512]{2,1,0:T(8,128)(2,1)S(1)}, bf16[4,64,512]{2,1,0:T(8,128)(2,1)S(1)}, u32[]{:S(2)}, u32[]{:S(2)}) collective-permute-start(bf16[4,64,512]{2,1,0:T(8,128)(2,1)S(1)} %collect.2.refs_1_), channel_id=1, source_target_pairs={{0,64},{8,72},{16,80},{24,88},{32,96},{40,104},{48,112},{56,120},{... | collective-permute-start | bytes 786440 | tf_op jit(solution)/shard_map/ppermute | solution.py:475
  157.5 19.3 %collective-permute-start.49 = (bf16[512,512]{1,0:T(8,128)(2,1)S(1)}, bf16[512,512]{1,0:T(8,128)(2,1)S(1)}, u32[]{:S(2)}, u32[]{:S(2)}) collective-permute-start(bf16[512,512]{1,0:T(8,128)(2,1)S(1)} %hold.7.refs_11_), channel_id=1, source_target_pairs={{0,1},{1,0},{2,3},{3,2},{4,5},{5,4},{6,7},{7,6},{8,9},{9,8},{10,11... | collective-permute-start | bytes 1572872 | tf_op jit(solution)/shard_map/ppermute | solution.py:488
  157.7 15.5 %collective-permute-start.44 = (bf16[4,64,512]{2,1,0:T(8,128)(2,1)S(1)}, bf16[4,64,512]{2,1,0:T(8,128)(2,1)S(1)}, u32[]{:S(2)}, u32[]{:S(2)}) collective-permute-start(bf16[4,64,512]{2,1,0:T(8,128)(2,1)S(1)} %collect.3.refs_1_), channel_id=1, source_target_pairs={{0,64},{8,72},{16,80},{24,88},{32,96},{40,104},{48,112},{56,120},{... | collective-permute-start | bytes 786440 | tf_op jit(solution)/shard_map/ppermute | solution.py:289
  157.7 15.5 %collective-permute-start.43 = (bf16[4,64,512]{2,1,0:T(8,128)(2,1)S(1)}, bf16[4,64,512]{2,1,0:T(8,128)(2,1)S(1)}, u32[]{:S(2)}, u32[]{:S(2)}) collective-permute-start(bf16[4,64,512]{2,1,0:T(8,128)(2,1)S(1)} %collect.3.refs_1_), channel_id=1, source_target_pairs={{0,192},{8,200},{16,208},{24,216},{32,224},{40,232},{48,240},{56,2... | collective-permute-start | bytes 786440 | tf_op jit(solution)/shard_map/ppermute | solution.py:290
  161.0 15.9 %collective-permute-start.50 = (bf16[4,64,512]{2,1,0:T(8,128)(2,1)S(1)}, bf16[4,64,512]{2,1,0:T(8,128)(2,1)S(1)}, u32[]{:S(2)}, u32[]{:S(2)}) collective-permute-start(bf16[4,64,512]{2,1,0:T(8,128)(2,1)S(1)} %collect.2.refs_1_), channel_id=1, source_target_pairs={{0,128},{8,136},{16,144},{24,152},{32,160},{40,168},{48,176},{56,1... | collective-permute-start | bytes 786440 | tf_op jit(solution)/shard_map/ppermute | solution.py:477
  173.2 8.6 %collective-permute-start.45 = (bf16[2,64,512]{2,1,0:T(8,128)(2,1)S(1)}, bf16[2,64,512]{2,1,0:T(8,128)(2,1)S(1)}, u32[]{:S(2)}, u32[]{:S(2)}) collective-permute-start(bf16[2,64,512]{2,1,0:T(8,128)(2,1)S(1)} %slice.73), channel_id=1, source_target_pairs={{0,64},{8,72},{16,80},{24,88},{32,96},{40,104},{48,112},{56,120},{... | collective-permute-start | bytes 393224 | tf_op jit(solution)/shard_map/ppermute | solution.py:291
  173.3 8.5 %collective-permute-start.46 = (bf16[2,64,512]{2,1,0:T(8,128)(2,1)S(1)}, bf16[2,64,512]{2,1,0:T(8,128)(2,1)S(1)}, u32[]{:S(2)}, u32[]{:S(2)}) collective-permute-start(bf16[2,64,512]{2,1,0:T(8,128)(2,1)S(1)} %slice.74), channel_id=1, source_target_pairs={{0,192},{8,200},{16,208},{24,216},{32,224},{40,232},{48,240},{56,2... | collective-permute-start | bytes 393224 | tf_op jit(solution)/shard_map/ppermute | solution.py:292
  (17 other events, 219.9 us)

commit v4 on v3

--- a/solution.py
+++ b/solution.py
@@ -427,8 +427,8 @@
     zr = [lax.ppermute(ready[i], "row", from_plane(3, i)) for i in range(NY - 1)]
     near1 = hold([after(panel1, zr[0]), left1, right1], stack=True)
     near_other1 = lax.ppermute(near1, "col", SWAP)
-    left, right, near_other1, left1, right1, *zr = lax.optimization_barrier(
-        (left, right, near_other1, left1[:half], right1[half:], *zr)
+    left, right, near_other1, left1, right1, sc, *zr = lax.optimization_barrier(
+        (left, right, near_other1, left1[:half], right1[half:], sc, *zr)
     )
     base = by_plane(*zr, zq[3])
     far_a, far_b = left[:half], right[half:]
@@ -437,9 +437,11 @@
     far_b = lax.ppermute(far_b, "col", shift_x(-1))
     near_other = lax.ppermute(near, "col", SWAP)
     far_a, far_b, near_other = lax.optimization_barrier((far_a, far_b, near_other))
-    far = hold([far_a, far_b])
-    far_other = hold([lax.ppermute(far, "col", SWAP)])
-    blocks0 = [near, far, near_other, far_other]
+    far = jnp.concatenate([far_a, far_b])
+    far_other = lax.ppermute(far, "col", SWAP)
+    far_kept = hold([far_a, far_b])
+    far_other = hold([after(far_other, far_kept)])
+    blocks0 = [near, far_kept, near_other, far_other]
 
     fresh, inv = first(base, inverse)
     solved = [fresh]

time: 190 us -> 181 us (0.953); the launches traced: 187 us -> 180 us
  Pallas kernels: 31.9 us -> 22.2 us
  starting transfers between devices: 55.8 us -> 64.8 us
  waiting for transfers between devices: 85.3 us -> 79.1 us
  other arithmetic: 2.32 us -> 4.75 us
  local copies, waits for them, and re-layouts: 10.2 us -> 7.83 us
    ppermute x1, waiting for transfers between devices: 11.8 us -> 5.2 us  [spread_y(): before = lax.ppermute(rows, 'row', shift_y(1))]
    unnamed x29 -> x11, local copies, waits for them, and re-layouts: 5.68 us -> 0.95 us
    ppermute x1, starting transfers between devices: 0.08 us -> 4.56 us  [spread_y(): far_a = lax.ppermute(before[:half], 'row', shift_y(1))]
    pallas_call x7, Pallas kernels: 7.72 us -> 3.86 us  [step(): pl.pallas_call(lambda *refs: step_kernel(t, *refs), out_shape=jax.ShapeDt...]
    pallas_call x6, Pallas kernels: 6.41 us -> 3.35 us  [early(): pl.pallas_call(lambda *refs: early_kernel(t, *refs), out_shape=(jax.Shape...]
    ppermute x6, waiting for transfers between devices: 10.4 us -> 12.8 us  [on_device(): sent = lax.ppermute(known, 'row', hop_z_early(t))]
    slice x2, local copies, waits for them, and re-layouts: 0.04 us -> 1.94 us  [on_device(): far_a, far_b = (left[:half], right[half:])]
  transfers between devices with their start and end apart: 51 -> 51, of which waited for: 18 -> 18; matrix products, arithmetic and copies ran while one was open for 3% -> 4% of each run, Pallas kernels for 12% -> 8%
where the time goes in v4:
time: 181 us; the launch traced here: 180 us
  waiting for transfers between devices  79.1 us (44%)
  starting transfers between devices  64.8 us (36%)
  Pallas kernels  22.2 us (12%)
  local copies, waits for them, and re-layouts  7.83 us (4%)
  other arithmetic  4.75 us (3%)
    ppermute x7, waiting for transfers between devices, on_device(): lax.ppermute(own_s, 'row', back_z(d, range(4, 8)))  18.1 us
    ppermute x6, waiting for transfers between devices, on_device(): sent = lax.ppermute(known, 'row', hop_z_early(t))  12.8 us
    ppermute x3, waiting for transfers between devices, on_device(): lax.ppermute((back_a or [own_s])[-1], 'row', back_z(1, range(1, 4)))  10.5 us
    pallas_call x2, Pallas kernels, final(): pl.pallas_call(lambda *refs: final_kernel(start, *refs), out_shape=(jax.S...  9.2 us
    ppermute x1, waiting for transfers between devices, on_device(): right = lax.ppermute(window, 'col', shift_x(-1))  7.9 us
    ppermute x7, starting transfers between devices, on_device(): last = lax.ppermute(fresh, 'row', hop_z(t))  7.44 us
    ppermute x7, starting transfers between devices, on_device(): lax.ppermute(own_s, 'row', back_z(d, range(4, 8)))  7.28 us
    ppermute x1, waiting for transfers between devices, on_device(): right1 = lax.ppermute(panel1, 'col', shift_x(-1))  6.63 us
  transfers between devices with their start and end apart: 51, of which 18 were waited for; matrix products, arithmetic and copies ran while one was open for 4% of the time, Pallas kernels for 8%

profile of v4, /device:TPU:2, one launch (start us, length us, event | category | flops | bytes accessed | tf_op | source)
XLA Modules:
  0.0 180.0 jit_solution(12624504701263414831)
XLA Ops:
  1.8 1.3 collective-permute-start
  3.1 1.4 collective-permute-start.4
  4.5 4.3 %collective-permute-start.1 = (bf16[256,512]{1,0:T(8,128)(2,1)S(1)}, bf16[256,512]{1,0:T(8,128)(2,1)}, u32[]{:S(2)}, u32[]{:S(2)}) collective-permute-start(bf16[256,512]{1,0:T(8,128)(2,1)S(1)} %get-tuple-element.122), channel_id=1, source_target_pairs={{192,128},{200,136},{208,144},{216,152},{224,160},{232,168},{240,1... | collective-permute-start | bytes 786440 | tf_op jit(solution)/shard_map/ppermute | solution.py:404
  8.7 1.3 collective-permute-start.3
  11.9 1.2 collective-permute-done
  13.1 1.3 collective-permute-start.10
  14.3 2.3 %collective-permute-start.2 = (bf16[256,512]{1,0:T(8,128)(2,1)}, bf16[256,512]{1,0:T(8,128)(2,1)}, u32[]{:S(2)}, u32[]{:S(2)}) collective-permute-start(bf16[256,512]{1,0:T(8,128)(2,1)} %collective-permute-done), channel_id=1, source_target_pairs={{0,64},{8,72},{16,80},{24,88},{32,96},{40,104},{48,112},{56,120},{... | collective-permute-start | bytes 786440 | tf_op jit(solution)/shard_map/ppermute | solution.py:405
  16.7 1.4 collective-permute-start.5
  18.7 2.3 %collective-permute-done.10 = bf16[64,512]{1,0:T(8,128)(2,1)S(1)} collective-permute-done((bf16[64,512]{1,0:T(8,128)(2,1)S(1)}, bf16[64,512]{1,0:T(8,128)(2,1)S(1)}, u32[]{:S(2)}, u32[]{:S(2)}) %collective-permute-start.10) | collective-permute-done | bytes 65568 | tf_op jit(solution)/shard_map/ppermute | solution.py:427
  21.0 1.5 collective-permute-start.6
  22.5 1.3 select_select_fusion.1
  24.6 6.6 %collective-permute-done.7.refs_2_ = bf16[512,512]{1,0:T(8,128)(2,1)S(1)} collective-permute-done((bf16[512,512]{1,0:T(8,128)(2,1)S(1)}, bf16[512,512]{1,0:T(8,128)(2,1)S(1)}, u32[]{:S(2)}, u32[]{:S(2)}) %collective-permute-start.7) | collective-permute-done | bytes 524320 | tf_op jit(solution)/shard_map/ppermute | solution.py:419
  31.3 2.4 %collective-permute-done.6.refs_1_ = bf16[512,512]{1,0:T(8,128)(2,1)S(1)} collective-permute-done((bf16[512,512]{1,0:T(8,128)(2,1)S(1)}, bf16[512,512]{1,0:T(8,128)(2,1)S(1)}, u32[]{:S(2)}, u32[]{:S(2)}) %collective-permute-start.6) | collective-permute-done | bytes 524320 | tf_op jit(solution)/shard_map/ppermute | solution.py:418
  34.6 1.9 %collective-permute-start.9 = (bf16[512,512]{1,0:T(8,128)(2,1)}, bf16[512,512]{1,0:T(8,128)(2,1)}, u32[]{:S(2)}, u32[]{:S(2)}) collective-permute-start(bf16[512,512]{1,0:T(8,128)(2,1)} %pad_maximum_fusion.1), channel_id=1, source_target_pairs={{0,6},{1,7},{2,0},{3,1},{4,2},{5,3},{6,4},{7,5},{8,14},{9,15},{10,... | collective-permute-start | bytes 1572872 | tf_op jit(solution)/shard_map/ppermute | solution.py:423
  36.7 1.3 collective-permute-start.13
  38.0 1.3 collective-permute-start.12
  41.4 7.9 %collective-permute-done.9 = bf16[512,512]{1,0:T(8,128)(2,1)} collective-permute-done((bf16[512,512]{1,0:T(8,128)(2,1)}, bf16[512,512]{1,0:T(8,128)(2,1)}, u32[]{:S(2)}, u32[]{:S(2)}) %collective-permute-start.9) | collective-permute-done | bytes 524320 | tf_op jit(solution)/shard_map/ppermute | solution.py:423
  49.3 1.6 collective-permute-done.8
  52.8 1.7 pad_maximum_fusion.refs_4_.refs_6_
  54.6 2.7 %collective-permute-start.16 = (bf16[256,512]{1,0:T(8,128)(2,1)S(1)}, bf16[256,512]{1,0:T(8,128)(2,1)S(1)}, u32[]{:S(2)}, u32[]{:S(2)}) collective-permute-start(bf16[256,512]{1,0:T(8,128)(2,1)S(1)} %slice.65), channel_id=1, source_target_pairs={{0,6},{1,7},{2,0},{3,1},{4,2},{5,3},{6,4},{7,5},{8,14},{9,15},{10,... | collective-permute-start | bytes 786440 | tf_op jit(solution)/shard_map/ppermute | solution.py:437
  57.3 6.1 %collective-permute-done.16.refs_1_ = bf16[256,512]{1,0:T(8,128)(2,1)S(1)} collective-permute-done((bf16[256,512]{1,0:T(8,128)(2,1)S(1)}, bf16[256,512]{1,0:T(8,128)(2,1)S(1)}, u32[]{:S(2)}, u32[]{:S(2)}) %collective-permute-start.16) | collective-permute-done | bytes 262176 | tf_op jit(solution)/shard_map/ppermute | solution.py:437
  63.5 2.2 %collective-permute-done.15.refs_0_ = bf16[256,512]{1,0:T(8,128)(2,1)S(1)} collective-permute-done((bf16[256,512]{1,0:T(8,128)(2,1)S(1)}, bf16[256,512]{1,0:T(8,128)(2,1)S(1)}, u32[]{:S(2)}, u32[]{:S(2)}) %collective-permute-start.15) | collective-permute-done | bytes 262176 | tf_op jit(solution)/shard_map/ppermute | solution.py:436
  67.1 3.5 %collective-permute-start.14 = (bf16[64,512]{1,0:T(8,128)(2,1)S(1)}, bf16[64,512]{1,0:T(8,128)(2,1)S(1)}, u32[]{:S(2)}, u32[]{:S(2)}) collective-permute-start(bf16[64,512]{1,0:T(8,128)(2,1)S(1)} %get-tuple-element.71.refs_0_), channel_id=1, source_target_pairs={{0,8},{64,72},{128,136},{192,200},{1,9},{65,73},{129,137},{193,201... | collective-permute-start | bytes 196616 | tf_op jit(solution)/shard_map/ppermute | solution.py:456
  70.5 2.0 %collective-permute-done.14.refs_2_.refs_4_ = bf16[64,512]{1,0:T(8,128)(2,1)S(1)} collective-permute-done((bf16[64,512]{1,0:T(8,128)(2,1)S(1)}, bf16[64,512]{1,0:T(8,128)(2,1)S(1)}, u32[]{:S(2)}, u32[]{:S(2)}) %collective-permute-start.14) | collective-permute-done | bytes 65568 | tf_op jit(solution)/shard_map/ppermute | solution.py:456
  78.7 1.3 collective-permute-start.23
  81.2 11.6 %collective-permute-done.23.refs_2_.known.refs_9_ = bf16[3,64,512]{2,1,0:T(8,128)(2,1)S(1)} collective-permute-done((bf16[3,64,512]{2,1,0:T(8,128)(2,1)S(1)}, bf16[3,64,512]{2,1,0:T(8,128)(2,1)S(1)}, u32[]{:S(2)}, u32[]{:S(2)}) %collective-permute-start.23) | collective-permute-done | bytes 196640 | tf_op jit(solution)/shard_map/ppermute | solution.py:455
  94.0 1.3 collective-permute-start.25
  97.1 1.5 collective-permute-start.27
  100.3 3.1 %collective-permute-done.27.refs_1_ = bf16[64,512]{1,0:T(8,128)(2,1)S(1)} collective-permute-done((bf16[64,512]{1,0:T(8,128)(2,1)S(1)}, bf16[64,512]{1,0:T(8,128)(2,1)S(1)}, u32[]{:S(2)}, u32[]{:S(2)}) %collective-permute-start.27) | collective-permute-done | bytes 65568 | tf_op jit(solution)/shard_map/ppermute | solution.py:470
  105.9 1.3 collective-permute-start.30
  107.8 5.2 %collective-permute-done.30.refs_2_ = bf16[64,512]{1,0:T(8,128)(2,1)S(1)} collective-permute-done((bf16[64,512]{1,0:T(8,128)(2,1)S(1)}, bf16[64,512]{1,0:T(8,128)(2,1)S(1)}, u32[]{:S(2)}, u32[]{:S(2)}) %collective-permute-start.30) | collective-permute-done | bytes 65568 | tf_op jit(solution)/shard_map/ppermute | solution.py:470
  115.5 1.3 collective-permute-start.32
  117.1 1.7 collective-permute-start.48
  119.4 2.2 %collective-permute-done.32.refs_3_ = bf16[64,512]{1,0:T(8,128)(2,1)S(1)} collective-permute-done((bf16[64,512]{1,0:T(8,128)(2,1)S(1)}, bf16[64,512]{1,0:T(8,128)(2,1)S(1)}, u32[]{:S(2)}, u32[]{:S(2)}) %collective-permute-start.32) | collective-permute-done | bytes 65568 | tf_op jit(solution)/shard_map/ppermute | solution.py:470
  125.6 1.3 collective-permute-start.37
  126.9 1.3 collective-permute-start.36
  128.2 1.3 collective-permute-start.35
  129.5 11.6 %collective-permute-done.37.refs_3_ = bf16[64,512]{1,0:T(8,128)(2,1)S(1)} collective-permute-done((bf16[64,512]{1,0:T(8,128)(2,1)S(1)}, bf16[64,512]{1,0:T(8,128)(2,1)S(1)}, u32[]{:S(2)}, u32[]{:S(2)}) %collective-permute-start.37) | collective-permute-done | bytes 65568 | tf_op jit(solution)/shard_map/ppermute | solution.py:487
  141.1 1.3 collective-permute-start.34
  142.4 2.2 %collective-permute-start.42 = (bf16[4,64,512]{2,1,0:T(8,128)(2,1)S(1)}, bf16[4,64,512]{2,1,0:T(8,128)(2,1)S(1)}, u32[]{:S(2)}, u32[]{:S(2)}) collective-permute-start(bf16[4,64,512]{2,1,0:T(8,128)(2,1)S(1)} %collect.2.refs_1_), channel_id=1, source_target_pairs={{0,192},{8,200},{16,208},{24,216},{32,224},{40,232},{48,240},{56,2... | collective-permute-start | bytes 786440 | tf_op jit(solution)/shard_map/ppermute | solution.py:478
  144.5 6.6 %collective-permute-done.34.refs_0_ = bf16[64,512]{1,0:T(8,128)(2,1)S(1)} collective-permute-done((bf16[64,512]{1,0:T(8,128)(2,1)S(1)}, bf16[64,512]{1,0:T(8,128)(2,1)S(1)}, u32[]{:S(2)}, u32[]{:S(2)}) %collective-permute-start.34) | collective-permute-done | bytes 65568 | tf_op jit(solution)/shard_map/ppermute | solution.py:487
  152.1 3.2 %collective-permute-start.43 = (bf16[4,64,512]{2,1,0:T(8,128)(2,1)S(1)}, bf16[4,64,512]{2,1,0:T(8,128)(2,1)S(1)}, u32[]{:S(2)}, u32[]{:S(2)}) collective-permute-start(bf16[4,64,512]{2,1,0:T(8,128)(2,1)S(1)} %collect.3.refs_1_), channel_id=1, source_target_pairs={{0,192},{8,200},{16,208},{24,216},{32,224},{40,232},{48,240},{56,2... | collective-permute-start | bytes 786440 | tf_op jit(solution)/shard_map/ppermute | solution.py:290
  155.4 1.6 collective-permute-start.50
  157.0 5.2 %collective-permute-done.44.refs_5_ = bf16[4,64,512]{2,1,0:T(8,128)(2,1)S(1)} collective-permute-done((bf16[4,64,512]{2,1,0:T(8,128)(2,1)S(1)}, bf16[4,64,512]{2,1,0:T(8,128)(2,1)S(1)}, u32[]{:S(2)}, u32[]{:S(2)}) %collective-permute-start.44) | collective-permute-done | bytes 262176 | tf_op jit(solution)/shard_map/ppermute | solution.py:289
  162.2 4.6 %collective-permute-start.45 = (bf16[2,64,512]{2,1,0:T(8,128)(2,1)S(1)}, bf16[2,64,512]{2,1,0:T(8,128)(2,1)S(1)}, u32[]{:S(2)}, u32[]{:S(2)}) collective-permute-start(bf16[2,64,512]{2,1,0:T(8,128)(2,1)S(1)} %slice.73), channel_id=1, source_target_pairs={{0,64},{8,72},{16,80},{24,88},{32,96},{40,104},{48,112},{56,120},{... | collective-permute-start | bytes 393224 | tf_op jit(solution)/shard_map/ppermute | solution.py:291
  166.8 4.0 %collective-permute-start.46 = (bf16[2,64,512]{2,1,0:T(8,128)(2,1)S(1)}, bf16[2,64,512]{2,1,0:T(8,128)(2,1)S(1)}, u32[]{:S(2)}, u32[]{:S(2)}) collective-permute-start(bf16[2,64,512]{2,1,0:T(8,128)(2,1)S(1)} %slice.74), channel_id=1, source_target_pairs={{0,192},{8,200},{16,208},{24,216},{32,224},{40,232},{48,240},{56,2... | collective-permute-start | bytes 393224 | tf_op jit(solution)/shard_map/ppermute | solution.py:292
  170.8 4.4 %final.2 = (f32[8,512,256]{2,1,0:T(8,128)}, f32[2,1,512,256]{3,2,1,0:T(8,128)S(1)}) custom-call(s32[22]{0:T(128)S(1)} %concatenate.10.refs_0_.sc, bf16[4,64,512]{2,1,0:T(8,128)(2,1)S(1)} %collect.2.refs_1_, bf16[4,64,512]{2,1,0:T(8,128)(2,1)S(1)} %collective-permute-done.42.refs_2_, bf16[4,64,512]{2,1,0:T(8,128)(2,1)S(1)} %collective-permute-done.50.refs_3_.refs_4_, ...), custom_call_target="tpu_custom_call" | custom-call | flops 1610612736 | bytes 2097152 | tf_op jit(solution)/shard_map/final/pallas_call | solution.py:355
  175.2 4.8 %final.3 = (f32[8,512,256]{2,1,0:T(8,128)}, f32[2,1,512,256]{3,2,1,0:T(8,128)}) custom-call(s32[22]{0:T(128)S(1)} %concatenate.10.refs_0_.sc, bf16[4,64,512]{2,1,0:T(8,128)(2,1)S(1)} %collect.3.refs_1_, bf16[4,64,512]{2,1,0:T(8,128)(2,1)S(1)} %collective-permute-done.43.refs_2_, ...), custom_call_target="tpu_custom_call", output_to_operand_aliasing={{0}: (15, {})} | custom-call | flops 1610612736 | bytes 2097152 | tf_op jit(solution)/shard_map/final/pallas_call | solution.py:355
  (112 shorter events, 34.3 us)
Async XLA Ops:
  1.8 11.3 %collective-permute-start = (bf16[256,512]{1,0:T(8,128)(2,1)S(1)}, bf16[256,512]{1,0:T(8,128)(2,1)}, u32[]{:S(2)}, u32[]{:S(2)}) collective-permute-start(bf16[256,512]{1,0:T(8,128)(2,1)S(1)} %get-tuple-element.122), channel_id=1, source_target_pairs={{192,0},{200,8},{208,16},{216,24},{224,32},{232,40},{240,48},{248,... | collective-permute-start | bytes 786440 | tf_op jit(solution)/shard_map/ppermute | solution.py:401
  3.1 13.6 %collective-permute-start.4 = (bf16[256,512]{1,0:T(8,128)(2,1)S(1)}, bf16[256,512]{1,0:T(8,128)(2,1)}, u32[]{:S(2)}, u32[]{:S(2)}) collective-permute-start(bf16[256,512]{1,0:T(8,128)(2,1)S(1)} %get-tuple-element.123), channel_id=1, source_target_pairs={{192,128},{200,136},{208,144},{216,152},{224,160},{232,168},{240,1... | collective-permute-start | bytes 786440 | tf_op jit(solution)/shard_map/ppermute | solution.py:402
  4.5 13.6 %collective-permute-start.1 = (bf16[256,512]{1,0:T(8,128)(2,1)S(1)}, bf16[256,512]{1,0:T(8,128)(2,1)}, u32[]{:S(2)}, u32[]{:S(2)}) collective-permute-start(bf16[256,512]{1,0:T(8,128)(2,1)S(1)} %get-tuple-element.122), channel_id=1, source_target_pairs={{192,128},{200,136},{208,144},{216,152},{224,160},{232,168},{240,1... | collective-permute-start | bytes 786440 | tf_op jit(solution)/shard_map/ppermute | solution.py:404
  8.7 13.8 %collective-permute-start.3 = (bf16[256,512]{1,0:T(8,128)(2,1)S(1)}, bf16[256,512]{1,0:T(8,128)(2,1)}, u32[]{:S(2)}, u32[]{:S(2)}) collective-permute-start(bf16[256,512]{1,0:T(8,128)(2,1)S(1)} %get-tuple-element.123), channel_id=1, source_target_pairs={{192,0},{200,8},{208,16},{216,24},{224,32},{232,40},{240,48},{248,... | collective-permute-start | bytes 786440 | tf_op jit(solution)/shard_map/ppermute | solution.py:403
  13.1 7.9 %collective-permute-start.10 = (bf16[64,512]{1,0:T(8,128)(2,1)S(1)}, bf16[64,512]{1,0:T(8,128)(2,1)S(1)}, u32[]{:S(2)}, u32[]{:S(2)}) collective-permute-start(bf16[64,512]{1,0:T(8,128)(2,1)S(1)} %get-tuple-element.61), channel_id=1, source_target_pairs={{192,0},{200,8},{208,16},{216,24},{224,32},{232,40},{240,48},{248,... | collective-permute-start | bytes 196616 | tf_op jit(solution)/shard_map/ppermute | solution.py:427
  14.3 8.1 %collective-permute-start.2 = (bf16[256,512]{1,0:T(8,128)(2,1)}, bf16[256,512]{1,0:T(8,128)(2,1)}, u32[]{:S(2)}, u32[]{:S(2)}) collective-permute-start(bf16[256,512]{1,0:T(8,128)(2,1)} %collective-permute-done), channel_id=1, source_target_pairs={{0,64},{8,72},{16,80},{24,88},{32,96},{40,104},{48,112},{56,120},{... | collective-permute-start | bytes 786440 | tf_op jit(solution)/shard_map/ppermute | solution.py:405
  16.7 5.8 %collective-permute-start.5 = (bf16[256,512]{1,0:T(8,128)(2,1)}, bf16[256,512]{1,0:T(8,128)(2,1)}, u32[]{:S(2)}, u32[]{:S(2)}) collective-permute-start(bf16[256,512]{1,0:T(8,128)(2,1)} %collective-permute-done.4), channel_id=1, source_target_pairs={{128,64},{136,72},{144,80},{152,88},{160,96},{168,104},{176,112},{... | collective-permute-start | bytes 786440 | tf_op jit(solution)/shard_map/ppermute | solution.py:406
  18.1 13.2 %collective-permute-start.7 = (bf16[512,512]{1,0:T(8,128)(2,1)S(1)}, bf16[512,512]{1,0:T(8,128)(2,1)S(1)}, u32[]{:S(2)}, u32[]{:S(2)}) collective-permute-start(bf16[512,512]{1,0:T(8,128)(2,1)S(1)} %slice_bitcast_fusion.refs_0_), channel_id=1, source_target_pairs={{0,6},{1,7},{2,0},{3,1},{4,2},{5,3},{6,4},{7,5},{8,14},{9,15},{10,... | collective-permute-start | bytes 1572872 | tf_op jit(solution)/shard_map/ppermute | solution.py:419
  21.0 12.6 %collective-permute-start.6 = (bf16[512,512]{1,0:T(8,128)(2,1)S(1)}, bf16[512,512]{1,0:T(8,128)(2,1)S(1)}, u32[]{:S(2)}, u32[]{:S(2)}) collective-permute-start(bf16[512,512]{1,0:T(8,128)(2,1)S(1)} %slice_bitcast_fusion.refs_0_), channel_id=1, source_target_pairs={{0,2},{1,3},{2,4},{3,5},{4,6},{5,7},{6,0},{7,1},{8,10},{9,11},{10,... | collective-permute-start | bytes 1572872 | tf_op jit(solution)/shard_map/ppermute | solution.py:418
  34.5 16.3 %collective-permute-start.11 = (bf16[3,512,512]{2,1,0:T(8,128)(2,1)S(1)}, bf16[3,512,512]{2,1,0:T(8,128)(2,1)S(1)}, u32[]{:S(2)}, u32[]{:S(2)}) collective-permute-start(bf16[3,512,512]{2,1,0:T(8,128)(2,1)S(1)} %hold.4.refs_10_), channel_id=1, source_target_pairs={{0,1},{1,0},{2,3},{3,2},{4,5},{5,4},{6,7},{7,6},{8,9},{9,8},{10,11... | collective-permute-start | bytes 4718600 | tf_op jit(solution)/shard_map/ppermute | solution.py:429
  34.6 14.6 %collective-permute-start.9 = (bf16[512,512]{1,0:T(8,128)(2,1)}, bf16[512,512]{1,0:T(8,128)(2,1)}, u32[]{:S(2)}, u32[]{:S(2)}) collective-permute-start(bf16[512,512]{1,0:T(8,128)(2,1)} %pad_maximum_fusion.1), channel_id=1, source_target_pairs={{0,6},{1,7},{2,0},{3,1},{4,2},{5,3},{6,4},{7,5},{8,14},{9,15},{10,... | collective-permute-start | bytes 1572872 | tf_op jit(solution)/shard_map/ppermute | solution.py:423
  36.6 14.3 %collective-permute-start.8 = (bf16[512,512]{1,0:T(8,128)(2,1)}, bf16[512,512]{1,0:T(8,128)(2,1)}, u32[]{:S(2)}, u32[]{:S(2)}) collective-permute-start(bf16[512,512]{1,0:T(8,128)(2,1)} %pad_maximum_fusion.1), channel_id=1, source_target_pairs={{0,2},{1,3},{2,4},{3,5},{4,6},{5,7},{6,0},{7,1},{8,10},{9,11},{10,... | collective-permute-start | bytes 1572872 | tf_op jit(solution)/shard_map/ppermute | solution.py:422
  36.7 4.6 %collective-permute-start.13 = (bf16[64,512]{1,0:T(8,128)(2,1)}, bf16[64,512]{1,0:T(8,128)(2,1)}, u32[]{:S(2)}, u32[]{:S(2)}) collective-permute-start(bf16[64,512]{1,0:T(8,128)(2,1)} %get-tuple-element.66), channel_id=1, source_target_pairs={{192,128},{200,136},{208,144},{216,152},{224,160},{232,168},{240,1... | collective-permute-start | bytes 196616 | tf_op jit(solution)/shard_map/ppermute | solution.py:427
  38.0 3.3 %collective-permute-start.12 = (bf16[64,512]{1,0:T(8,128)(2,1)S(1)}, bf16[64,512]{1,0:T(8,128)(2,1)}, u32[]{:S(2)}, u32[]{:S(2)}) collective-permute-start(bf16[64,512]{1,0:T(8,128)(2,1)S(1)} %get-tuple-element.65), channel_id=1, source_target_pairs={{192,64},{200,72},{208,80},{216,88},{224,96},{232,104},{240,112},{... | collective-permute-start | bytes 196616 | tf_op jit(solution)/shard_map/ppermute | solution.py:427
  54.5 11.2 %collective-permute-start.17 = (bf16[3,512,512]{2,1,0:T(8,128)(2,1)S(1)}, bf16[3,512,512]{2,1,0:T(8,128)(2,1)S(1)}, u32[]{:S(2)}, u32[]{:S(2)}) collective-permute-start(bf16[3,512,512]{2,1,0:T(8,128)(2,1)S(1)} %pad_maximum_fusion.refs_4_.refs_6_), channel_id=1, source_target_pairs={{0,1},{1,0},{2,3},{3,2},{4,5},{5,4},{6,7},{7,6},{8,9},{9,8},{10,11... | collective-permute-start | bytes 4718600 | tf_op jit(solution)/shard_map/ppermute | solution.py:438
  54.6 8.9 %collective-permute-start.16 = (bf16[256,512]{1,0:T(8,128)(2,1)S(1)}, bf16[256,512]{1,0:T(8,128)(2,1)S(1)}, u32[]{:S(2)}, u32[]{:S(2)}) collective-permute-start(bf16[256,512]{1,0:T(8,128)(2,1)S(1)} %slice.65), channel_id=1, source_target_pairs={{0,6},{1,7},{2,0},{3,1},{4,2},{5,3},{6,4},{7,5},{8,14},{9,15},{10,... | collective-permute-start | bytes 786440 | tf_op jit(solution)/shard_map/ppermute | solution.py:437
  57.3 8.4 %collective-permute-start.15 = (bf16[256,512]{1,0:T(8,128)(2,1)S(1)}, bf16[256,512]{1,0:T(8,128)(2,1)S(1)}, u32[]{:S(2)}, u32[]{:S(2)}) collective-permute-start(bf16[256,512]{1,0:T(8,128)(2,1)S(1)} %slice.64), channel_id=1, source_target_pairs={{0,2},{1,3},{2,4},{3,5},{4,6},{5,7},{6,0},{7,1},{8,10},{9,11},{10,... | collective-permute-start | bytes 786440 | tf_op jit(solution)/shard_map/ppermute | solution.py:436
  65.7 7.5 %collective-permute-start.18 = (bf16[512,512]{1,0:T(8,128)(2,1)S(1)}, bf16[512,512]{1,0:T(8,128)(2,1)S(1)}, u32[]{:S(2)}, u32[]{:S(2)}) collective-permute-start(bf16[512,512]{1,0:T(8,128)(2,1)S(1)} %pad_maximum_fusion.2), channel_id=1, source_target_pairs={{0,1},{1,0},{2,3},{3,2},{4,5},{5,4},{6,7},{7,6},{8,9},{9,8},{10,11... | collective-permute-start | bytes 1572872 | tf_op jit(solution)/shard_map/ppermute | solution.py:441
  67.1 5.4 %collective-permute-start.14 = (bf16[64,512]{1,0:T(8,128)(2,1)S(1)}, bf16[64,512]{1,0:T(8,128)(2,1)S(1)}, u32[]{:S(2)}, u32[]{:S(2)}) collective-permute-start(bf16[64,512]{1,0:T(8,128)(2,1)S(1)} %get-tuple-element.71.refs_0_), channel_id=1, source_target_pairs={{0,8},{64,72},{128,136},{192,200},{1,9},{65,73},{129,137},{193,201... | collective-permute-start | bytes 196616 | tf_op jit(solution)/shard_map/ppermute | solution.py:456
  72.5 2.0 %collective-permute-start.19 = (bf16[1,64,512]{2,1,0:T(8,128)(2,1)S(1)}, bf16[1,64,512]{2,1,0:T(8,128)(2,1)S(1)}, u32[]{:S(2)}, u32[]{:S(2)}) collective-permute-start(bf16[1,64,512]{2,1,0:T(8,128)(2,1)S(1)} %bitcast.21), channel_id=1, source_target_pairs={{8,16},{72,80},{136,144},{200,208},{40,48},{9,17},{73,81},{137,145... | collective-permute-start | bytes 196616 | tf_op jit(solution)/shard_map/ppermute | solution.py:455
  78.7 14.1 %collective-permute-start.23 = (bf16[3,64,512]{2,1,0:T(8,128)(2,1)S(1)}, bf16[3,64,512]{2,1,0:T(8,128)(2,1)S(1)}, u32[]{:S(2)}, u32[]{:S(2)}) collective-permute-start(bf16[3,64,512]{2,1,0:T(8,128)(2,1)S(1)} %append.6), channel_id=1, source_target_pairs={{24,32},{88,96},{152,160},{216,224},{56,0},{25,33},{89,97},{153,16... | collective-permute-start | bytes 589832 | tf_op jit(solution)/shard_map/ppermute | solution.py:455
  80.6 12.8 %collective-permute-start.24 = (bf16[64,512]{1,0:T(8,128)(2,1)S(1)}, bf16[64,512]{1,0:T(8,128)(2,1)S(1)}, u32[]{:S(2)}, u32[]{:S(2)}) collective-permute-start(bf16[64,512]{1,0:T(8,128)(2,1)S(1)} %step.9.refs_3_), channel_id=1, source_target_pairs={{24,32},{88,96},{152,160},{216,224},{25,33},{89,97},{153,161},{217... | collective-permute-start | bytes 196616 | tf_op jit(solution)/shard_map/ppermute | solution.py:456
  94.0 5.8 %collective-permute-start.25 = (bf16[4,64,512]{2,1,0:T(8,128)(2,1)S(1)}, bf16[4,64,512]{2,1,0:T(8,128)(2,1)S(1)}, u32[]{:S(2)}, u32[]{:S(2)}) collective-permute-start(bf16[4,64,512]{2,1,0:T(8,128)(2,1)S(1)} %append.7), channel_id=1, source_target_pairs={{32,40},{96,104},{160,168},{224,232},{0,8},{33,41},{97,105},{161,1... | collective-permute-start | bytes 786440 | tf_op jit(solution)/shard_map/ppermute | solution.py:455
  95.9 4.5 %collective-permute-start.26 = (bf16[64,512]{1,0:T(8,128)(2,1)S(1)}, bf16[64,512]{1,0:T(8,128)(2,1)S(1)}, u32[]{:S(2)}, u32[]{:S(2)}) collective-permute-start(bf16[64,512]{1,0:T(8,128)(2,1)S(1)} %step.10.refs_4_), channel_id=1, source_target_pairs={{32,40},{96,104},{160,168},{224,232},{33,41},{97,105},{161,169},{2... | collective-permute-start | bytes 196616 | tf_op jit(solution)/shard_map/ppermute | solution.py:456
  97.1 6.3 %collective-permute-start.27 = (bf16[64,512]{1,0:T(8,128)(2,1)S(1)}, bf16[64,512]{1,0:T(8,128)(2,1)S(1)}, u32[]{:S(2)}, u32[]{:S(2)}) collective-permute-start(bf16[64,512]{1,0:T(8,128)(2,1)S(1)} %own_row.2.refs_0_), channel_id=1, source_target_pairs={{8,0},{16,8},{24,16},{72,64},{80,72},{88,80},{136,128},{144,136},{... | collective-permute-start | bytes 196616 | tf_op jit(solution)/shard_map/ppermute | solution.py:470
  104.0 3.2 %collective-permute-start.28 = (bf16[5,64,512]{2,1,0:T(8,128)(2,1)S(1)}, bf16[5,64,512]{2,1,0:T(8,128)(2,1)S(1)}, u32[]{:S(2)}, u32[]{:S(2)}) collective-permute-start(bf16[5,64,512]{2,1,0:T(8,128)(2,1)S(1)} %append.8), channel_id=1, source_target_pairs={{40,48},{104,112},{168,176},{232,240},{8,16},{41,49},{105,113},{16... | collective-permute-start | bytes 983048 | tf_op jit(solution)/shard_map/ppermute | solution.py:455
  105.3 2.6 %collective-permute-start.29 = (bf16[64,512]{1,0:T(8,128)(2,1)S(1)}, bf16[64,512]{1,0:T(8,128)(2,1)S(1)}, u32[]{:S(2)}, u32[]{:S(2)}) collective-permute-start(bf16[64,512]{1,0:T(8,128)(2,1)S(1)} %step.11.refs_5_), channel_id=1, source_target_pairs={{40,48},{104,112},{168,176},{232,240},{41,49},{105,113},{169,177},... | collective-permute-start | bytes 196616 | tf_op jit(solution)/shard_map/ppermute | solution.py:456
  105.9 7.0 %collective-permute-start.30 = (bf16[64,512]{1,0:T(8,128)(2,1)S(1)}, bf16[64,512]{1,0:T(8,128)(2,1)S(1)}, u32[]{:S(2)}, u32[]{:S(2)}) collective-permute-start(bf16[64,512]{1,0:T(8,128)(2,1)S(1)} %collective-permute-done.27.refs_1_), channel_id=1, source_target_pairs={{8,0},{16,8},{24,16},{72,64},{80,72},{88,80},{136,128},{144,136},{... | collective-permute-start | bytes 196616 | tf_op jit(solution)/shard_map/ppermute | solution.py:470
  113.5 5.3 %collective-permute-start.31 = (bf16[6,64,512]{2,1,0:T(8,128)(2,1)S(1)}, bf16[6,64,512]{2,1,0:T(8,128)(2,1)S(1)}, u32[]{:S(2)}, u32[]{:S(2)}) collective-permute-start(bf16[6,64,512]{2,1,0:T(8,128)(2,1)S(1)} %append.9), channel_id=1, source_target_pairs={{48,56},{112,120},{176,184},{240,248},{16,24},{49,57},{113,121},{1... | collective-permute-start | bytes 1179656 | tf_op jit(solution)/shard_map/ppermute | solution.py:455
  114.8 4.6 %collective-permute-start.33 = (bf16[64,512]{1,0:T(8,128)(2,1)S(1)}, bf16[64,512]{1,0:T(8,128)(2,1)S(1)}, u32[]{:S(2)}, u32[]{:S(2)}) collective-permute-start(bf16[64,512]{1,0:T(8,128)(2,1)S(1)} %step.12.refs_6_), channel_id=1, source_target_pairs={{48,56},{112,120},{176,184},{240,248},{49,57},{113,121},{177,185},... | collective-permute-start | bytes 196616 | tf_op jit(solution)/shard_map/ppermute | solution.py:456
  115.5 6.2 %collective-permute-start.32 = (bf16[64,512]{1,0:T(8,128)(2,1)S(1)}, bf16[64,512]{1,0:T(8,128)(2,1)S(1)}, u32[]{:S(2)}, u32[]{:S(2)}) collective-permute-start(bf16[64,512]{1,0:T(8,128)(2,1)S(1)} %collective-permute-done.30.refs_2_), channel_id=1, source_target_pairs={{8,0},{16,8},{24,16},{72,64},{80,72},{88,80},{136,128},{144,136},{... | collective-permute-start | bytes 196616 | tf_op jit(solution)/shard_map/ppermute | solution.py:470
  116.8 35.0 %collective-permute-start.47 = (bf16[256,512]{1,0:T(8,128)(2,1)S(1)}, bf16[256,512]{1,0:T(8,128)(2,1)S(1)}, u32[]{:S(2)}, u32[]{:S(2)}) collective-permute-start(bf16[256,512]{1,0:T(8,128)(2,1)S(1)} %slice.59), channel_id=1, source_target_pairs={{0,2},{1,3},{2,4},{3,5},{4,6},{5,7},{6,0},{7,1},{8,10},{9,11},{10,... | collective-permute-start | bytes 786440 | tf_op jit(solution)/shard_map/ppermute | solution.py:463
  117.1 34.6 %collective-permute-start.48 = (bf16[256,512]{1,0:T(8,128)(2,1)S(1)}, bf16[256,512]{1,0:T(8,128)(2,1)S(1)}, u32[]{:S(2)}, u32[]{:S(2)}) collective-permute-start(bf16[256,512]{1,0:T(8,128)(2,1)S(1)} %slice.60), channel_id=1, source_target_pairs={{0,6},{1,7},{2,0},{3,1},{4,2},{5,3},{6,4},{7,5},{8,14},{9,15},{10,... | collective-permute-start | bytes 786440 | tf_op jit(solution)/shard_map/ppermute | solution.py:464
  123.4 2.2 %collective-permute-start.40 = (bf16[64,512]{1,0:T(8,128)(2,1)S(1)}, bf16[64,512]{1,0:T(8,128)(2,1)S(1)}, u32[]{:S(2)}, u32[]{:S(2)}) collective-permute-start(bf16[64,512]{1,0:T(8,128)(2,1)S(1)} %own_row.3.refs_7_), channel_id=1, source_target_pairs={{32,24},{40,32},{48,40},{56,48},{96,88},{104,96},{112,104},{120,11... | collective-permute-start | bytes 196616 | tf_op jit(solution)/shard_map/ppermute | solution.py:487
  124.2 2.7 %collective-permute-start.39 = (bf16[64,512]{1,0:T(8,128)(2,1)S(1)}, bf16[64,512]{1,0:T(8,128)(2,1)S(1)}, u32[]{:S(2)}, u32[]{:S(2)}) collective-permute-start(bf16[64,512]{1,0:T(8,128)(2,1)S(1)} %own_row.3.refs_7_), channel_id=1, source_target_pairs={{32,16},{40,24},{48,32},{56,40},{96,80},{104,88},{112,96},{120,104... | collective-permute-start | bytes 196616 | tf_op jit(solution)/shard_map/ppermute | solution.py:487
  124.9 3.3 %collective-permute-start.38 = (bf16[64,512]{1,0:T(8,128)(2,1)S(1)}, bf16[64,512]{1,0:T(8,128)(2,1)S(1)}, u32[]{:S(2)}, u32[]{:S(2)}) collective-permute-start(bf16[64,512]{1,0:T(8,128)(2,1)S(1)} %own_row.3.refs_7_), channel_id=1, source_target_pairs={{32,8},{40,16},{48,24},{56,32},{96,72},{104,80},{112,88},{120,96},... | collective-permute-start | bytes 196616 | tf_op jit(solution)/shard_map/ppermute | solution.py:487
  125.6 15.5 %collective-permute-start.37 = (bf16[64,512]{1,0:T(8,128)(2,1)S(1)}, bf16[64,512]{1,0:T(8,128)(2,1)S(1)}, u32[]{:S(2)}, u32[]{:S(2)}) collective-permute-start(bf16[64,512]{1,0:T(8,128)(2,1)S(1)} %own_row.3.refs_7_), channel_id=1, source_target_pairs={{56,0},{120,64},{184,128},{248,192},{57,1},{121,65},{185,129},{249... | collective-permute-start | bytes 196616 | tf_op jit(solution)/shard_map/ppermute | solution.py:487
  126.9 15.5 %collective-permute-start.36 = (bf16[64,512]{1,0:T(8,128)(2,1)S(1)}, bf16[64,512]{1,0:T(8,128)(2,1)S(1)}, u32[]{:S(2)}, u32[]{:S(2)}) collective-permute-start(bf16[64,512]{1,0:T(8,128)(2,1)S(1)} %own_row.3.refs_7_), channel_id=1, source_target_pairs={{48,0},{56,8},{112,64},{120,72},{176,128},{184,136},{240,192},{248... | collective-permute-start | bytes 196616 | tf_op jit(solution)/shard_map/ppermute | solution.py:487
  128.2 16.3 %collective-permute-start.35 = (bf16[64,512]{1,0:T(8,128)(2,1)S(1)}, bf16[64,512]{1,0:T(8,128)(2,1)S(1)}, u32[]{:S(2)}, u32[]{:S(2)}) collective-permute-start(bf16[64,512]{1,0:T(8,128)(2,1)S(1)} %own_row.3.refs_7_), channel_id=1, source_target_pairs={{40,0},{48,8},{56,16},{104,64},{112,72},{120,80},{168,128},{176,13... | collective-permute-start | bytes 196616 | tf_op jit(solution)/shard_map/ppermute | solution.py:487
  141.1 10.1 %collective-permute-start.34 = (bf16[64,512]{1,0:T(8,128)(2,1)S(1)}, bf16[64,512]{1,0:T(8,128)(2,1)S(1)}, u32[]{:S(2)}, u32[]{:S(2)}) collective-permute-start(bf16[64,512]{1,0:T(8,128)(2,1)S(1)} %own_row.3.refs_7_), channel_id=1, source_target_pairs={{32,0},{40,8},{48,16},{56,24},{96,64},{104,72},{112,80},{120,88},{... | collective-permute-start | bytes 196616 | tf_op jit(solution)/shard_map/ppermute | solution.py:487
  142.4 9.5 %collective-permute-start.42 = (bf16[4,64,512]{2,1,0:T(8,128)(2,1)S(1)}, bf16[4,64,512]{2,1,0:T(8,128)(2,1)S(1)}, u32[]{:S(2)}, u32[]{:S(2)}) collective-permute-start(bf16[4,64,512]{2,1,0:T(8,128)(2,1)S(1)} %collect.2.refs_1_), channel_id=1, source_target_pairs={{0,192},{8,200},{16,208},{24,216},{32,224},{40,232},{48,240},{56,2... | collective-permute-start | bytes 786440 | tf_op jit(solution)/shard_map/ppermute | solution.py:478
  144.5 7.6 %collective-permute-start.41 = (bf16[4,64,512]{2,1,0:T(8,128)(2,1)S(1)}, bf16[4,64,512]{2,1,0:T(8,128)(2,1)S(1)}, u32[]{:S(2)}, u32[]{:S(2)}) collective-permute-start(bf16[4,64,512]{2,1,0:T(8,128)(2,1)S(1)} %collect.2.refs_1_), channel_id=1, source_target_pairs={{0,64},{8,72},{16,80},{24,88},{32,96},{40,104},{48,112},{56,120},{... | collective-permute-start | bytes 786440 | tf_op jit(solution)/shard_map/ppermute | solution.py:477
  151.8 19.0 %collective-permute-start.49 = (bf16[512,512]{1,0:T(8,128)(2,1)S(1)}, bf16[512,512]{1,0:T(8,128)(2,1)S(1)}, u32[]{:S(2)}, u32[]{:S(2)}) collective-permute-start(bf16[512,512]{1,0:T(8,128)(2,1)S(1)} %hold.7.refs_11_), channel_id=1, source_target_pairs={{0,1},{1,0},{2,3},{3,2},{4,5},{5,4},{6,7},{7,6},{8,9},{9,8},{10,11... | collective-permute-start | bytes 1572872 | tf_op jit(solution)/shard_map/ppermute | solution.py:490
  152.1 10.1 %collective-permute-start.44 = (bf16[4,64,512]{2,1,0:T(8,128)(2,1)S(1)}, bf16[4,64,512]{2,1,0:T(8,128)(2,1)S(1)}, u32[]{:S(2)}, u32[]{:S(2)}) collective-permute-start(bf16[4,64,512]{2,1,0:T(8,128)(2,1)S(1)} %collect.3.refs_1_), channel_id=1, source_target_pairs={{0,64},{8,72},{16,80},{24,88},{32,96},{40,104},{48,112},{56,120},{... | collective-permute-start | bytes 786440 | tf_op jit(solution)/shard_map/ppermute | solution.py:289
  152.1 14.7 %collective-permute-start.43 = (bf16[4,64,512]{2,1,0:T(8,128)(2,1)S(1)}, bf16[4,64,512]{2,1,0:T(8,128)(2,1)S(1)}, u32[]{:S(2)}, u32[]{:S(2)}) collective-permute-start(bf16[4,64,512]{2,1,0:T(8,128)(2,1)S(1)} %collect.3.refs_1_), channel_id=1, source_target_pairs={{0,192},{8,200},{16,208},{24,216},{32,224},{40,232},{48,240},{56,2... | collective-permute-start | bytes 786440 | tf_op jit(solution)/shard_map/ppermute | solution.py:290
  155.4 15.4 %collective-permute-start.50 = (bf16[4,64,512]{2,1,0:T(8,128)(2,1)S(1)}, bf16[4,64,512]{2,1,0:T(8,128)(2,1)S(1)}, u32[]{:S(2)}, u32[]{:S(2)}) collective-permute-start(bf16[4,64,512]{2,1,0:T(8,128)(2,1)S(1)} %collect.2.refs_1_), channel_id=1, source_target_pairs={{0,128},{8,136},{16,144},{24,152},{32,160},{40,168},{48,176},{56,1... | collective-permute-start | bytes 786440 | tf_op jit(solution)/shard_map/ppermute | solution.py:479
  162.2 13.0 %collective-permute-start.45 = (bf16[2,64,512]{2,1,0:T(8,128)(2,1)S(1)}, bf16[2,64,512]{2,1,0:T(8,128)(2,1)S(1)}, u32[]{:S(2)}, u32[]{:S(2)}) collective-permute-start(bf16[2,64,512]{2,1,0:T(8,128)(2,1)S(1)} %slice.73), channel_id=1, source_target_pairs={{0,64},{8,72},{16,80},{24,88},{32,96},{40,104},{48,112},{56,120},{... | collective-permute-start | bytes 393224 | tf_op jit(solution)/shard_map/ppermute | solution.py:291
  166.8 8.4 %collective-permute-start.46 = (bf16[2,64,512]{2,1,0:T(8,128)(2,1)S(1)}, bf16[2,64,512]{2,1,0:T(8,128)(2,1)S(1)}, u32[]{:S(2)}, u32[]{:S(2)}) collective-permute-start(bf16[2,64,512]{2,1,0:T(8,128)(2,1)S(1)} %slice.74), channel_id=1, source_target_pairs={{0,192},{8,200},{16,208},{24,216},{32,224},{40,232},{48,240},{56,2... | collective-permute-start | bytes 393224 | tf_op jit(solution)/shard_map/ppermute | solution.py:292
  (8 other events, 86.3 us)

commit v5 on v4

--- a/solution.py
+++ b/solution.py
@@ -425,25 +425,28 @@
     zq = [zt[i * quarter : (i + 1) * quarter] for i in range(NY)]
     ready = [after(zq[0], up_a), after(zq[1], far_a), after(zq[2], down_b)]
     zr = [lax.ppermute(ready[i], "row", from_plane(3, i)) for i in range(NY - 1)]
-    near1 = hold([after(panel1, zr[0]), left1, right1], stack=True)
+    near1 = hold([after(panel1, *zr), left1, right1], stack=True)
     near_other1 = lax.ppermute(near1, "col", SWAP)
     left, right, near_other1, left1, right1, sc, *zr = lax.optimization_barrier(
         (left, right, near_other1, left1[:half], right1[half:], sc, *zr)
     )
     base = by_plane(*zr, zq[3])
+    fresh, inv = first(base, inverse)
+    last = lax.ppermute(fresh, "row", hop_z(1))
     far_a, far_b = left[:half], right[half:]
     near = jnp.stack([after(window, far_a, far_b), left, right])
     far_a = lax.ppermute(far_a, "col", shift_x(1))
     far_b = lax.ppermute(far_b, "col", shift_x(-1))
     near_other = lax.ppermute(near, "col", SWAP)
-    far_a, far_b, near_other = lax.optimization_barrier((far_a, far_b, near_other))
+    far_a, far_b, near_other, last = lax.optimization_barrier(
+        (far_a, far_b, near_other, last)
+    )
     far = jnp.concatenate([far_a, far_b])
     far_other = lax.ppermute(far, "col", SWAP)
     far_kept = hold([far_a, far_b])
     far_other = hold([after(far_other, far_kept)])
     blocks0 = [near, far_kept, near_other, far_other]
 
-    fresh, inv = first(base, inverse)
     solved = [fresh]
     acc = base.astype(F32)
     known = None
@@ -453,7 +456,8 @@
         sent = None
         if t > 1:
             sent = lax.ppermute(known, "row", hop_z_early(t))
-        last = lax.ppermute(fresh, "row", hop_z(t))
+        if t > 1:
+            last = lax.ppermute(fresh, "row", hop_z(t))
         if t > 1:
             acc, inv = early(t, sc, base, after(sent, fresh), inverse, blocks0)
             last = after(last, acc)

time: 181 us -> 184 us (1.017)
  waiting for transfers between devices: 79.1 us -> 88.2 us
  starting transfers between devices: 64.8 us -> 56.1 us
  local copies, waits for them, and re-layouts: 7.83 us -> 10.5 us
    ppermute x1, waiting for transfers between devices: 1.18 us -> 8.69 us  [on_device(): up_a = lax.ppermute(top, 'row', from_plane(3, 0))]
    ppermute x1, waiting for transfers between devices: 0.01 us -> 5.37 us  [spread_y(): behind = lax.ppermute(rows, 'row', shift_y(-1))]
    ppermute x1, waiting for transfers between devices: 6.15 us -> 1.09 us  [on_device(): far_b = lax.ppermute(far_b, 'col', shift_x(-1))]
    ppermute x1, starting transfers between devices: 4.56 us -> 0.39 us  [spread_y(): far_a = lax.ppermute(before[:half], 'row', shift_y(1))]
    ppermute x1, waiting for transfers between devices: 6.63 us -> 2.75 us  [on_device(): right1 = lax.ppermute(panel1, 'col', shift_x(-1))]
    ppermute x7 -> x6, starting transfers between devices: 7.44 us -> 3.99 us  [on_device(): last = lax.ppermute(fresh, 'row', hop_z(t))]
    ppermute x6, waiting for transfers between devices: 12.8 us -> 16.2 us  [on_device(): sent = lax.ppermute(known, 'row', hop_z_early(t))]
    ppermute x0 -> x1, starting transfers between devices: none -> 3.2 us  [on_device(): last = lax.ppermute(fresh, 'row', hop_z(1))]
  transfers between devices with their start and end apart: 51 -> 51, of which waited for: 18 -> 21; matrix products, arithmetic and copies ran while one was open for 4% -> 4% of each run, Pallas kernels for 8% -> 8%
where the time goes in v5:
time: 184 us; the launch traced here: 182 us
  waiting for transfers between devices  88.2 us (48%)
  starting transfers between devices  56.1 us (30%)
  Pallas kernels  22.2 us (12%)
  local copies, waits for them, and re-layouts  10.5 us (6%)
  other arithmetic  3.74 us (2%)
    ppermute x7, waiting for transfers between devices, on_device(): lax.ppermute(own_s, 'row', back_z(d, range(4, 8)))  17.5 us
    ppermute x6, waiting for transfers between devices, on_device(): sent = lax.ppermute(known, 'row', hop_z_early(t))  16.2 us
    ppermute x1, waiting for transfers between devices, on_device(): right = lax.ppermute(window, 'col', shift_x(-1))  10.1 us
    ppermute x3, waiting for transfers between devices, on_device(): lax.ppermute((back_a or [own_s])[-1], 'row', back_z(1, range(1, 4)))  9.57 us
    pallas_call x2, Pallas kernels, final(): pl.pallas_call(lambda *refs: final_kernel(start, *refs), out_shape=(jax.S...  9.19 us
    ppermute x1, waiting for transfers between devices, on_device(): up_a = lax.ppermute(top, 'row', from_plane(3, 0))  8.69 us
    ppermute x7, starting transfers between devices, on_device(): lax.ppermute(own_s, 'row', back_z(d, range(4, 8)))  7.28 us
    ppermute x1, waiting for transfers between devices, spread_y(): before = lax.ppermute(rows, 'row', shift_y(1))  5.63 us
  transfers between devices with their start and end apart: 51, of which 21 were waited for; matrix products, arithmetic and copies ran while one was open for 4% of the time, Pallas kernels for 8%

profile of v5, /device:TPU:2, one launch (start us, length us, event | category | flops | bytes accessed | tf_op | source)
XLA Modules:
  0.0 182.1 jit_solution(7697605050251619820)
XLA Ops:
  0.6 1.9 %slice_bitcast_fusion.2 = (bf16[256,512]{1,0:T(8,128)(2,1)}, bf16[256,512]{1,0:T(8,128)(2,1)S(1)}) fusion(bf16[2,1,512,1,512]{4,2,3,1,0:T(8,128)(2,1)} %param.3), kind=kLoop, calls=%fused_computation.8 | loop fusion | bytes 1048576 | tf_op jit(solution)/shard_map/slice | solution.py:400
  2.5 1.3 collective-permute-start
  3.8 1.4 collective-permute-start.4
  5.2 8.7 %collective-permute-done = bf16[256,512]{1,0:T(8,128)(2,1)S(1)} collective-permute-done((bf16[256,512]{1,0:T(8,128)(2,1)}, bf16[256,512]{1,0:T(8,128)(2,1)S(1)}, u32[]{:S(2)}, u32[]{:S(2)}) %collective-permute-start) | collective-permute-done | bytes 262176 | tf_op jit(solution)/shard_map/ppermute | solution.py:401
  13.8 2.0 %collective-permute-start.2 = (bf16[256,512]{1,0:T(8,128)(2,1)S(1)}, bf16[256,512]{1,0:T(8,128)(2,1)}, u32[]{:S(2)}, u32[]{:S(2)}) collective-permute-start(bf16[256,512]{1,0:T(8,128)(2,1)S(1)} %collective-permute-done), channel_id=1, source_target_pairs={{0,64},{8,72},{16,80},{24,88},{32,96},{40,104},{48,112},{56,120},{... | collective-permute-start | bytes 786440 | tf_op jit(solution)/shard_map/ppermute | solution.py:405
  15.8 2.0 %collective-permute-start.1 = (bf16[256,512]{1,0:T(8,128)(2,1)}, bf16[256,512]{1,0:T(8,128)(2,1)}, u32[]{:S(2)}, u32[]{:S(2)}) collective-permute-start(bf16[256,512]{1,0:T(8,128)(2,1)} %get-tuple-element.124), channel_id=1, source_target_pairs={{192,128},{200,136},{208,144},{216,152},{224,160},{232,168},{240,1... | collective-permute-start | bytes 786440 | tf_op jit(solution)/shard_map/ppermute | solution.py:404
  17.8 1.3 collective-permute-start.3
  19.1 1.4 collective-permute-start.5
  23.4 1.5 collective-permute-start.6
  25.8 1.3 collective-permute-start.10
  29.6 1.3 select_select_fusion.1
  31.7 2.8 %collective-permute-done.7.refs_2_ = bf16[512,512]{1,0:T(8,128)(2,1)S(1)} collective-permute-done((bf16[512,512]{1,0:T(8,128)(2,1)S(1)}, bf16[512,512]{1,0:T(8,128)(2,1)S(1)}, u32[]{:S(2)}, u32[]{:S(2)}) %collective-permute-start.7) | collective-permute-done | bytes 524320 | tf_op jit(solution)/shard_map/ppermute | solution.py:419
  34.4 2.6 %collective-permute-done.6.refs_1_ = bf16[512,512]{1,0:T(8,128)(2,1)S(1)} collective-permute-done((bf16[512,512]{1,0:T(8,128)(2,1)S(1)}, bf16[512,512]{1,0:T(8,128)(2,1)S(1)}, u32[]{:S(2)}, u32[]{:S(2)}) %collective-permute-start.6) | collective-permute-done | bytes 524320 | tf_op jit(solution)/shard_map/ppermute | solution.py:418
  38.4 3.0 %collective-permute-start.9 = (bf16[512,512]{1,0:T(8,128)(2,1)}, bf16[512,512]{1,0:T(8,128)(2,1)}, u32[]{:S(2)}, u32[]{:S(2)}) collective-permute-start(bf16[512,512]{1,0:T(8,128)(2,1)} %pad_maximum_fusion.1), channel_id=1, source_target_pairs={{0,6},{1,7},{2,0},{3,1},{4,2},{5,3},{6,4},{7,5},{8,14},{9,15},{10,... | collective-permute-start | bytes 1572872 | tf_op jit(solution)/shard_map/ppermute | solution.py:423
  43.5 10.1 %collective-permute-done.9 = bf16[512,512]{1,0:T(8,128)(2,1)} collective-permute-done((bf16[512,512]{1,0:T(8,128)(2,1)}, bf16[512,512]{1,0:T(8,128)(2,1)}, u32[]{:S(2)}, u32[]{:S(2)}) %collective-permute-start.9) | collective-permute-done | bytes 524320 | tf_op jit(solution)/shard_map/ppermute | solution.py:423
  53.6 2.2 %collective-permute-done.8 = bf16[512,512]{1,0:T(8,128)(2,1)} collective-permute-done((bf16[512,512]{1,0:T(8,128)(2,1)}, bf16[512,512]{1,0:T(8,128)(2,1)}, u32[]{:S(2)}, u32[]{:S(2)}) %collective-permute-start.8) | collective-permute-done | bytes 524320 | tf_op jit(solution)/shard_map/ppermute | solution.py:422
  55.8 1.1 slice.64
  56.9 1.2 slice.65
  58.1 1.5 pad_maximum_fusion.refs_4_.refs_6_
  59.7 1.6 collective-permute-start.15
  62.2 3.2 %collective-permute-start.17 = (bf16[64,512]{1,0:T(8,128)(2,1)S(1)}, bf16[64,512]{1,0:T(8,128)(2,1)S(1)}, u32[]{:S(2)}, u32[]{:S(2)}) collective-permute-start(bf16[64,512]{1,0:T(8,128)(2,1)S(1)} %get-tuple-element.72.refs_0_), channel_id=1, source_target_pairs={{0,8},{64,72},{128,136},{192,200},{1,9},{65,73},{129,137},{193,201... | collective-permute-start | bytes 196616 | tf_op jit(solution)/shard_map/ppermute | solution.py:435
  65.4 1.9 %collective-permute-done.17.refs_2_.refs_4_ = bf16[64,512]{1,0:T(8,128)(2,1)S(1)} collective-permute-done((bf16[64,512]{1,0:T(8,128)(2,1)S(1)}, bf16[64,512]{1,0:T(8,128)(2,1)S(1)}, u32[]{:S(2)}, u32[]{:S(2)}) %collective-permute-start.17) | collective-permute-done | bytes 65568 | tf_op jit(solution)/shard_map/ppermute | solution.py:435
  68.4 1.2 collective-permute-done.14.refs_0_
  70.5 1.2 collective-permute-done.18.refs_0_
  77.1 1.3 collective-permute-start.23
  79.7 15.0 %collective-permute-done.23.refs_2_.known.refs_9_ = bf16[3,64,512]{2,1,0:T(8,128)(2,1)S(1)} collective-permute-done((bf16[3,64,512]{2,1,0:T(8,128)(2,1)S(1)}, bf16[3,64,512]{2,1,0:T(8,128)(2,1)S(1)}, u32[]{:S(2)}, u32[]{:S(2)}) %collective-permute-start.23) | collective-permute-done | bytes 196640 | tf_op jit(solution)/shard_map/ppermute | solution.py:458
  95.8 1.3 collective-permute-start.25
  98.9 1.5 collective-permute-start.27
  100.4 1.2 collective-permute-done.25.refs_2_.known.refs_11_
  102.2 3.1 %collective-permute-done.27.refs_1_ = bf16[64,512]{1,0:T(8,128)(2,1)S(1)} collective-permute-done((bf16[64,512]{1,0:T(8,128)(2,1)S(1)}, bf16[64,512]{1,0:T(8,128)(2,1)S(1)}, u32[]{:S(2)}, u32[]{:S(2)}) %collective-permute-start.27) | collective-permute-done | bytes 65568 | tf_op jit(solution)/shard_map/ppermute | solution.py:474
  107.8 1.3 collective-permute-start.30
  109.6 4.3 %collective-permute-done.30.refs_2_ = bf16[64,512]{1,0:T(8,128)(2,1)S(1)} collective-permute-done((bf16[64,512]{1,0:T(8,128)(2,1)S(1)}, bf16[64,512]{1,0:T(8,128)(2,1)S(1)}, u32[]{:S(2)}, u32[]{:S(2)}) %collective-permute-start.30) | collective-permute-done | bytes 65568 | tf_op jit(solution)/shard_map/ppermute | solution.py:474
  116.4 1.3 collective-permute-start.32
  118.3 1.5 collective-permute-start.48
  120.4 2.2 %collective-permute-done.32.refs_3_ = bf16[64,512]{1,0:T(8,128)(2,1)S(1)} collective-permute-done((bf16[64,512]{1,0:T(8,128)(2,1)S(1)}, bf16[64,512]{1,0:T(8,128)(2,1)S(1)}, u32[]{:S(2)}, u32[]{:S(2)}) %collective-permute-start.32) | collective-permute-done | bytes 65568 | tf_op jit(solution)/shard_map/ppermute | solution.py:474
  126.5 1.3 collective-permute-start.37
  127.8 1.3 collective-permute-start.36
  129.1 1.3 collective-permute-start.35
  130.4 11.7 %collective-permute-done.37.refs_3_ = bf16[64,512]{1,0:T(8,128)(2,1)S(1)} collective-permute-done((bf16[64,512]{1,0:T(8,128)(2,1)S(1)}, bf16[64,512]{1,0:T(8,128)(2,1)S(1)}, u32[]{:S(2)}, u32[]{:S(2)}) %collective-permute-start.37) | collective-permute-done | bytes 65568 | tf_op jit(solution)/shard_map/ppermute | solution.py:491
  142.2 1.3 collective-permute-start.34
  143.5 3.0 %collective-permute-start.42 = (bf16[4,64,512]{2,1,0:T(8,128)(2,1)S(1)}, bf16[4,64,512]{2,1,0:T(8,128)(2,1)S(1)}, u32[]{:S(2)}, u32[]{:S(2)}) collective-permute-start(bf16[4,64,512]{2,1,0:T(8,128)(2,1)S(1)} %collect.2.refs_1_), channel_id=1, source_target_pairs={{0,192},{8,200},{16,208},{24,216},{32,224},{40,232},{48,240},{56,2... | collective-permute-start | bytes 786440 | tf_op jit(solution)/shard_map/ppermute | solution.py:482
  146.5 5.7 %collective-permute-done.34.refs_0_ = bf16[64,512]{1,0:T(8,128)(2,1)S(1)} collective-permute-done((bf16[64,512]{1,0:T(8,128)(2,1)S(1)}, bf16[64,512]{1,0:T(8,128)(2,1)S(1)}, u32[]{:S(2)}, u32[]{:S(2)}) %collective-permute-start.34) | collective-permute-done | bytes 65568 | tf_op jit(solution)/shard_map/ppermute | solution.py:491
  154.1 3.2 %collective-permute-start.43 = (bf16[4,64,512]{2,1,0:T(8,128)(2,1)S(1)}, bf16[4,64,512]{2,1,0:T(8,128)(2,1)S(1)}, u32[]{:S(2)}, u32[]{:S(2)}) collective-permute-start(bf16[4,64,512]{2,1,0:T(8,128)(2,1)S(1)} %collect.3.refs_1_), channel_id=1, source_target_pairs={{0,192},{8,200},{16,208},{24,216},{32,224},{40,232},{48,240},{56,2... | collective-permute-start | bytes 786440 | tf_op jit(solution)/shard_map/ppermute | solution.py:290
  157.3 5.6 %collective-permute-done.44.refs_5_ = bf16[4,64,512]{2,1,0:T(8,128)(2,1)S(1)} collective-permute-done((bf16[4,64,512]{2,1,0:T(8,128)(2,1)S(1)}, bf16[4,64,512]{2,1,0:T(8,128)(2,1)S(1)}, u32[]{:S(2)}, u32[]{:S(2)}) %collective-permute-start.44) | collective-permute-done | bytes 262176 | tf_op jit(solution)/shard_map/ppermute | solution.py:289
  163.3 5.4 %collective-permute-done.43.refs_2_ = bf16[4,64,512]{2,1,0:T(8,128)(2,1)S(1)} collective-permute-done((bf16[4,64,512]{2,1,0:T(8,128)(2,1)S(1)}, bf16[4,64,512]{2,1,0:T(8,128)(2,1)S(1)}, u32[]{:S(2)}, u32[]{:S(2)}) %collective-permute-start.43) | collective-permute-done | bytes 262176 | tf_op jit(solution)/shard_map/ppermute | solution.py:290
  168.7 4.1 %collective-permute-start.46 = (bf16[2,64,512]{2,1,0:T(8,128)(2,1)S(1)}, bf16[2,64,512]{2,1,0:T(8,128)(2,1)S(1)}, u32[]{:S(2)}, u32[]{:S(2)}) collective-permute-start(bf16[2,64,512]{2,1,0:T(8,128)(2,1)S(1)} %slice.74), channel_id=1, source_target_pairs={{0,192},{8,200},{16,208},{24,216},{32,224},{40,232},{48,240},{56,2... | collective-permute-start | bytes 393224 | tf_op jit(solution)/shard_map/ppermute | solution.py:292
  172.9 4.4 %final.2 = (f32[8,512,256]{2,1,0:T(8,128)}, f32[2,1,512,256]{3,2,1,0:T(8,128)S(1)}) custom-call(s32[22]{0:T(128)S(1)} %concatenate.10.refs_0_.sc, bf16[4,64,512]{2,1,0:T(8,128)(2,1)S(1)} %collect.2.refs_1_, bf16[4,64,512]{2,1,0:T(8,128)(2,1)S(1)} %collective-permute-done.42.refs_2_, bf16[4,64,512]{2,1,0:T(8,128)(2,1)S(1)} %collective-permute-done.50.refs_3_.refs_4_, ...), custom_call_target="tpu_custom_call" | custom-call | flops 1610612736 | bytes 2097152 | tf_op jit(solution)/shard_map/final/pallas_call | solution.py:355
  177.3 4.8 %final.3 = (f32[8,512,256]{2,1,0:T(8,128)}, f32[2,1,512,256]{3,2,1,0:T(8,128)}) custom-call(s32[22]{0:T(128)S(1)} %concatenate.10.refs_0_.sc, bf16[4,64,512]{2,1,0:T(8,128)(2,1)S(1)} %collect.3.refs_1_, bf16[4,64,512]{2,1,0:T(8,128)(2,1)S(1)} %collective-permute-done.43.refs_2_, ...), custom_call_target="tpu_custom_call", output_to_operand_aliasing={{0}: (15, {})} | custom-call | flops 1610612736 | bytes 2097152 | tf_op jit(solution)/shard_map/final/pallas_call | solution.py:355
  (118 shorter events, 36.3 us)
Async XLA Ops:
  2.5 11.3 %collective-permute-start = (bf16[256,512]{1,0:T(8,128)(2,1)}, bf16[256,512]{1,0:T(8,128)(2,1)S(1)}, u32[]{:S(2)}, u32[]{:S(2)}) collective-permute-start(bf16[256,512]{1,0:T(8,128)(2,1)} %get-tuple-element.124), channel_id=1, source_target_pairs={{192,0},{200,8},{208,16},{216,24},{224,32},{232,40},{240,48},{248,... | collective-permute-start | bytes 786440 | tf_op jit(solution)/shard_map/ppermute | solution.py:401
  3.8 15.3 %collective-permute-start.4 = (bf16[256,512]{1,0:T(8,128)(2,1)S(1)}, bf16[256,512]{1,0:T(8,128)(2,1)}, u32[]{:S(2)}, u32[]{:S(2)}) collective-permute-start(bf16[256,512]{1,0:T(8,128)(2,1)S(1)} %get-tuple-element.125), channel_id=1, source_target_pairs={{192,128},{200,136},{208,144},{216,152},{224,160},{232,168},{240,1... | collective-permute-start | bytes 786440 | tf_op jit(solution)/shard_map/ppermute | solution.py:402
  13.8 9.6 %collective-permute-start.2 = (bf16[256,512]{1,0:T(8,128)(2,1)S(1)}, bf16[256,512]{1,0:T(8,128)(2,1)}, u32[]{:S(2)}, u32[]{:S(2)}) collective-permute-start(bf16[256,512]{1,0:T(8,128)(2,1)S(1)} %collective-permute-done), channel_id=1, source_target_pairs={{0,64},{8,72},{16,80},{24,88},{32,96},{40,104},{48,112},{56,120},{... | collective-permute-start | bytes 786440 | tf_op jit(solution)/shard_map/ppermute | solution.py:405
  15.8 10.0 %collective-permute-start.1 = (bf16[256,512]{1,0:T(8,128)(2,1)}, bf16[256,512]{1,0:T(8,128)(2,1)}, u32[]{:S(2)}, u32[]{:S(2)}) collective-permute-start(bf16[256,512]{1,0:T(8,128)(2,1)} %get-tuple-element.124), channel_id=1, source_target_pairs={{192,128},{200,136},{208,144},{216,152},{224,160},{232,168},{240,1... | collective-permute-start | bytes 786440 | tf_op jit(solution)/shard_map/ppermute | solution.py:404
  17.8 10.4 %collective-permute-start.3 = (bf16[256,512]{1,0:T(8,128)(2,1)S(1)}, bf16[256,512]{1,0:T(8,128)(2,1)}, u32[]{:S(2)}, u32[]{:S(2)}) collective-permute-start(bf16[256,512]{1,0:T(8,128)(2,1)S(1)} %get-tuple-element.125), channel_id=1, source_target_pairs={{192,0},{200,8},{208,16},{216,24},{224,32},{232,40},{240,48},{248,... | collective-permute-start | bytes 786440 | tf_op jit(solution)/shard_map/ppermute | solution.py:403
  19.1 9.8 %collective-permute-start.5 = (bf16[256,512]{1,0:T(8,128)(2,1)}, bf16[256,512]{1,0:T(8,128)(2,1)}, u32[]{:S(2)}, u32[]{:S(2)}) collective-permute-start(bf16[256,512]{1,0:T(8,128)(2,1)} %collective-permute-done.4), channel_id=1, source_target_pairs={{128,64},{136,72},{144,80},{152,88},{160,96},{168,104},{176,112},{... | collective-permute-start | bytes 786440 | tf_op jit(solution)/shard_map/ppermute | solution.py:406
  21.6 12.9 %collective-permute-start.7 = (bf16[512,512]{1,0:T(8,128)(2,1)S(1)}, bf16[512,512]{1,0:T(8,128)(2,1)S(1)}, u32[]{:S(2)}, u32[]{:S(2)}) collective-permute-start(bf16[512,512]{1,0:T(8,128)(2,1)S(1)} %slice_bitcast_fusion.refs_0_), channel_id=1, source_target_pairs={{0,6},{1,7},{2,0},{3,1},{4,2},{5,3},{6,4},{7,5},{8,14},{9,15},{10,... | collective-permute-start | bytes 1572872 | tf_op jit(solution)/shard_map/ppermute | solution.py:419
  23.4 13.6 %collective-permute-start.6 = (bf16[512,512]{1,0:T(8,128)(2,1)S(1)}, bf16[512,512]{1,0:T(8,128)(2,1)S(1)}, u32[]{:S(2)}, u32[]{:S(2)}) collective-permute-start(bf16[512,512]{1,0:T(8,128)(2,1)S(1)} %slice_bitcast_fusion.refs_0_), channel_id=1, source_target_pairs={{0,2},{1,3},{2,4},{3,5},{4,6},{5,7},{6,0},{7,1},{8,10},{9,11},{10,... | collective-permute-start | bytes 1572872 | tf_op jit(solution)/shard_map/ppermute | solution.py:418
  25.8 11.2 %collective-permute-start.10 = (bf16[64,512]{1,0:T(8,128)(2,1)}, bf16[64,512]{1,0:T(8,128)(2,1)S(1)}, u32[]{:S(2)}, u32[]{:S(2)}) collective-permute-start(bf16[64,512]{1,0:T(8,128)(2,1)} %get-tuple-element.62), channel_id=1, source_target_pairs={{192,0},{200,8},{208,16},{216,24},{224,32},{232,40},{240,48},{248,... | collective-permute-start | bytes 196616 | tf_op jit(solution)/shard_map/ppermute | solution.py:427
  28.2 8.8 %collective-permute-start.12 = (bf16[64,512]{1,0:T(8,128)(2,1)}, bf16[64,512]{1,0:T(8,128)(2,1)S(1)}, u32[]{:S(2)}, u32[]{:S(2)}) collective-permute-start(bf16[64,512]{1,0:T(8,128)(2,1)} %get-tuple-element.64), channel_id=1, source_target_pairs={{192,128},{200,136},{208,144},{216,152},{224,160},{232,168},{240,1... | collective-permute-start | bytes 196616 | tf_op jit(solution)/shard_map/ppermute | solution.py:427
  28.9 8.2 %collective-permute-start.11 = (bf16[64,512]{1,0:T(8,128)(2,1)}, bf16[64,512]{1,0:T(8,128)(2,1)S(1)}, u32[]{:S(2)}, u32[]{:S(2)}) collective-permute-start(bf16[64,512]{1,0:T(8,128)(2,1)} %get-tuple-element.63), channel_id=1, source_target_pairs={{192,64},{200,72},{208,80},{216,88},{224,96},{232,104},{240,112},{... | collective-permute-start | bytes 196616 | tf_op jit(solution)/shard_map/ppermute | solution.py:427
  38.4 17.3 %collective-permute-start.13 = (bf16[3,512,512]{2,1,0:T(8,128)(2,1)S(1)}, bf16[3,512,512]{2,1,0:T(8,128)(2,1)S(1)}, u32[]{:S(2)}, u32[]{:S(2)}) collective-permute-start(bf16[3,512,512]{2,1,0:T(8,128)(2,1)S(1)} %hold.4.refs_10_), channel_id=1, source_target_pairs={{0,1},{1,0},{2,3},{3,2},{4,5},{5,4},{6,7},{7,6},{8,9},{9,8},{10,11... | collective-permute-start | bytes 4718600 | tf_op jit(solution)/shard_map/ppermute | solution.py:429
  38.4 15.1 %collective-permute-start.9 = (bf16[512,512]{1,0:T(8,128)(2,1)}, bf16[512,512]{1,0:T(8,128)(2,1)}, u32[]{:S(2)}, u32[]{:S(2)}) collective-permute-start(bf16[512,512]{1,0:T(8,128)(2,1)} %pad_maximum_fusion.1), channel_id=1, source_target_pairs={{0,6},{1,7},{2,0},{3,1},{4,2},{5,3},{6,4},{7,5},{8,14},{9,15},{10,... | collective-permute-start | bytes 1572872 | tf_op jit(solution)/shard_map/ppermute | solution.py:423
  41.4 14.4 %collective-permute-start.8 = (bf16[512,512]{1,0:T(8,128)(2,1)}, bf16[512,512]{1,0:T(8,128)(2,1)}, u32[]{:S(2)}, u32[]{:S(2)}) collective-permute-start(bf16[512,512]{1,0:T(8,128)(2,1)} %pad_maximum_fusion.1), channel_id=1, source_target_pairs={{0,2},{1,3},{2,4},{3,5},{4,6},{5,7},{6,0},{7,1},{8,10},{9,11},{10,... | collective-permute-start | bytes 1572872 | tf_op jit(solution)/shard_map/ppermute | solution.py:422
  59.6 10.0 %collective-permute-start.16 = (bf16[3,512,512]{2,1,0:T(8,128)(2,1)S(1)}, bf16[3,512,512]{2,1,0:T(8,128)(2,1)S(1)}, u32[]{:S(2)}, u32[]{:S(2)}) collective-permute-start(bf16[3,512,512]{2,1,0:T(8,128)(2,1)S(1)} %pad_maximum_fusion.refs_4_.refs_6_), channel_id=1, source_target_pairs={{0,1},{1,0},{2,3},{3,2},{4,5},{5,4},{6,7},{7,6},{8,9},{9,8},{10,11... | collective-permute-start | bytes 4718600 | tf_op jit(solution)/shard_map/ppermute | solution.py:440
  59.7 8.7 %collective-permute-start.15 = (bf16[256,512]{1,0:T(8,128)(2,1)S(1)}, bf16[256,512]{1,0:T(8,128)(2,1)S(1)}, u32[]{:S(2)}, u32[]{:S(2)}) collective-permute-start(bf16[256,512]{1,0:T(8,128)(2,1)S(1)} %slice.65), channel_id=1, source_target_pairs={{0,6},{1,7},{2,0},{3,1},{4,2},{5,3},{6,4},{7,5},{8,14},{9,15},{10,... | collective-permute-start | bytes 786440 | tf_op jit(solution)/shard_map/ppermute | solution.py:439
  61.3 8.4 %collective-permute-start.14 = (bf16[256,512]{1,0:T(8,128)(2,1)S(1)}, bf16[256,512]{1,0:T(8,128)(2,1)S(1)}, u32[]{:S(2)}, u32[]{:S(2)}) collective-permute-start(bf16[256,512]{1,0:T(8,128)(2,1)S(1)} %slice.64), channel_id=1, source_target_pairs={{0,2},{1,3},{2,4},{3,5},{4,6},{5,7},{6,0},{7,1},{8,10},{9,11},{10,... | collective-permute-start | bytes 786440 | tf_op jit(solution)/shard_map/ppermute | solution.py:438
  62.2 5.1 %collective-permute-start.17 = (bf16[64,512]{1,0:T(8,128)(2,1)S(1)}, bf16[64,512]{1,0:T(8,128)(2,1)S(1)}, u32[]{:S(2)}, u32[]{:S(2)}) collective-permute-start(bf16[64,512]{1,0:T(8,128)(2,1)S(1)} %get-tuple-element.72.refs_0_), channel_id=1, source_target_pairs={{0,8},{64,72},{128,136},{192,200},{1,9},{65,73},{129,137},{193,201... | collective-permute-start | bytes 196616 | tf_op jit(solution)/shard_map/ppermute | solution.py:435
  69.7 2.0 %collective-permute-start.18 = (bf16[512,512]{1,0:T(8,128)(2,1)S(1)}, bf16[512,512]{1,0:T(8,128)(2,1)S(1)}, u32[]{:S(2)}, u32[]{:S(2)}) collective-permute-start(bf16[512,512]{1,0:T(8,128)(2,1)S(1)} %pad_maximum_fusion.2), channel_id=1, source_target_pairs={{0,1},{1,0},{2,3},{3,2},{4,5},{5,4},{6,7},{7,6},{8,9},{9,8},{10,11... | collective-permute-start | bytes 1572872 | tf_op jit(solution)/shard_map/ppermute | solution.py:445
  69.8 3.1 %collective-permute-start.19 = (bf16[1,64,512]{2,1,0:T(8,128)(2,1)S(1)}, bf16[1,64,512]{2,1,0:T(8,128)(2,1)S(1)}, u32[]{:S(2)}, u32[]{:S(2)}) collective-permute-start(bf16[1,64,512]{2,1,0:T(8,128)(2,1)S(1)} %bitcast.21), channel_id=1, source_target_pairs={{8,16},{72,80},{136,144},{200,208},{40,48},{9,17},{73,81},{137,145... | collective-permute-start | bytes 196616 | tf_op jit(solution)/shard_map/ppermute | solution.py:458
  77.1 17.5 %collective-permute-start.23 = (bf16[3,64,512]{2,1,0:T(8,128)(2,1)S(1)}, bf16[3,64,512]{2,1,0:T(8,128)(2,1)S(1)}, u32[]{:S(2)}, u32[]{:S(2)}) collective-permute-start(bf16[3,64,512]{2,1,0:T(8,128)(2,1)S(1)} %append.6), channel_id=1, source_target_pairs={{24,32},{88,96},{152,160},{216,224},{56,0},{25,33},{89,97},{153,16... | collective-permute-start | bytes 589832 | tf_op jit(solution)/shard_map/ppermute | solution.py:458
  79.0 16.2 %collective-permute-start.24 = (bf16[64,512]{1,0:T(8,128)(2,1)S(1)}, bf16[64,512]{1,0:T(8,128)(2,1)S(1)}, u32[]{:S(2)}, u32[]{:S(2)}) collective-permute-start(bf16[64,512]{1,0:T(8,128)(2,1)S(1)} %step.9.refs_3_), channel_id=1, source_target_pairs={{24,32},{88,96},{152,160},{216,224},{25,33},{89,97},{153,161},{217... | collective-permute-start | bytes 196616 | tf_op jit(solution)/shard_map/ppermute | solution.py:460
  95.8 5.8 %collective-permute-start.25 = (bf16[4,64,512]{2,1,0:T(8,128)(2,1)S(1)}, bf16[4,64,512]{2,1,0:T(8,128)(2,1)S(1)}, u32[]{:S(2)}, u32[]{:S(2)}) collective-permute-start(bf16[4,64,512]{2,1,0:T(8,128)(2,1)S(1)} %append.7), channel_id=1, source_target_pairs={{32,40},{96,104},{160,168},{224,232},{0,8},{33,41},{97,105},{161,1... | collective-permute-start | bytes 786440 | tf_op jit(solution)/shard_map/ppermute | solution.py:458
  97.7 4.5 %collective-permute-start.26 = (bf16[64,512]{1,0:T(8,128)(2,1)S(1)}, bf16[64,512]{1,0:T(8,128)(2,1)S(1)}, u32[]{:S(2)}, u32[]{:S(2)}) collective-permute-start(bf16[64,512]{1,0:T(8,128)(2,1)S(1)} %step.10.refs_4_), channel_id=1, source_target_pairs={{32,40},{96,104},{160,168},{224,232},{33,41},{97,105},{161,169},{2... | collective-permute-start | bytes 196616 | tf_op jit(solution)/shard_map/ppermute | solution.py:460
  98.9 6.3 %collective-permute-start.27 = (bf16[64,512]{1,0:T(8,128)(2,1)S(1)}, bf16[64,512]{1,0:T(8,128)(2,1)S(1)}, u32[]{:S(2)}, u32[]{:S(2)}) collective-permute-start(bf16[64,512]{1,0:T(8,128)(2,1)S(1)} %own_row.2.refs_0_), channel_id=1, source_target_pairs={{8,0},{16,8},{24,16},{72,64},{80,72},{88,80},{136,128},{144,136},{... | collective-permute-start | bytes 196616 | tf_op jit(solution)/shard_map/ppermute | solution.py:474
  105.8 3.2 %collective-permute-start.28 = (bf16[5,64,512]{2,1,0:T(8,128)(2,1)S(1)}, bf16[5,64,512]{2,1,0:T(8,128)(2,1)S(1)}, u32[]{:S(2)}, u32[]{:S(2)}) collective-permute-start(bf16[5,64,512]{2,1,0:T(8,128)(2,1)S(1)} %append.8), channel_id=1, source_target_pairs={{40,48},{104,112},{168,176},{232,240},{8,16},{41,49},{105,113},{16... | collective-permute-start | bytes 983048 | tf_op jit(solution)/shard_map/ppermute | solution.py:458
  107.1 2.6 %collective-permute-start.29 = (bf16[64,512]{1,0:T(8,128)(2,1)S(1)}, bf16[64,512]{1,0:T(8,128)(2,1)S(1)}, u32[]{:S(2)}, u32[]{:S(2)}) collective-permute-start(bf16[64,512]{1,0:T(8,128)(2,1)S(1)} %step.11.refs_5_), channel_id=1, source_target_pairs={{40,48},{104,112},{168,176},{232,240},{41,49},{105,113},{169,177},... | collective-permute-start | bytes 196616 | tf_op jit(solution)/shard_map/ppermute | solution.py:460
  107.8 6.2 %collective-permute-start.30 = (bf16[64,512]{1,0:T(8,128)(2,1)S(1)}, bf16[64,512]{1,0:T(8,128)(2,1)S(1)}, u32[]{:S(2)}, u32[]{:S(2)}) collective-permute-start(bf16[64,512]{1,0:T(8,128)(2,1)S(1)} %collective-permute-done.27.refs_1_), channel_id=1, source_target_pairs={{8,0},{16,8},{24,16},{72,64},{80,72},{88,80},{136,128},{144,136},{... | collective-permute-start | bytes 196616 | tf_op jit(solution)/shard_map/ppermute | solution.py:474
  114.5 5.3 %collective-permute-start.31 = (bf16[6,64,512]{2,1,0:T(8,128)(2,1)S(1)}, bf16[6,64,512]{2,1,0:T(8,128)(2,1)S(1)}, u32[]{:S(2)}, u32[]{:S(2)}) collective-permute-start(bf16[6,64,512]{2,1,0:T(8,128)(2,1)S(1)} %append.9), channel_id=1, source_target_pairs={{48,56},{112,120},{176,184},{240,248},{16,24},{49,57},{113,121},{1... | collective-permute-start | bytes 1179656 | tf_op jit(solution)/shard_map/ppermute | solution.py:458
  115.7 4.6 %collective-permute-start.33 = (bf16[64,512]{1,0:T(8,128)(2,1)S(1)}, bf16[64,512]{1,0:T(8,128)(2,1)S(1)}, u32[]{:S(2)}, u32[]{:S(2)}) collective-permute-start(bf16[64,512]{1,0:T(8,128)(2,1)S(1)} %step.12.refs_6_), channel_id=1, source_target_pairs={{48,56},{112,120},{176,184},{240,248},{49,57},{113,121},{177,185},... | collective-permute-start | bytes 196616 | tf_op jit(solution)/shard_map/ppermute | solution.py:460
  116.4 6.2 %collective-permute-start.32 = (bf16[64,512]{1,0:T(8,128)(2,1)S(1)}, bf16[64,512]{1,0:T(8,128)(2,1)S(1)}, u32[]{:S(2)}, u32[]{:S(2)}) collective-permute-start(bf16[64,512]{1,0:T(8,128)(2,1)S(1)} %collective-permute-done.30.refs_2_), channel_id=1, source_target_pairs={{8,0},{16,8},{24,16},{72,64},{80,72},{88,80},{136,128},{144,136},{... | collective-permute-start | bytes 196616 | tf_op jit(solution)/shard_map/ppermute | solution.py:474
  117.7 35.2 %collective-permute-start.47 = (bf16[256,512]{1,0:T(8,128)(2,1)S(1)}, bf16[256,512]{1,0:T(8,128)(2,1)S(1)}, u32[]{:S(2)}, u32[]{:S(2)}) collective-permute-start(bf16[256,512]{1,0:T(8,128)(2,1)S(1)} %slice.61), channel_id=1, source_target_pairs={{0,2},{1,3},{2,4},{3,5},{4,6},{5,7},{6,0},{7,1},{8,10},{9,11},{10,... | collective-permute-start | bytes 786440 | tf_op jit(solution)/shard_map/ppermute | solution.py:467
  118.3 34.6 %collective-permute-start.48 = (bf16[256,512]{1,0:T(8,128)(2,1)S(1)}, bf16[256,512]{1,0:T(8,128)(2,1)S(1)}, u32[]{:S(2)}, u32[]{:S(2)}) collective-permute-start(bf16[256,512]{1,0:T(8,128)(2,1)S(1)} %slice.62), channel_id=1, source_target_pairs={{0,6},{1,7},{2,0},{3,1},{4,2},{5,3},{6,4},{7,5},{8,14},{9,15},{10,... | collective-permute-start | bytes 786440 | tf_op jit(solution)/shard_map/ppermute | solution.py:468
  124.4 2.2 %collective-permute-start.40 = (bf16[64,512]{1,0:T(8,128)(2,1)S(1)}, bf16[64,512]{1,0:T(8,128)(2,1)S(1)}, u32[]{:S(2)}, u32[]{:S(2)}) collective-permute-start(bf16[64,512]{1,0:T(8,128)(2,1)S(1)} %own_row.3.refs_7_), channel_id=1, source_target_pairs={{32,24},{40,32},{48,40},{56,48},{96,88},{104,96},{112,104},{120,11... | collective-permute-start | bytes 196616 | tf_op jit(solution)/shard_map/ppermute | solution.py:491
  125.2 2.7 %collective-permute-start.39 = (bf16[64,512]{1,0:T(8,128)(2,1)S(1)}, bf16[64,512]{1,0:T(8,128)(2,1)S(1)}, u32[]{:S(2)}, u32[]{:S(2)}) collective-permute-start(bf16[64,512]{1,0:T(8,128)(2,1)S(1)} %own_row.3.refs_7_), channel_id=1, source_target_pairs={{32,16},{40,24},{48,32},{56,40},{96,80},{104,88},{112,96},{120,104... | collective-permute-start | bytes 196616 | tf_op jit(solution)/shard_map/ppermute | solution.py:491
  125.8 3.3 %collective-permute-start.38 = (bf16[64,512]{1,0:T(8,128)(2,1)S(1)}, bf16[64,512]{1,0:T(8,128)(2,1)S(1)}, u32[]{:S(2)}, u32[]{:S(2)}) collective-permute-start(bf16[64,512]{1,0:T(8,128)(2,1)S(1)} %own_row.3.refs_7_), channel_id=1, source_target_pairs={{32,8},{40,16},{48,24},{56,32},{96,72},{104,80},{112,88},{120,96},... | collective-permute-start | bytes 196616 | tf_op jit(solution)/shard_map/ppermute | solution.py:491
  126.5 15.6 %collective-permute-start.37 = (bf16[64,512]{1,0:T(8,128)(2,1)S(1)}, bf16[64,512]{1,0:T(8,128)(2,1)S(1)}, u32[]{:S(2)}, u32[]{:S(2)}) collective-permute-start(bf16[64,512]{1,0:T(8,128)(2,1)S(1)} %own_row.3.refs_7_), channel_id=1, source_target_pairs={{56,0},{120,64},{184,128},{248,192},{57,1},{121,65},{185,129},{249... | collective-permute-start | bytes 196616 | tf_op jit(solution)/shard_map/ppermute | solution.py:491
  127.8 15.6 %collective-permute-start.36 = (bf16[64,512]{1,0:T(8,128)(2,1)S(1)}, bf16[64,512]{1,0:T(8,128)(2,1)S(1)}, u32[]{:S(2)}, u32[]{:S(2)}) collective-permute-start(bf16[64,512]{1,0:T(8,128)(2,1)S(1)} %own_row.3.refs_7_), channel_id=1, source_target_pairs={{48,0},{56,8},{112,64},{120,72},{176,128},{184,136},{240,192},{248... | collective-permute-start | bytes 196616 | tf_op jit(solution)/shard_map/ppermute | solution.py:491
  129.1 17.3 %collective-permute-start.35 = (bf16[64,512]{1,0:T(8,128)(2,1)S(1)}, bf16[64,512]{1,0:T(8,128)(2,1)S(1)}, u32[]{:S(2)}, u32[]{:S(2)}) collective-permute-start(bf16[64,512]{1,0:T(8,128)(2,1)S(1)} %own_row.3.refs_7_), channel_id=1, source_target_pairs={{40,0},{48,8},{56,16},{104,64},{112,72},{120,80},{168,128},{176,13... | collective-permute-start | bytes 196616 | tf_op jit(solution)/shard_map/ppermute | solution.py:491
  142.2 10.1 %collective-permute-start.34 = (bf16[64,512]{1,0:T(8,128)(2,1)S(1)}, bf16[64,512]{1,0:T(8,128)(2,1)S(1)}, u32[]{:S(2)}, u32[]{:S(2)}) collective-permute-start(bf16[64,512]{1,0:T(8,128)(2,1)S(1)} %own_row.3.refs_7_), channel_id=1, source_target_pairs={{32,0},{40,8},{48,16},{56,24},{96,64},{104,72},{112,80},{120,88},{... | collective-permute-start | bytes 196616 | tf_op jit(solution)/shard_map/ppermute | solution.py:491
  143.5 9.5 %collective-permute-start.42 = (bf16[4,64,512]{2,1,0:T(8,128)(2,1)S(1)}, bf16[4,64,512]{2,1,0:T(8,128)(2,1)S(1)}, u32[]{:S(2)}, u32[]{:S(2)}) collective-permute-start(bf16[4,64,512]{2,1,0:T(8,128)(2,1)S(1)} %collect.2.refs_1_), channel_id=1, source_target_pairs={{0,192},{8,200},{16,208},{24,216},{32,224},{40,232},{48,240},{56,2... | collective-permute-start | bytes 786440 | tf_op jit(solution)/shard_map/ppermute | solution.py:482
  146.5 7.6 %collective-permute-start.41 = (bf16[4,64,512]{2,1,0:T(8,128)(2,1)S(1)}, bf16[4,64,512]{2,1,0:T(8,128)(2,1)S(1)}, u32[]{:S(2)}, u32[]{:S(2)}) collective-permute-start(bf16[4,64,512]{2,1,0:T(8,128)(2,1)S(1)} %collect.2.refs_1_), channel_id=1, source_target_pairs={{0,64},{8,72},{16,80},{24,88},{32,96},{40,104},{48,112},{56,120},{... | collective-permute-start | bytes 786440 | tf_op jit(solution)/shard_map/ppermute | solution.py:481
  152.9 20.0 %collective-permute-start.49 = (bf16[512,512]{1,0:T(8,128)(2,1)S(1)}, bf16[512,512]{1,0:T(8,128)(2,1)S(1)}, u32[]{:S(2)}, u32[]{:S(2)}) collective-permute-start(bf16[512,512]{1,0:T(8,128)(2,1)S(1)} %hold.7.refs_11_), channel_id=1, source_target_pairs={{0,1},{1,0},{2,3},{3,2},{4,5},{5,4},{6,7},{7,6},{8,9},{9,8},{10,11... | collective-permute-start | bytes 1572872 | tf_op jit(solution)/shard_map/ppermute | solution.py:494
  154.1 8.9 %collective-permute-start.44 = (bf16[4,64,512]{2,1,0:T(8,128)(2,1)S(1)}, bf16[4,64,512]{2,1,0:T(8,128)(2,1)S(1)}, u32[]{:S(2)}, u32[]{:S(2)}) collective-permute-start(bf16[4,64,512]{2,1,0:T(8,128)(2,1)S(1)} %collect.3.refs_1_), channel_id=1, source_target_pairs={{0,64},{8,72},{16,80},{24,88},{32,96},{40,104},{48,112},{56,120},{... | collective-permute-start | bytes 786440 | tf_op jit(solution)/shard_map/ppermute | solution.py:289
  154.1 14.6 %collective-permute-start.43 = (bf16[4,64,512]{2,1,0:T(8,128)(2,1)S(1)}, bf16[4,64,512]{2,1,0:T(8,128)(2,1)S(1)}, u32[]{:S(2)}, u32[]{:S(2)}) collective-permute-start(bf16[4,64,512]{2,1,0:T(8,128)(2,1)S(1)} %collect.3.refs_1_), channel_id=1, source_target_pairs={{0,192},{8,200},{16,208},{24,216},{32,224},{40,232},{48,240},{56,2... | collective-permute-start | bytes 786440 | tf_op jit(solution)/shard_map/ppermute | solution.py:290
  157.3 15.6 %collective-permute-start.50 = (bf16[4,64,512]{2,1,0:T(8,128)(2,1)S(1)}, bf16[4,64,512]{2,1,0:T(8,128)(2,1)S(1)}, u32[]{:S(2)}, u32[]{:S(2)}) collective-permute-start(bf16[4,64,512]{2,1,0:T(8,128)(2,1)S(1)} %collect.2.refs_1_), channel_id=1, source_target_pairs={{0,128},{8,136},{16,144},{24,152},{32,160},{40,168},{48,176},{56,1... | collective-permute-start | bytes 786440 | tf_op jit(solution)/shard_map/ppermute | solution.py:483
  163.0 14.3 %collective-permute-start.45 = (bf16[2,64,512]{2,1,0:T(8,128)(2,1)S(1)}, bf16[2,64,512]{2,1,0:T(8,128)(2,1)S(1)}, u32[]{:S(2)}, u32[]{:S(2)}) collective-permute-start(bf16[2,64,512]{2,1,0:T(8,128)(2,1)S(1)} %slice.73), channel_id=1, source_target_pairs={{0,64},{8,72},{16,80},{24,88},{32,96},{40,104},{48,112},{56,120},{... | collective-permute-start | bytes 393224 | tf_op jit(solution)/shard_map/ppermute | solution.py:291
  168.7 8.6 %collective-permute-start.46 = (bf16[2,64,512]{2,1,0:T(8,128)(2,1)S(1)}, bf16[2,64,512]{2,1,0:T(8,128)(2,1)S(1)}, u32[]{:S(2)}, u32[]{:S(2)}) collective-permute-start(bf16[2,64,512]{2,1,0:T(8,128)(2,1)S(1)} %slice.74), channel_id=1, source_target_pairs={{0,192},{8,200},{16,208},{24,216},{32,224},{40,232},{48,240},{56,2... | collective-permute-start | bytes 393224 | tf_op jit(solution)/shard_map/ppermute | solution.py:292
  (11 other events, 120.9 us)
